TPU v7x, 256 devices: a whole 4x4x8 slice. The times are simulated.
256 devices in a mesh: facet: 4 (over z_lo, core), vis: 64 (over z_hi, y, x).
Axes of the slice: x: 4, y: 4, z: 8 (z_hi: 4, z_lo: 2; z = z_hi * 2 + z_lo), core: 2. Of those that a mesh axis runs over, the one named last changes fastest.
Arguments:
- visibilities: bfloat16 [2048, 128], P('vis'), may hold values from -6 to 6
- uv_coords: float32 [2048, 2], P('vis'), may hold values from -1280 to 1280
- cells: int32 [2, 2048, 64], P(None, 'vis'), may hold values from 0 to 4095
- centres: float32 [4, 2], P('facet'), may hold values from -0.03 to 0.03
- intersection_mask: int32 [4, 64, 256], P('facet', 'vis'), may hold values 0 or 1
Outputs:
- stitched: float32 [3, 64, 16384], P(None, 'vis', 'facet')
All inputs are finite; a program needn't handle non-finite values. No bound on the sum of `intersection_mask` on one device may be relied on, other than what follows from the above.
Results may differ from a plain program's by a relative error of at most 0.0055.
Values may be sent and summed in bfloat16 or wider, within the bound.
No kernel may reach another device: no remote copies, remote signals or barrier semaphores. Data moves between devices by JAX's collectives and lax.ppermute only.
A program may use at most 64 MiB of HBM per device.

v0:
```python
import math

import jax
import jax.numpy as jnp
from jax import lax
from jax.sharding import PartitionSpec as P

GRID = 4096
CH = 64
TERMS = 3
OVER = 256


def from_behind(shard, axis, by):
    length = lax.axis_size(axis)
    pairs = [(i, i + by) for i in range(length) if 0 <= i + by < length]
    return lax.ppermute(shard, axis, pairs)


def channel_nu(chans):
    return (2.0 * jnp.arange(chans, dtype=jnp.float32) + 1.0 - chans) / chans


def rotate_rows(visibilities, uv_coords, centre):
    chans = visibilities.shape[1] // 2
    freq = 1.0 + 0.15 * channel_nu(chans)
    proj = uv_coords[:, 0:1] * centre[0] + uv_coords[:, 1:2] * centre[1]
    phase = 2.0 * math.pi * proj * freq[None, :]
    cosine = jnp.cos(phase)
    sine = jnp.sin(phase)
    real_part = visibilities[:, :chans].astype(jnp.float32)
    imag_part = visibilities[:, chans:].astype(jnp.float32)
    joined = jnp.concatenate(
        [real_part * cosine + imag_part * sine, imag_part * cosine - real_part * sine], axis=1
    )
    return joined.astype(jnp.bfloat16)


def row_terms(rotated, cell_rows, count, img_rows, grid):
    chans = rotated.shape[1] // 2
    nu_vals = channel_nu(chans)
    power_list = [jnp.ones_like(nu_vals)]
    for term in range(TERMS - 1):
        power_list.append(power_list[-1] * nu_vals)
    powers = jnp.tile(jnp.stack(power_list), (1, rotated.shape[0]))
    offset = jnp.arange(count, dtype=jnp.int32) - img_rows // 2
    turns = jnp.mod(offset[:, None] * cell_rows[None, :], grid)
    alpha = turns.astype(jnp.float32) * (2.0 * math.pi / grid)
    cosine = jnp.cos(alpha)
    sine = jnp.sin(alpha)
    real_part = rotated[:, :chans].astype(jnp.float32).reshape(-1)
    imag_part = rotated[:, chans:].astype(jnp.float32).reshape(-1)
    base_real = cosine * real_part[None, :] - sine * imag_part[None, :]
    base_imag = cosine * imag_part[None, :] + sine * real_part[None, :]
    stacked = jnp.stack(
        [base_real[:, None, :] * powers[None], base_imag[:, None, :] * powers[None]], axis=1
    )
    return stacked.astype(jnp.bfloat16)


def dft_table(grid, first, width):
    cell_index = jnp.arange(grid, dtype=jnp.int32)
    pixels = first + jnp.arange(width, dtype=jnp.int32) - grid // 2
    turns = jnp.mod(cell_index[:, None] * pixels[None, :], grid)
    theta = turns.astype(jnp.float32) * (2.0 * math.pi / grid)
    return jnp.concatenate([jnp.cos(theta), -jnp.sin(theta)], axis=0).astype(jnp.bfloat16)


def grid_rows_of(rotated, cell_rows, cell_cols, count, img_rows):
    chans = rotated.shape[1] // 2
    num_rows = rotated.shape[0]
    step_rows = math.gcd(num_rows, max(1, 512 // chans))
    blocks = num_rows // step_rows
    rot_blocks = rotated.reshape(blocks, step_rows, 2 * chans)
    row_blocks = cell_rows.reshape(blocks, step_rows * chans)
    col_blocks = cell_cols.reshape(blocks, step_rows * chans)
    columns = jnp.arange(GRID, dtype=jnp.int32)

    def one_step(carry, item):
        rot_block, row_block, col_block = item
        values = row_terms(rot_block, row_block, count, img_rows, GRID)
        left_side = values.reshape(count * 2 * TERMS, step_rows * chans)
        one_hot = (col_block[:, None] == columns[None, :]).astype(jnp.bfloat16)
        return (carry + jnp.dot(left_side, one_hot, preferred_element_type=jnp.float32), None)

    empty = jnp.zeros((count * 2 * TERMS, GRID), jnp.float32)
    total, unused = lax.scan(one_step, empty, (rot_blocks, row_blocks, col_blocks))
    return total.reshape(count, 2, TERMS, GRID)


def transform_columns(rowsum, block_width):
    rows = rowsum.shape[0]
    left_side = rowsum.astype(jnp.bfloat16).transpose(0, 2, 1, 3).reshape(rows * TERMS, 2 * GRID)

    def one_block(position):
        table = dft_table(GRID, position * block_width, block_width)
        return jnp.dot(left_side, table, preferred_element_type=jnp.float32)

    blocks = lax.map(one_block, jnp.arange(GRID // block_width, dtype=jnp.int32))
    return blocks.transpose(1, 0, 2).reshape(rows * TERMS, GRID)


def per_device(visibilities, uv_coords, cells, centres, intersection_mask):
    rows_dev = intersection_mask.shape[1]
    img_rows = rows_dev * lax.axis_size("vis")
    vis_all = visibilities.shape[0] * lax.axis_size("vis") * CH
    rotated = rotate_rows(visibilities, uv_coords, centres[0])
    rowsum = lax.psum_scatter(
        grid_rows_of(rotated, cells[0], cells[1], rows_dev * lax.axis_size("vis"), img_rows),
        "vis",
        scatter_dimension=0,
        tiled=True,
    )
    block_width = 512
    image = transform_columns(rowsum, block_width).reshape(rows_dev, TERMS, GRID).transpose(1, 0, 2)
    image = image * (1.0 / math.sqrt(vis_all))
    strip = image[:, :, GRID - OVER :]
    neighbour = from_behind(strip, "facet", 1)
    ramp = 1.0 - (jnp.arange(OVER, dtype=jnp.float32) + 0.5) / OVER
    has_left = (lax.axis_index("facet") > 0).astype(jnp.float32)
    weight = intersection_mask[0].astype(jnp.float32) * ramp[None, :] * has_left
    head = image[:, :, :OVER] + weight[None] * (neighbour - image[:, :, :OVER])
    return jnp.concatenate([head, image[:, :, OVER:]], axis=2)


def solution(mesh):
    placed = (
        P("vis", None),
        P("vis", None),
        P(None, "vis", None),
        P("facet", None),
        P("facet", "vis", None),
    )
    return jax.shard_map(
        per_device, mesh=mesh, in_specs=placed, out_specs=P(None, "vis", "facet"), check_vma=False
    )
```

profile of v0, /device:TPU:1, one launch (start us, length us, event | category | flops | bytes accessed | tf_op | source)
XLA Modules:
  0.0 821.2 jit_solution(12095056442273497291)
XLA Ops:
  2.2 2.0 multiply_bitcast_fusion.1
  5.2 36.3 %while.28 = (s32[]{:T(128)}, f32[384,4096]{1,0:T(8,128)}, s32[4,512]{1,0:T(4,128)S(1)}, bf16[4,8,128]{2,1,0:T(8,128)(2,1)S(1)}, s32[4,512]{1,0:T(4,128)S(1)}, /*index=5*/s32[]{:T(128)}, f32[]{:T(128)}, f32[]{:T(128)}, s32[]{:T(128)}) while((s32[]{:T(128)}, f32[384,4096]{1,0:T(8,128)}, s32[4,512]{1,0:T(4,128)S(1)}, ...), condition=%wide.region_1.2_spmd.clone, body=%wide.region_0.1_spmd.clone.sunk | while | flops 1617102592 | bytes 15529103 | solution.py:87
  7.2 5.0 select_add_fusion.2
  14.1 7.8 select_add_fusion.2
  23.9 7.8 select_add_fusion.2
  33.7 7.8 select_add_fusion.2
  41.5 9.1 %reshape.262 = f32[64,2,3,4096]{3,2,1,0:T(4,128)} reshape(f32[384,4096]{1,0:T(8,128)} %get-tuple-element.185) | data formatting | bytes 12582912 | tf_op jit(solution)/shard_map/reshape | solution.py:88
  50.6 11.9 %copy.8 = f32[64,2,3,4096]{3,1,2,0:T(2,128)} copy(f32[64,2,3,4096]{3,2,1,0:T(4,128)} %reshape.262) | data formatting | bytes 12582912 | tf_op jit(solution)/shard_map/reshape | solution.py:88
  62.5 408.6 %all-reduce.2 = bf16[64,2,3,4096]{3,1,2,0:T(2,128)(2,1)S(1)} all-reduce(f32[64,2,3,4096]{3,1,2,0:T(2,128)} %copy.8), channel_id=2, replica_groups=mesh['facet'=4,'vis'=64] {'vis'}, use_global_device_ids=true, to_apply=%region_2.3.clone | all-reduce | flops 1572864 | bytes 9437184
  472.5 293.8 %while.27 = (s32[]{:T(128)}, f32[8,3,512]{2,1,0:T(4,128)S(1)}, s32[8]{0:T(128)S(1)}, bf16[3,8192]{1,0:T(4,128)(2,1)S(1)}, s32[]{:T(128)}, /*index=5*/s32[1]{0:T(128)}) while((s32[]{:T(128)}, f32[8,3,512]{2,1,0:T(4,128)S(1)}, s32[8]{0:T(128)S(1)}, bf16[3,8192]{1,0:T(4,128)(2,1)S(1)}, s32[]{:T(128)}, /*index=5*/s32[1]{0:T(128)}) %tuple.86), condition=%wide.region_4.5_spmd, body=%wide.region_3.4_spmd.sunk | while | flops 77595648 | bytes 16855140 | solution.py:99
  473.8 34.1 %cosine_convert_fusion.2 = (bf16[4096,512]{1,0:T(8,128)(2,1)S(1)}, bf16[4096,512]{1,0:T(8,128)(2,1)S(1)}) fusion(s32[512]{0:T(512)S(1)} %add_add_fusion.2), kind=kLoop, calls=%fused_computation.12.clone.1 | loop fusion | flops 35651584 | bytes 8390656 | tf_op jit(solution)/shard_map/convert
  507.9 1.4 fusion.48
  510.5 34.1 %cosine_convert_fusion.2 = (bf16[4096,512]{1,0:T(8,128)(2,1)S(1)}, bf16[4096,512]{1,0:T(8,128)(2,1)S(1)}) fusion(s32[512]{0:T(512)S(1)} %add_add_fusion.2), kind=kLoop, calls=%fused_computation.12.clone.1 | loop fusion | flops 35651584 | bytes 8390656 | tf_op jit(solution)/shard_map/convert
  544.6 1.4 fusion.48
  547.2 34.1 %cosine_convert_fusion.2 = (bf16[4096,512]{1,0:T(8,128)(2,1)S(1)}, bf16[4096,512]{1,0:T(8,128)(2,1)S(1)}) fusion(s32[512]{0:T(512)S(1)} %add_add_fusion.2), kind=kLoop, calls=%fused_computation.12.clone.1 | loop fusion | flops 35651584 | bytes 8390656 | tf_op jit(solution)/shard_map/convert
  584.0 34.1 %cosine_convert_fusion.2 = (bf16[4096,512]{1,0:T(8,128)(2,1)S(1)}, bf16[4096,512]{1,0:T(8,128)(2,1)S(1)}) fusion(s32[512]{0:T(512)S(1)} %add_add_fusion.2), kind=kLoop, calls=%fused_computation.12.clone.1 | loop fusion | flops 35651584 | bytes 8390656 | tf_op jit(solution)/shard_map/convert
  618.1 1.4 fusion.48
  620.7 34.1 %cosine_convert_fusion.2 = (bf16[4096,512]{1,0:T(8,128)(2,1)S(1)}, bf16[4096,512]{1,0:T(8,128)(2,1)S(1)}) fusion(s32[512]{0:T(512)S(1)} %add_add_fusion.2), kind=kLoop, calls=%fused_computation.12.clone.1 | loop fusion | flops 35651584 | bytes 8390656 | tf_op jit(solution)/shard_map/convert
  654.8 1.4 fusion.48
  657.4 34.1 %cosine_convert_fusion.2 = (bf16[4096,512]{1,0:T(8,128)(2,1)S(1)}, bf16[4096,512]{1,0:T(8,128)(2,1)S(1)}) fusion(s32[512]{0:T(512)S(1)} %add_add_fusion.2), kind=kLoop, calls=%fused_computation.12.clone.1 | loop fusion | flops 35651584 | bytes 8390656 | tf_op jit(solution)/shard_map/convert
  694.2 34.1 %cosine_convert_fusion.2 = (bf16[4096,512]{1,0:T(8,128)(2,1)S(1)}, bf16[4096,512]{1,0:T(8,128)(2,1)S(1)}) fusion(s32[512]{0:T(512)S(1)} %add_add_fusion.2), kind=kLoop, calls=%fused_computation.12.clone.1 | loop fusion | flops 35651584 | bytes 8390656 | tf_op jit(solution)/shard_map/convert
  730.9 34.1 %cosine_convert_fusion.2 = (bf16[4096,512]{1,0:T(8,128)(2,1)S(1)}, bf16[4096,512]{1,0:T(8,128)(2,1)S(1)}) fusion(s32[512]{0:T(512)S(1)} %add_add_fusion.2), kind=kLoop, calls=%fused_computation.12.clone.1 | loop fusion | flops 35651584 | bytes 8390656 | tf_op jit(solution)/shard_map/convert
  765.0 1.4 fusion.48
  766.5 53.3 %collective-permute-start = (f32[3,1,256]{2,1,0:T(1,128)S(1)}, f32[3,1,256]{2,1,0:T(1,128)S(1)}, u32[]{:S(2)}, u32[]{:S(2)}) collective-permute-start(f32[3,1,256]{2,1,0:T(1,128)S(1)} %slice.68), channel_id=1, source_target_pairs={{0,64},{64,128},{128,192},{1,65},{65,129},{129,193},{2,66},{66,130... | collective-permute-start | bytes 9224 | tf_op jit(solution)/shard_map/ppermute | solution.py:17
  (105 shorter events, 23.0 us)
Async XLA Ops:
  62.5 408.6 %copy-start.1 = (u32[256]{0:T(256)S(1)}, u32[256]{0:T(256)}, u32[]{:S(2)}) copy-start(u32[256]{0:T(256)} %constant.185) | copy-start | bytes 3076
  472.5 347.3 %copy-start = (s32[1,1,256]{2,1,0:T(1,128)S(1)}, s32[1,1,256]{2,1,0:T(1,128)}, u32[]{:S(2)}) copy-start(s32[1,1,256]{2,1,0:T(1,128)} %param.13) | copy-start | bytes 3076
  766.5 54.0 %collective-permute-start = (f32[3,1,256]{2,1,0:T(1,128)S(1)}, f32[3,1,256]{2,1,0:T(1,128)S(1)}, u32[]{:S(2)}, u32[]{:S(2)}) collective-permute-start(f32[3,1,256]{2,1,0:T(1,128)S(1)} %slice.68), channel_id=1, source_target_pairs={{0,64},{64,128},{128,192},{1,65},{65,129},{129,193},{2,66},{66,130... | collective-permute-start | bytes 9224 | tf_op jit(solution)/shard_map/ppermute | solution.py:17
where the time goes:
time: 822 us; the launch traced here: 821 us
  blocking collectives  409 us (50%)
  other arithmetic  281 us (34%)
  starting transfers between devices  53.3 us (6%)
  matrix products  39.3 us (5%)
  local copies, waits for them, and re-layouts  32.3 us (4%)
    unnamed x1, blocking collectives  409 us
    another operation x12, other arithmetic  273 us
    ppermute x1, starting transfers between devices, from_behind(): return lax.ppermute(shard, axis, pairs)  53.3 us
    dot_general x4, matrix products, one_step(): jnp.dot(left_side, one_hot, preferred_element_type=jnp.float32)  28.5 us
    reshape x2, local copies, waits for them, and re-layouts, grid_rows_of(): return total.reshape(count, 2, TERMS, GRID)  21 us
  transfers between devices with their start and end apart: 1, of which 1 were waited for; matrix products, arithmetic and copies ran while one was open for 0% of the time, Pallas kernels for 0%

commit v1 on v0

v1 whole, which is shorter than its diff:
```python
import math

import jax
import jax.numpy as jnp
import numpy as np
from jax import lax
from jax.experimental import pallas as pl
from jax.experimental.pallas import tpu as pltpu
from jax.sharding import PartitionSpec as P

GRID = 4096
CH = 64
TERMS = 3
OVER = 256
FACETS = 4
VIS_ROWS = 2048
IMG_ROWS = 64
VIS_ALL = VIS_ROWS * CH
SIDE = 4
BLOCKS = SIDE * SIDE
ROWS = VIS_ROWS // IMG_ROWS
HALF = ROWS // 2
SECT = 7
FINE = 8
COARSE = GRID // 2 // FINE
XB = GRID // FINE
VALS = FACETS * TERMS
CHUNK = 32

COS = (0.99999999, -19.73920447, 64.93911593, -85.45011343, 60.16742979, -25.96688461, 6.52770596)
SIN = (6.28318491, -41.3415883, 81.59991362, -76.6141403, 41.34136538, -12.46881862)


def tables():
    gh = np.arange(COARSE)[:, None]
    xb = np.arange(XB)[None, :]
    ang = 2 * np.pi * ((gh * xb) % XB) / XB
    cosine, sine = np.cos(ang), np.sin(ang)
    first = np.concatenate(
        [np.concatenate([cosine, sine], 1), np.concatenate([-sine, cosine], 1)], 0
    )
    gl = np.arange(FINE)[:, None]
    tw = 2 * np.pi * (gl * xb) / GRID
    scale = np.where(gl % 2 == 0, 1.0, -1.0) / math.sqrt(VIS_ALL)
    twiddle = np.concatenate([np.cos(tw) * scale, np.sin(tw) * scale], 0)
    xa = np.arange(FINE)[:, None]
    turn = 2 * np.pi * ((xa * np.arange(FINE)[None, :]) % FINE) / FINE
    real, imag = np.cos(turn), -np.sin(turn)
    imag[:, 0] = 1.0
    eye = np.eye(VALS)
    second = np.concatenate([np.kron(eye, real), np.kron(eye, imag)], 1)
    return (
        jnp.asarray(first, jnp.bfloat16),
        jnp.asarray(twiddle, jnp.float32),
        jnp.asarray(second, jnp.float32),
    )


def turns_cos_sin(turns):
    frac = turns - jnp.round(turns)
    sq = frac * frac
    cosine = jnp.full_like(sq, COS[-1])
    for coef in COS[-2::-1]:
        cosine = cosine * sq + coef
    sine = jnp.full_like(sq, SIN[-1])
    for coef in SIN[-2::-1]:
        sine = sine * sq + coef
    return cosine, sine * frac


def pack_kernel(vis_ref, uv_ref, cells_ref, centre_ref, out_ref):
    lane = lax.broadcasted_iota(jnp.int32, (HALF, 2 * CH), 1)
    left = lane < CH
    vis = vis_ref[...].astype(jnp.float32)
    top, low = vis[:HALF], vis[HALF:]
    out_ref[0:16] = jnp.where(left, top, pltpu.roll(low, CH, 1)).astype(jnp.bfloat16)
    out_ref[16:32] = jnp.where(left, pltpu.roll(top, CH, 1), low).astype(jnp.bfloat16)
    for which in range(2):
        cells = cells_ref[which]
        both = jnp.concatenate([cells[:HALF], cells[HALF:]], 1)
        at = 32 + 32 * which
        out_ref[at : at + 16] = (both >> 6).astype(jnp.float32).astype(jnp.bfloat16)
        out_ref[at + 16 : at + 32] = (both & 63).astype(jnp.float32).astype(jnp.bfloat16)

    def pieces(value):
        high = value.astype(jnp.bfloat16).astype(jnp.float32)
        rest = value - high
        mid = rest.astype(jnp.bfloat16).astype(jnp.float32)
        return [high, mid, rest - mid]

    uv = uv_ref[...]
    cen = jnp.broadcast_to(centre_ref[...], (HALF, 2))
    zero = jnp.zeros((HALF, CH - 12), jnp.float32)
    whole = jnp.concatenate(
        pieces(uv[:HALF]) + pieces(cen) + [zero] + pieces(uv[HALF:]) + pieces(cen) + [zero], 1
    )
    out_ref[96:112] = whole.astype(jnp.bfloat16)


def grid_kernel(
    place_ref, blocks_ref, first_ref, twiddle_ref, second_ref, o0, o1, o2, o3,
    terms_ref, cell_ref, left0, left1, right0, right1, total_ref, image_ref,
):
    own, zpos, row = place_ref[0], place_ref[1], place_ref[2]
    lane = lax.broadcasted_iota(jnp.int32, (HALF, 2 * CH), 1)
    chan = (lane % CH).astype(jnp.float32)
    nu = (2.0 * chan + 1.0 - CH) / CH
    freq = 1.0 + 0.15 * nu
    nu2 = nu * nu
    step = (row - IMG_ROWS // 2).astype(jnp.float32) * (1.0 / GRID)
    fine_iota = lax.broadcasted_iota(jnp.int32, (FINE, 2 * CH), 0)
    coarse_iota = lax.broadcasted_iota(jnp.int32, (COARSE, 2 * CH), 0)

    def joined(section):
        return section + pltpu.roll(section, 2 * CH - 2, 1) + pltpu.roll(section, 2 * CH - 4, 1)

    cens = []
    for q in range(SIDE):
        sect = joined(blocks_ref[q * SIDE, 96:112].astype(jnp.float32))
        cens.append((sect[0:1, 6:7], sect[0:1, 7:8]))

    def build(block, left_ref, right_ref):
        def section(at):
            return blocks_ref[block, 16 * at : 16 * at + 16].astype(jnp.float32)

        real, imag = section(0), section(1)
        gr = section(2) * 64.0 + section(3)
        gc = section(4) * 64.0 + section(5)
        place = joined(section(6))
        is_left = lane < CH
        u = jnp.where(is_left, place[:, 0:1], place[:, CH : CH + 1])
        v = jnp.where(is_left, place[:, 1:2], place[:, CH + 1 : CH + 2])
        mid = (gc == float(GRID // 2)).astype(jnp.float32)
        folded = jnp.where(gc > GRID // 2, GRID - gc, gc * (1.0 - mid))
        sign = jnp.where(gc > GRID // 2, -1.0, jnp.where(folded == 0.0, 0.0, 1.0))
        cell = folded.astype(jnp.int32)
        cell_ref[0] = cell & (FINE - 1)
        cell_ref[1] = cell >> (FINE.bit_length() - 1)
        keep = 1.0 - mid
        ca, sa = turns_cos_sin(gr * step)
        for q in range(SIDE):
            proj = u * cens[q][0] + v * cens[q][1]
            cp, sp = turns_cos_sin(proj * freq)
            rr = (real * cp + imag * sp).astype(jnp.bfloat16).astype(jnp.float32)
            ri = (imag * cp - real * sp).astype(jnp.bfloat16).astype(jnp.float32)
            br = ca * rr - sa * ri
            bi = ca * ri + sa * rr
            bi = bi * sign + br * mid
            br = br * keep
            for part, base in ((0, br), (1, bi)):
                at = part * VALS + q * TERMS
                terms_ref[at] = base
                terms_ref[at + 1] = base * nu
                terms_ref[at + 2] = base * nu2
        for i in range(HALF):
            fine = jnp.broadcast_to(cell_ref[0, i : i + 1, :], (FINE, 2 * CH)) == fine_iota
            vals = jnp.broadcast_to(terms_ref[:, i : i + 1, :], (2 * VALS, FINE, 2 * CH))
            vals = jnp.where(fine[None], vals, 0.0)
            cols = slice(i * 2 * CH, (i + 1) * 2 * CH)
            left_ref[:, cols] = vals.reshape(2 * VALS * FINE, 2 * CH).astype(jnp.bfloat16)
            coarse = jnp.broadcast_to(cell_ref[1, i : i + 1, :], (COARSE, 2 * CH)) == coarse_iota
            right_ref[:, cols] = jnp.where(coarse, 1.0, 0.0).astype(jnp.bfloat16)

    def add(left_ref, right_ref):
        total_ref[...] += lax.dot_general(
            left_ref[...], right_ref[...], (((1,), (1,)), ((), ())),
            preferred_element_type=jnp.float32,
        )

    total_ref[...] = jnp.zeros_like(total_ref)
    build(0, left0, right0)

    def two(i, carry):
        add(left0, right0)
        build(2 * i + 1, left1, right1)
        add(left1, right1)
        build(jnp.minimum(2 * i + 2, BLOCKS - 1), left0, right0)
        return carry

    lax.fori_loop(0, BLOCKS // 2, two, 0)

    span = VALS * FINE
    total = jnp.concatenate([total_ref[0:span], total_ref[span : 2 * span]], 1)
    mixed = jnp.dot(total.astype(jnp.bfloat16), first_ref[...], preferred_element_type=jnp.float32)
    ur = mixed[:, :XB].reshape(VALS, FINE, XB)
    ui = mixed[:, XB:].reshape(VALS, FINE, XB)
    wr, wi = twiddle_ref[0:FINE][None], twiddle_ref[FINE : 2 * FINE][None]
    vr = ur * wr - ui * wi
    vi = ur * wi + ui * wr
    middle = total[:, COARSE : COARSE + 1].reshape(VALS, FINE, 1)
    odd = lax.broadcasted_iota(jnp.int32, (1, 1, XB), 2) % 2 == 1
    flip = jnp.where(odd, -1.0, 1.0) * (1.0 / math.sqrt(VIS_ALL))
    at_zero = lax.broadcasted_iota(jnp.int32, (1, FINE, XB), 1) == 0
    vi = jnp.where(at_zero, middle * flip, vi)
    both = jnp.concatenate([vr.reshape(span, XB), vi.reshape(span, XB)], 0)
    image_ref[...] = jnp.dot(
        second_ref[...], both, preferred_element_type=jnp.float32, precision=lax.Precision.HIGHEST
    )
    size = TERMS * FINE
    for s, out in enumerate((o0, o1, o2, o3)):
        facet = lax.rem(own + s, FACETS)
        spot = lax.rem(facet - zpos + FACETS, FACETS)
        before = lax.rem(facet - zpos + 2 * FACETS - 1, FACETS)
        out[0:size] = image_ref[pl.ds(pl.multiple_of(spot * size, 8), size), :]
        prior = image_ref[pl.ds(pl.multiple_of(before * size, 8), size), :]
        for term in range(TERMS):
            at = term * FINE + FINE - 1
            out[size + term : size + term + 1, 0:OVER] = prior[at : at + 1, XB - OVER :]


def blend_kernel(place_ref, p0, p1, p2, p3, mask_ref, out_ref):
    size = TERMS * FINE
    image = (p0[0:size] + p1[0:size]) + (p2[0:size] + p3[0:size])
    tail = slice(size, size + TERMS)
    strip = (p0[tail, 0:OVER] + p1[tail, 0:OVER]) + (p2[tail, 0:OVER] + p3[tail, 0:OVER])
    has_left = (place_ref[0] > 0).astype(jnp.float32)
    pixel = lax.broadcasted_iota(jnp.int32, (1, OVER), 1).astype(jnp.float32)
    ramp = 1.0 - (pixel + 0.5) / OVER
    weight = mask_ref[0].astype(jnp.float32) * ramp * has_left
    for term in range(TERMS):
        for xa in range(FINE):
            line = image[term * FINE + xa : term * FINE + xa + 1]
            if xa == 0:
                head = line[:, :OVER]
                head = head + weight * (strip[term : term + 1] - head)
                out_ref[term, :, 0:OVER] = head
                out_ref[term, :, OVER:XB] = line[:, OVER:]
            else:
                out_ref[term, :, xa * XB : (xa + 1) * XB] = line


def swap_pairs():
    pairs = []
    for facet in range(FACETS):
        for z in range(SIDE):
            for y in range(SIDE):
                for x in range(SIDE):
                    source = facet * IMG_ROWS + z * BLOCKS + y * SIDE + x
                    target = z * IMG_ROWS + ((facet - y) % FACETS) * BLOCKS + y * SIDE + x
                    pairs.append((source, target))
    return pairs


def per_device(visibilities, uv_coords, cells, centres, intersection_mask):
    vmem = pl.BlockSpec(memory_space=pltpu.VMEM)
    smem = pl.BlockSpec(memory_space=pltpu.SMEM)
    facet, spot = lax.axis_index("facet"), lax.axis_index("vis")
    place = jnp.stack([facet, spot // BLOCKS, spot]).astype(jnp.int32)
    packed = pl.pallas_call(
        pack_kernel,
        out_shape=jax.ShapeDtypeStruct((16 * SECT, 2 * CH), jnp.bfloat16),
        in_specs=[vmem] * 4,
        out_specs=vmem,
        name="pack",
    )(visibilities, uv_coords, cells, centres)
    packed = lax.ppermute(packed, ("facet", "vis"), swap_pairs())
    planes = [[z * BLOCKS + i for i in range(BLOCKS)] for z in range(SIDE)]
    blocks = lax.all_to_all(
        jnp.broadcast_to(packed[None], (BLOCKS,) + packed.shape),
        "vis", 0, 0, axis_index_groups=planes,
    )
    first, twiddle, second = tables()
    chunk = jax.ShapeDtypeStruct((CHUNK, XB), jnp.float32)
    span = 2 * VALS * FINE
    wide = ROWS * CH
    parts = pl.pallas_call(
        grid_kernel,
        out_shape=[chunk] * FACETS,
        in_specs=[smem] + [vmem] * 4,
        out_specs=[vmem] * FACETS,
        scratch_shapes=[
            pltpu.VMEM((2 * VALS, HALF, 2 * CH), jnp.float32),
            pltpu.VMEM((2, HALF, 2 * CH), jnp.int32),
            pltpu.VMEM((span, wide), jnp.bfloat16),
            pltpu.VMEM((span, wide), jnp.bfloat16),
            pltpu.VMEM((COARSE, wide), jnp.bfloat16),
            pltpu.VMEM((COARSE, wide), jnp.bfloat16),
            pltpu.VMEM((span, COARSE), jnp.float32),
            pltpu.VMEM((VALS * FINE, XB), jnp.float32),
        ],
        compiler_params=pltpu.CompilerParams(vmem_limit_bytes=40 << 20),
        name="grid",
    )(place, blocks, first, twiddle, second)
    got = [parts[0]]
    for s in range(1, FACETS):
        got.append(lax.ppermute(parts[s], "facet", [(i, (i + s) % FACETS) for i in range(FACETS)]))
    return pl.pallas_call(
        blend_kernel,
        out_shape=jax.ShapeDtypeStruct((TERMS, 1, GRID), jnp.float32),
        in_specs=[smem] + [vmem] * 5,
        out_specs=vmem,
        name="blend",
    )(place, *got, intersection_mask)


def solution(mesh):
    placed = (
        P("vis", None),
        P("vis", None),
        P(None, "vis", None),
        P("facet", None),
        P("facet", "vis", None),
    )
    return jax.shard_map(
        per_device, mesh=mesh, in_specs=placed, out_specs=P(None, "vis", "facet"), check_vma=False
    )
```

time: 822 us -> 56 us (0.07)
  blocking collectives: 409 us -> 0 us
  other arithmetic: 281 us -> 0.08 us
  matrix products: 39.3 us -> 0 us
  starting transfers between devices: 53.3 us -> 20 us
  local copies, waits for them, and re-layouts: 32.3 us -> 3.54 us
  Pallas kernels: 0 us -> 17.1 us
  waiting for transfers between devices: 0.67 us -> 14.8 us
    unnamed x1 -> x0, blocking collectives: 409 us -> none
    another operation x20 -> x1, other arithmetic: 275 us -> 0.08 us  [per_device(): place = jnp.stack([facet, spot // BLOCKS, spot]).astype(jnp.int32)]
    ppermute x1 -> x4, starting transfers between devices: 53.3 us -> 9.99 us  [the longest x1 6.28 us: per_device(): packed = lax.ppermute(packed, ('facet', 'vis'), swap_pairs())]
    dot_general x12 -> x0, matrix products: 39.3 us -> none  [the longest x4 28.5 us: one_step(): jnp.dot(left_side, one_hot, preferred_element_type=jnp.float32)]
    reshape x2 -> x0, local copies, waits for them, and re-layouts: 21 us -> none  [grid_rows_of(): return total.reshape(count, 2, TERMS, GRID)]
    pallas_call x0 -> x3, Pallas kernels: none -> 17.1 us  [the longest x1 14.1 us: per_device(): pl.pallas_call(grid_kernel, out_shape=[chunk] * FACETS, in_specs=[smem] +...]
    all_to_all x0 -> x1, starting transfers between devices: none -> 10 us  [per_device(): lax.all_to_all(jnp.broadcast_to(packed[None], (BLOCKS,) + packed.shape),...]
    all_to_all x0 -> x1, waiting for transfers between devices: none -> 9.28 us  [per_device(): lax.all_to_all(jnp.broadcast_to(packed[None], (BLOCKS,) + packed.shape),...]
  transfers between devices with their start and end apart: 1 -> 5, of which waited for: 1 -> 5; matrix products, arithmetic and copies ran while one was open for 0% -> 0% of each run, Pallas kernels for 0% -> 0%
where the time goes in v1:
time: 56 us; the launch traced here: 55.6 us
  starting transfers between devices  20 us (36%)
  Pallas kernels  17.1 us (31%)
  waiting for transfers between devices  14.8 us (26%)
  local copies, waits for them, and re-layouts  3.54 us (6%)
    pallas_call x1, Pallas kernels, per_device(): pl.pallas_call(grid_kernel, out_shape=[chunk] * FACETS, in_specs=[smem] +...  14.1 us
    all_to_all x1, starting transfers between devices, per_device(): lax.all_to_all(jnp.broadcast_to(packed[None], (BLOCKS,) + packed.shape),...  10 us
    all_to_all x1, waiting for transfers between devices, per_device(): lax.all_to_all(jnp.broadcast_to(packed[None], (BLOCKS,) + packed.shape),...  9.28 us
    ppermute x1, starting transfers between devices, per_device(): packed = lax.ppermute(packed, ('facet', 'vis'), swap_pairs())  6.28 us
    ppermute x3, waiting for transfers between devices, per_device(): lax.ppermute(parts[s], 'facet', [(i, (i + s) % FACETS) for i in range(FAC...  3.75 us
    ppermute x3, starting transfers between devices, per_device(): lax.ppermute(parts[s], 'facet', [(i, (i + s) % FACETS) for i in range(FAC...  3.71 us
    unnamed x17, local copies, waits for them, and re-layouts  2.71 us
    ppermute x1, waiting for transfers between devices, per_device(): packed = lax.ppermute(packed, ('facet', 'vis'), swap_pairs())  1.75 us
  transfers between devices with their start and end apart: 5, of which 5 were waited for; matrix products, arithmetic and copies ran while one was open for 0% of the time, Pallas kernels for 0%

profile of v1, /device:TPU:1, one launch (start us, length us, event | category | flops | bytes accessed | tf_op | source)
XLA Modules:
  0.0 55.6 jit_solution(10072210531744993988)
XLA Ops:
  0.0 1.4 %copy.9.uv_ref = f32[32,2]{1,0:T(8,128)} copy(f32[32,2]{0,1:T(2,128)} %param.9) | data formatting | bytes 512 | tf_op args[1]
  1.4 1.5 %pack.1 = bf16[112,128]{1,0:T(8,128)(2,1)} custom-call(bf16[32,128]{1,0:T(8,128)(2,1)} %vis_ref.1, f32[32,2]{1,0:T(8,128)} %copy.9.uv_ref, s32[2,32,64]{2,1,0:T(8,128)} %cells_ref.1, f32[1,2]{1,0:T(1,128)} %centre_ref.1), custom_call_target="tpu_custom_call" | custom-call | tf_op jit(solution)/shard_map/pack/pallas_call | solution.py:249
  2.9 6.3 %collective-permute-start = (bf16[112,128]{1,0:T(8,128)(2,1)}, bf16[112,128]{1,0:T(8,128)(2,1)S(1)}, u32[]{:S(2)}, u32[]{:S(2)}) collective-permute-start(bf16[112,128]{1,0:T(8,128)(2,1)} %pack.1), channel_id=1, source_target_pairs={{0,0},{1,1},{2,2},{3,3},{4,52},{5,53},{6,54},{7,55},{8,40},{9,41},... | collective-permute-start | bytes 86024 | tf_op jit(solution)/shard_map/ppermute | solution.py:256
  9.2 1.8 %collective-permute-done = bf16[112,128]{1,0:T(8,128)(2,1)S(1)} collective-permute-done((bf16[112,128]{1,0:T(8,128)(2,1)}, bf16[112,128]{1,0:T(8,128)(2,1)S(1)}, u32[]{:S(2)}, u32[]{:S(2)}) %collective-permute-start) | collective-permute-done | bytes 28704 | tf_op jit(solution)/shard_map/ppermute | solution.py:256
  11.0 0.8 %broadcast_in_dim.2 = bf16[16,112,128]{2,1,0:T(8,128)(2,1)} broadcast(bf16[112,128]{1,0:T(8,128)(2,1)S(1)} %collective-permute-done), dimensions={1,2} | broadcast | bytes 487424 | tf_op jit(solution)/shard_map/broadcast_in_dim | solution.py:259
  11.8 10.0 %all-to-all-start = ((bf16[16,112,128]{2,1,0:T(8,128)(2,1)}), bf16[16,112,128]{2,1,0:T(8,128)(2,1)S(1)}, u32[]{:S(2)}, u32[]{:S(2)}) async-start(bf16[16,112,128]{2,1,0:T(8,128)(2,1)} %broadcast_in_dim.2), calls=%async_computation | async-start | bytes 917504 | tf_op jit(solution)/shard_map/all_to_all | solution.py:258
  21.9 0.0 copy-start.3
  21.9 0.1 pad_add_fusion.place_ref
  22.0 9.3 %all-to-all-done.blocks_ref = bf16[16,112,128]{2,1,0:T(8,128)(2,1)S(1)} async-done(((bf16[16,112,128]{2,1,0:T(8,128)(2,1)}), bf16[16,112,128]{2,1,0:T(8,128)(2,1)S(1)}, u32[]{:S(2)}, u32[]{:S(2)}) %all-to-all-start) | async-done | bytes 458784 | tf_op jit(solution)/shard_map/all_to_all | solution.py:258
  31.3 0.0 copy-done
  31.3 0.0 copy-done.1
  31.3 0.0 copy-done.3
  31.3 14.1 %grid.1 = (f32[32,512]{1,0:T(8,128)S(1)}, f32[32,512]{1,0:T(8,128)S(1)}, f32[32,512]{1,0:T(8,128)S(1)}, f32[32,512]{1,0:T(8,128)S(1)}) custom-call(s32[3]{0:T(128)S(1)} %pad_add_fusion.place_ref, bf16[16,112,128]{2,1,0:T(8,128)(2,1)S(1)} %all-to-all-done.blocks_ref, bf16[512,1024]{1,0:T(8,128)(2,1)S(1)} %copy-done, f32[16,512]{1,0:T(8,128)S(1)} %copy-done.3, ...), custom_call_target="tpu_custom_call" | custom-call | tf_op jit(solution)/shard_map/grid/pallas_call | solution.py:266
  45.3 0.0 copy-done.4
  45.3 0.6 %copy-done.2 = f32[32,512]{1,0:T(8,128)} copy-done((f32[32,512]{1,0:T(8,128)}, f32[32,512]{1,0:T(8,128)S(1)}, u32[]{:S(2)}) %copy-start.2) | copy-done | bytes 65560
  45.9 3.0 %collective-permute-start.1 = (f32[32,512]{1,0:T(8,128)S(1)}, f32[32,512]{1,0:T(8,128)S(1)}, u32[]{:S(2)}, u32[]{:S(2)}) collective-permute-start(f32[32,512]{1,0:T(8,128)S(1)} %get-tuple-element.10), channel_id=1, source_target_pairs={{0,64},{64,128},{128,192},{192,0},{1,65},{65,129},{129,193},{193,1... | collective-permute-start | bytes 196616 | tf_op jit(solution)/shard_map/ppermute | solution.py:286
  48.9 0.7 %collective-permute-start.2 = (f32[32,512]{1,0:T(8,128)S(1)}, f32[32,512]{1,0:T(8,128)S(1)}, u32[]{:S(2)}, u32[]{:S(2)}) collective-permute-start(f32[32,512]{1,0:T(8,128)S(1)} %get-tuple-element.11), channel_id=1, source_target_pairs={{0,128},{64,192},{128,0},{192,64},{1,129},{65,193},{129,1},{193,65... | collective-permute-start | bytes 196616 | tf_op jit(solution)/shard_map/ppermute | solution.py:286
  49.7 0.0 collective-permute-start.3
  49.7 0.6 %collective-permute-done.1.p1 = f32[32,512]{1,0:T(8,128)S(1)} collective-permute-done((f32[32,512]{1,0:T(8,128)S(1)}, f32[32,512]{1,0:T(8,128)S(1)}, u32[]{:S(2)}, u32[]{:S(2)}) %collective-permute-start.1) | collective-permute-done | bytes 65568 | tf_op jit(solution)/shard_map/ppermute | solution.py:286
  50.3 2.6 %collective-permute-done.2.p2 = f32[32,512]{1,0:T(8,128)S(1)} collective-permute-done((f32[32,512]{1,0:T(8,128)S(1)}, f32[32,512]{1,0:T(8,128)S(1)}, u32[]{:S(2)}, u32[]{:S(2)}) %collective-permute-start.2) | collective-permute-done | bytes 65568 | tf_op jit(solution)/shard_map/ppermute | solution.py:286
  52.9 0.6 %collective-permute-done.3.p3 = f32[32,512]{1,0:T(8,128)S(1)} collective-permute-done((f32[32,512]{1,0:T(8,128)S(1)}, f32[32,512]{1,0:T(8,128)S(1)}, u32[]{:S(2)}, u32[]{:S(2)}) %collective-permute-start.3) | collective-permute-done | bytes 65568 | tf_op jit(solution)/shard_map/ppermute | solution.py:286
  53.4 0.1 copy-done.6
  53.5 0.6 %copy-done.7 = f32[32,512]{1,0:T(8,128)} copy-done((f32[32,512]{1,0:T(8,128)}, f32[32,512]{1,0:T(8,128)S(1)}, u32[]{:S(2)}) %copy-start.7) | copy-done | bytes 65560
  54.0 1.6 %blend.1 = f32[3,1,4096]{2,1,0:T(1,128)} custom-call(s32[3]{0:T(128)} %copy-done.4, f32[32,512]{1,0:T(8,128)} %copy-done.2, f32[32,512]{1,0:T(8,128)} %copy-done.5, f32[32,512]{1,0:T(8,128)} %copy-done.6, f32[32,512]{1,0:T(8,128)} %copy-done.7, s32[1,1,256]{2,1,0:T(1,128)} %mask_ref.1), custom_call_target="tpu_custom_call" | custom-call | tf_op jit(solution)/shard_map/blend/pallas_call | solution.py:287
  (8 shorter events, 0.0 us)
Async XLA Ops:
  0.0 31.3 %copy-start = (bf16[512,1024]{1,0:T(8,128)(2,1)S(1)}, bf16[512,1024]{1,0:T(8,128)(2,1)}, u32[]{:S(2)}) copy-start(bf16[512,1024]{1,0:T(8,128)(2,1)} %constant.31.clone.first_ref) | copy-start | bytes 3145732
  2.9 8.0 %collective-permute-start = (bf16[112,128]{1,0:T(8,128)(2,1)}, bf16[112,128]{1,0:T(8,128)(2,1)S(1)}, u32[]{:S(2)}, u32[]{:S(2)}) collective-permute-start(bf16[112,128]{1,0:T(8,128)(2,1)} %pack.1), channel_id=1, source_target_pairs={{0,0},{1,1},{2,2},{3,3},{4,52},{5,53},{6,54},{7,55},{8,40},{9,41},... | collective-permute-start | bytes 86024 | tf_op jit(solution)/shard_map/ppermute | solution.py:256
  11.8 19.4 %copy-start.1 = (f32[96,192]{1,0:T(8,128)S(1)}, f32[96,192]{1,0:T(8,128)}, u32[]{:S(2)}) copy-start(f32[96,192]{1,0:T(8,128)} %constant.33.clone.second_ref) | copy-start | bytes 221188
  11.8 19.4 %all-to-all-start = ((bf16[16,112,128]{2,1,0:T(8,128)(2,1)}), bf16[16,112,128]{2,1,0:T(8,128)(2,1)S(1)}, u32[]{:S(2)}, u32[]{:S(2)}) async-start(bf16[16,112,128]{2,1,0:T(8,128)(2,1)} %broadcast_in_dim.2), calls=%async_computation | async-start | bytes 917504 | tf_op jit(solution)/shard_map/all_to_all | solution.py:258
  21.9 9.4 %copy-start.3 = (f32[16,512]{1,0:T(8,128)S(1)}, f32[16,512]{1,0:T(8,128)}, u32[]{:S(2)}) copy-start(f32[16,512]{1,0:T(8,128)} %constant.32.clone.twiddle_ref) | copy-start | bytes 98308
  22.0 23.4 %copy-start.4 = (s32[3]{0:T(128)}, s32[3]{0:T(128)S(1)}, u32[]{:S(2)}) copy-start(s32[3]{0:T(128)S(1)} %pad_add_fusion.place_ref) | copy-start | bytes 40
  45.3 0.6 %copy-start.2 = (f32[32,512]{1,0:T(8,128)}, f32[32,512]{1,0:T(8,128)S(1)}, u32[]{:S(2)}) copy-start(f32[32,512]{1,0:T(8,128)S(1)} %get-tuple-element.9.p0) | copy-start | bytes 196612
  45.9 4.3 %collective-permute-start.1 = (f32[32,512]{1,0:T(8,128)S(1)}, f32[32,512]{1,0:T(8,128)S(1)}, u32[]{:S(2)}, u32[]{:S(2)}) collective-permute-start(f32[32,512]{1,0:T(8,128)S(1)} %get-tuple-element.10), channel_id=1, source_target_pairs={{0,64},{64,128},{128,192},{192,0},{1,65},{65,129},{129,193},{193,1... | collective-permute-start | bytes 196616 | tf_op jit(solution)/shard_map/ppermute | solution.py:286
  48.9 3.9 %collective-permute-start.2 = (f32[32,512]{1,0:T(8,128)S(1)}, f32[32,512]{1,0:T(8,128)S(1)}, u32[]{:S(2)}, u32[]{:S(2)}) collective-permute-start(f32[32,512]{1,0:T(8,128)S(1)} %get-tuple-element.11), channel_id=1, source_target_pairs={{0,128},{64,192},{128,0},{192,64},{1,129},{65,193},{129,1},{193,65... | collective-permute-start | bytes 196616 | tf_op jit(solution)/shard_map/ppermute | solution.py:286
  49.7 3.8 %collective-permute-start.3 = (f32[32,512]{1,0:T(8,128)S(1)}, f32[32,512]{1,0:T(8,128)S(1)}, u32[]{:S(2)}, u32[]{:S(2)}) collective-permute-start(f32[32,512]{1,0:T(8,128)S(1)} %get-tuple-element.12), channel_id=1, source_target_pairs={{0,192},{64,0},{128,64},{192,128},{1,193},{65,1},{129,65},{193,129... | collective-permute-start | bytes 196616 | tf_op jit(solution)/shard_map/ppermute | solution.py:286
  50.3 3.2 %copy-start.5 = (f32[32,512]{1,0:T(8,128)}, f32[32,512]{1,0:T(8,128)S(1)}, u32[]{:S(2)}) copy-start(f32[32,512]{1,0:T(8,128)S(1)} %collective-permute-done.1.p1) | copy-start | bytes 196612
  52.9 0.6 %copy-start.6 = (f32[32,512]{1,0:T(8,128)}, f32[32,512]{1,0:T(8,128)S(1)}, u32[]{:S(2)}) copy-start(f32[32,512]{1,0:T(8,128)S(1)} %collective-permute-done.2.p2) | copy-start | bytes 196612
  53.4 0.6 %copy-start.7 = (f32[32,512]{1,0:T(8,128)}, f32[32,512]{1,0:T(8,128)S(1)}, u32[]{:S(2)}) copy-start(f32[32,512]{1,0:T(8,128)S(1)} %collective-permute-done.3.p3) | copy-start | bytes 196612

commit v2 on v1

--- a/solution.py
+++ b/solution.py
@@ -25,6 +25,7 @@
 COARSE = GRID // 2 // FINE
 XB = GRID // FINE
 VALS = FACETS * TERMS
+STEP = 256
 CHUNK = 32
 
 COS = (0.99999999, -19.73920447, 64.93911593, -85.45011343, 60.16742979, -25.96688461, 6.52770596)
@@ -86,20 +87,26 @@
         high = value.astype(jnp.bfloat16).astype(jnp.float32)
         rest = value - high
         mid = rest.astype(jnp.bfloat16).astype(jnp.float32)
-        return [high, mid, rest - mid]
-
-    uv = uv_ref[...]
-    cen = jnp.broadcast_to(centre_ref[...], (HALF, 2))
-    zero = jnp.zeros((HALF, CH - 12), jnp.float32)
-    whole = jnp.concatenate(
-        pieces(uv[:HALF]) + pieces(cen) + [zero] + pieces(uv[HALF:]) + pieces(cen) + [zero], 1
-    )
+        return high, mid, rest - mid
+
+    split = jnp.concatenate(pieces(uv_ref[...]), 0).astype(jnp.bfloat16)
+    spots = lax.broadcasted_iota(jnp.int32, (6, 2 * CH), 0)
+    spots = spots == lax.broadcasted_iota(jnp.int32, (6, 2 * CH), 1)
+    columns = lax.dot_general(
+        split, spots.astype(jnp.float32).astype(jnp.bfloat16), (((0,), (0,)), ((), ())),
+        preferred_element_type=jnp.float32,
+    )
+    cen = jnp.where(lane % 2 == 0, centre_ref[0:1, 0:1], centre_ref[0:1, 1:2])
+    whole = columns[:HALF] + pltpu.roll(columns[HALF:], CH, 1)
+    for i, piece in enumerate(pieces(cen)):
+        whole = jnp.where(lane // 2 == 3 + i, piece, whole)
     out_ref[96:112] = whole.astype(jnp.bfloat16)
 
 
 def grid_kernel(
     place_ref, blocks_ref, first_ref, twiddle_ref, second_ref, o0, o1, o2, o3,
-    terms_ref, cell_ref, left0, left1, right0, right1, total_ref, image_ref,
+    terms0, terms1, cells0, cells1, left0, left1, right0, right1, total_ref, image_ref,
+    iota_ref,
 ):
     own, zpos, row = place_ref[0], place_ref[1], place_ref[2]
     lane = lax.broadcasted_iota(jnp.int32, (HALF, 2 * CH), 1)
@@ -108,8 +115,11 @@
     freq = 1.0 + 0.15 * nu
     nu2 = nu * nu
     step = (row - IMG_ROWS // 2).astype(jnp.float32) * (1.0 / GRID)
-    fine_iota = lax.broadcasted_iota(jnp.int32, (FINE, 2 * CH), 0)
-    coarse_iota = lax.broadcasted_iota(jnp.int32, (COARSE, 2 * CH), 0)
+    count = lax.broadcasted_iota(jnp.int32, (COARSE, 2 * CH), 0)
+    iota_ref[...] = count.astype(jnp.float32).astype(jnp.bfloat16)
+    fine_iota = (count[: 2 * FINE] & (FINE - 1)).astype(jnp.float32).astype(jnp.bfloat16)
+    one = jnp.ones((2 * FINE, 2 * CH), jnp.bfloat16)
+    zero = jnp.zeros((2 * FINE, 2 * CH), jnp.bfloat16)
 
     def joined(section):
         return section + pltpu.roll(section, 2 * CH - 2, 1) + pltpu.roll(section, 2 * CH - 4, 1)
@@ -119,7 +129,7 @@
         sect = joined(blocks_ref[q * SIDE, 96:112].astype(jnp.float32))
         cens.append((sect[0:1, 6:7], sect[0:1, 7:8]))
 
-    def build(block, left_ref, right_ref):
+    def elements(block, terms_ref, cell_ref):
         def section(at):
             return blocks_ref[block, 16 * at : 16 * at + 16].astype(jnp.float32)
 
@@ -134,8 +144,8 @@
         folded = jnp.where(gc > GRID // 2, GRID - gc, gc * (1.0 - mid))
         sign = jnp.where(gc > GRID // 2, -1.0, jnp.where(folded == 0.0, 0.0, 1.0))
         cell = folded.astype(jnp.int32)
-        cell_ref[0] = cell & (FINE - 1)
-        cell_ref[1] = cell >> (FINE.bit_length() - 1)
+        cell_ref[0] = (cell & (FINE - 1)).astype(jnp.float32)
+        cell_ref[1] = (cell >> (FINE.bit_length() - 1)).astype(jnp.float32)
         keep = 1.0 - mid
         ca, sa = turns_cos_sin(gr * step)
         for q in range(SIDE):
@@ -152,35 +162,56 @@
                 terms_ref[at] = base
                 terms_ref[at + 1] = base * nu
                 terms_ref[at + 2] = base * nu2
-        for i in range(HALF):
-            fine = jnp.broadcast_to(cell_ref[0, i : i + 1, :], (FINE, 2 * CH)) == fine_iota
-            vals = jnp.broadcast_to(terms_ref[:, i : i + 1, :], (2 * VALS, FINE, 2 * CH))
-            vals = jnp.where(fine[None], vals, 0.0)
-            cols = slice(i * 2 * CH, (i + 1) * 2 * CH)
-            left_ref[:, cols] = vals.reshape(2 * VALS * FINE, 2 * CH).astype(jnp.bfloat16)
-            coarse = jnp.broadcast_to(cell_ref[1, i : i + 1, :], (COARSE, 2 * CH)) == coarse_iota
-            right_ref[:, cols] = jnp.where(coarse, 1.0, 0.0).astype(jnp.bfloat16)
-
-    def add(left_ref, right_ref):
-        total_ref[...] += lax.dot_general(
-            left_ref[...], right_ref[...], (((1,), (1,)), ((), ())),
+
+    def expand(i, terms_ref, cell_ref, left_ref, right_ref):
+        cols = slice(i * 2 * CH, (i + 1) * 2 * CH)
+        fine = jnp.broadcast_to(cell_ref[0, i : i + 1, :], (2 * FINE, 2 * CH)).astype(jnp.bfloat16)
+        here = fine == fine_iota
+        vals = jnp.broadcast_to(terms_ref[:, i : i + 1, :], (2 * VALS, FINE, 2 * CH))
+        vals = vals.reshape(2 * VALS * FINE, 2 * CH).astype(jnp.bfloat16)
+        coarse = jnp.broadcast_to(cell_ref[1, i : i + 1, :], (2 * FINE, 2 * CH))
+        coarse = coarse.astype(jnp.bfloat16)
+        for m in range(VALS):
+            rows = slice(m * 2 * FINE, (m + 1) * 2 * FINE)
+            left_ref[rows, cols] = jnp.where(here, vals[rows], zero)
+        for m in range(COARSE // (2 * FINE)):
+            rows = slice(m * 2 * FINE, (m + 1) * 2 * FINE)
+            right_ref[rows, cols] = jnp.where(coarse == iota_ref[rows], one, zero)
+
+    def product(i, left_ref, right_ref):
+        cols = slice(i * STEP, (i + 1) * STEP)
+        return lax.dot_general(
+            right_ref[:, cols], left_ref[:, cols], (((1,), (1,)), ((), ())),
             preferred_element_type=jnp.float32,
         )
 
+    def turn(block, here, ahead):
+        part = total_ref[...]
+        per = STEP // (2 * CH)
+        elements(block, here[0], here[1])
+        for i in range(ROWS * CH // STEP):
+            part = part + product(i, here[2], here[3])
+            for j in range(per):
+                expand(i * per + j, *ahead)
+        total_ref[...] = part
+
+    even, odd = (terms0, cells0, left0, right0), (terms1, cells1, left1, right1)
     total_ref[...] = jnp.zeros_like(total_ref)
-    build(0, left0, right0)
+    elements(0, terms0, cells0)
+    for i in range(HALF):
+        expand(i, *even)
+    elements(1, terms1, cells1)
 
     def two(i, carry):
-        add(left0, right0)
-        build(2 * i + 1, left1, right1)
-        add(left1, right1)
-        build(jnp.minimum(2 * i + 2, BLOCKS - 1), left0, right0)
+        turn(jnp.minimum(2 * i + 2, BLOCKS - 1), even, odd)
+        turn(jnp.minimum(2 * i + 3, BLOCKS - 1), odd, even)
         return carry
 
     lax.fori_loop(0, BLOCKS // 2, two, 0)
 
     span = VALS * FINE
-    total = jnp.concatenate([total_ref[0:span], total_ref[span : 2 * span]], 1)
+    flat = total_ref[...].T
+    total = jnp.concatenate([flat[0:span], flat[span : 2 * span]], 1)
     mixed = jnp.dot(total.astype(jnp.bfloat16), first_ref[...], preferred_element_type=jnp.float32)
     ur = mixed[:, :XB].reshape(VALS, FINE, XB)
     ui = mixed[:, XB:].reshape(VALS, FINE, XB)
@@ -188,8 +219,8 @@
     vr = ur * wr - ui * wi
     vi = ur * wi + ui * wr
     middle = total[:, COARSE : COARSE + 1].reshape(VALS, FINE, 1)
-    odd = lax.broadcasted_iota(jnp.int32, (1, 1, XB), 2) % 2 == 1
-    flip = jnp.where(odd, -1.0, 1.0) * (1.0 / math.sqrt(VIS_ALL))
+    is_odd = lax.broadcasted_iota(jnp.int32, (1, 1, XB), 2) % 2 == 1
+    flip = jnp.where(is_odd, -1.0, 1.0) * (1.0 / math.sqrt(VIS_ALL))
     at_zero = lax.broadcasted_iota(jnp.int32, (1, FINE, XB), 1) == 0
     vi = jnp.where(at_zero, middle * flip, vi)
     both = jnp.concatenate([vr.reshape(span, XB), vi.reshape(span, XB)], 0)
@@ -251,8 +282,9 @@
         out_shape=jax.ShapeDtypeStruct((16 * SECT, 2 * CH), jnp.bfloat16),
         in_specs=[vmem] * 4,
         out_specs=vmem,
+        compiler_params=pltpu.CompilerParams(vmem_limit_bytes=2 << 20),
         name="pack",
-    )(visibilities, uv_coords, cells, centres)
+    )(visibilities, uv_coords.T, cells, centres)
     packed = lax.ppermute(packed, ("facet", "vis"), swap_pairs())
     planes = [[z * BLOCKS + i for i in range(BLOCKS)] for z in range(SIDE)]
     blocks = lax.all_to_all(
@@ -270,13 +302,16 @@
         out_specs=[vmem] * FACETS,
         scratch_shapes=[
             pltpu.VMEM((2 * VALS, HALF, 2 * CH), jnp.float32),
-            pltpu.VMEM((2, HALF, 2 * CH), jnp.int32),
+            pltpu.VMEM((2 * VALS, HALF, 2 * CH), jnp.float32),
+            pltpu.VMEM((2, HALF, 2 * CH), jnp.float32),
+            pltpu.VMEM((2, HALF, 2 * CH), jnp.float32),
             pltpu.VMEM((span, wide), jnp.bfloat16),
             pltpu.VMEM((span, wide), jnp.bfloat16),
             pltpu.VMEM((COARSE, wide), jnp.bfloat16),
             pltpu.VMEM((COARSE, wide), jnp.bfloat16),
-            pltpu.VMEM((span, COARSE), jnp.float32),
+            pltpu.VMEM((COARSE, span), jnp.float32),
             pltpu.VMEM((VALS * FINE, XB), jnp.float32),
+            pltpu.VMEM((COARSE, 2 * CH), jnp.bfloat16),
         ],
         compiler_params=pltpu.CompilerParams(vmem_limit_bytes=40 << 20),
         name="grid",
@@ -289,6 +324,7 @@
         out_shape=jax.ShapeDtypeStruct((TERMS, 1, GRID), jnp.float32),
         in_specs=[smem] + [vmem] * 5,
         out_specs=vmem,
+        compiler_params=pltpu.CompilerParams(vmem_limit_bytes=2 << 20),
         name="blend",
     )(place, *got, intersection_mask)
 

time: 56 us -> 51 us (0.911)
  Pallas kernels: 17.1 us -> 12.2 us
    pallas_call x1, Pallas kernels: 14.1 us -> 10.7 us  [per_device(): pl.pallas_call(grid_kernel, out_shape=[chunk] * FACETS, in_specs=[smem] +...]
    pallas_call x1, Pallas kernels: 1.49 us -> 0.24 us  [per_device(): pl.pallas_call(pack_kernel, out_shape=jax.ShapeDtypeStruct((16 * SECT, 2...]
    unnamed x17 -> x16, local copies, waits for them, and re-layouts: 2.71 us -> 2.89 us
where the time goes in v2:
time: 51 us; the launch traced here: 50.7 us
  starting transfers between devices  20.1 us (39%)
  waiting for transfers between devices  14.6 us (29%)
  Pallas kernels  12.2 us (24%)
  local copies, waits for them, and re-layouts  3.72 us (7%)
    pallas_call x1, Pallas kernels, per_device(): pl.pallas_call(grid_kernel, out_shape=[chunk] * FACETS, in_specs=[smem] +...  10.7 us
    all_to_all x1, starting transfers between devices, per_device(): lax.all_to_all(jnp.broadcast_to(packed[None], (BLOCKS,) + packed.shape),...  10 us
    all_to_all x1, waiting for transfers between devices, per_device(): lax.all_to_all(jnp.broadcast_to(packed[None], (BLOCKS,) + packed.shape),...  9.28 us
    ppermute x1, starting transfers between devices, per_device(): packed = lax.ppermute(packed, ('facet', 'vis'), swap_pairs())  6.29 us
    ppermute x3, starting transfers between devices, per_device(): lax.ppermute(parts[s], 'facet', [(i, (i + s) % FACETS) for i in range(FAC...  3.79 us
    ppermute x3, waiting for transfers between devices, per_device(): lax.ppermute(parts[s], 'facet', [(i, (i + s) % FACETS) for i in range(FAC...  3.75 us
    unnamed x16, local copies, waits for them, and re-layouts  2.89 us
    ppermute x1, waiting for transfers between devices, per_device(): packed = lax.ppermute(packed, ('facet', 'vis'), swap_pairs())  1.54 us
  transfers between devices with their start and end apart: 5, of which 5 were waited for; matrix products, arithmetic and copies ran while one was open for 0% of the time, Pallas kernels for 0%

profile of v2, /device:TPU:1, one launch (start us, length us, event | category | flops | bytes accessed | tf_op | source)
XLA Modules:
  0.0 50.7 jit_solution(14291222258316363959)
XLA Ops:
  0.0 0.8 %copy-done.3 = s32[2,32,64]{2,1,0:T(8,128)S(1)} copy-done((s32[2,32,64]{2,1,0:T(8,128)S(1)}, s32[2,32,64]{2,1,0:T(8,128)}, u32[]{:S(2)}) %copy-start.3) | copy-done | bytes 16408
  0.9 0.7 %copy-done.4 = bf16[32,128]{1,0:T(8,128)(2,1)S(1)} copy-done((bf16[32,128]{1,0:T(8,128)(2,1)S(1)}, bf16[32,128]{1,0:T(8,128)(2,1)}, u32[]{:S(2)}) %copy-start.4) | copy-done | bytes 8216
  1.5 0.7 %copy-done.5 = f32[32,2]{0,1:T(2,128)S(1)} copy-done((f32[32,2]{0,1:T(2,128)S(1)}, f32[32,2]{0,1:T(2,128)}, u32[]{:S(2)}) %copy-start.5) | copy-done | bytes 280
  2.2 0.7 %copy-done.7 = f32[1,2]{1,0:T(1,128)S(1)} copy-done((f32[1,2]{1,0:T(1,128)S(1)}, f32[1,2]{1,0:T(1,128)}, u32[]{:S(2)}) %copy-start.7) | copy-done | bytes 32
  2.9 0.2 pack.1
  3.1 6.3 %collective-permute-start = (bf16[112,128]{1,0:T(8,128)(2,1)S(1)}, bf16[112,128]{1,0:T(8,128)(2,1)S(1)}, u32[]{:S(2)}, u32[]{:S(2)}) collective-permute-start(bf16[112,128]{1,0:T(8,128)(2,1)S(1)} %pack.1), channel_id=1, source_target_pairs={{0,0},{1,1},{2,2},{3,3},{4,52},{5,53},{6,54},{7,55},{8,40},{9,41},... | collective-permute-start | bytes 86024 | tf_op jit(solution)/shard_map/ppermute | solution.py:288
  9.4 1.5 %collective-permute-done = bf16[112,128]{1,0:T(8,128)(2,1)S(1)} collective-permute-done((bf16[112,128]{1,0:T(8,128)(2,1)S(1)}, bf16[112,128]{1,0:T(8,128)(2,1)S(1)}, u32[]{:S(2)}, u32[]{:S(2)}) %collective-permute-start) | collective-permute-done | bytes 28704 | tf_op jit(solution)/shard_map/ppermute | solution.py:288
  11.0 0.8 %broadcast_in_dim.2 = bf16[16,112,128]{2,1,0:T(8,128)(2,1)} broadcast(bf16[112,128]{1,0:T(8,128)(2,1)S(1)} %collective-permute-done), dimensions={1,2} | broadcast | bytes 487424 | tf_op jit(solution)/shard_map/broadcast_in_dim | solution.py:291
  11.8 10.0 %all-to-all-start = ((bf16[16,112,128]{2,1,0:T(8,128)(2,1)}), bf16[16,112,128]{2,1,0:T(8,128)(2,1)S(1)}, u32[]{:S(2)}, u32[]{:S(2)}) async-start(bf16[16,112,128]{2,1,0:T(8,128)(2,1)} %broadcast_in_dim.2), calls=%async_computation | async-start | bytes 917504 | tf_op jit(solution)/shard_map/all_to_all | solution.py:290
  21.9 0.0 copy-start.2
  21.9 0.1 pad_add_fusion.place_ref
  22.0 9.3 %all-to-all-done.blocks_ref = bf16[16,112,128]{2,1,0:T(8,128)(2,1)S(1)} async-done(((bf16[16,112,128]{2,1,0:T(8,128)(2,1)}), bf16[16,112,128]{2,1,0:T(8,128)(2,1)S(1)}, u32[]{:S(2)}, u32[]{:S(2)}) %all-to-all-start) | async-done | bytes 458784 | tf_op jit(solution)/shard_map/all_to_all | solution.py:290
  31.2 0.0 copy-done
  31.2 0.0 copy-done.1
  31.2 0.0 copy-done.2
  31.2 10.7 %grid.1 = (f32[32,512]{1,0:T(8,128)S(1)}, f32[32,512]{1,0:T(8,128)S(1)}, f32[32,512]{1,0:T(8,128)S(1)}, f32[32,512]{1,0:T(8,128)S(1)}) custom-call(s32[3]{0:T(128)S(1)} %pad_add_fusion.place_ref, bf16[16,112,128]{2,1,0:T(8,128)(2,1)S(1)} %all-to-all-done.blocks_ref, bf16[512,1024]{1,0:T(8,128)(2,1)S(1)} %copy-done, f32[16,512]{1,0:T(8,128)S(1)} %copy-done.2, ...), custom_call_target="tpu_custom_call" | custom-call | tf_op jit(solution)/shard_map/grid/pallas_call | solution.py:298
  42.0 3.1 %collective-permute-start.1 = (f32[32,512]{1,0:T(8,128)S(1)}, f32[32,512]{1,0:T(8,128)S(1)}, u32[]{:S(2)}, u32[]{:S(2)}) collective-permute-start(f32[32,512]{1,0:T(8,128)S(1)} %get-tuple-element.10), channel_id=1, source_target_pairs={{0,64},{64,128},{128,192},{192,0},{1,65},{65,129},{129,193},{193,1... | collective-permute-start | bytes 196616 | tf_op jit(solution)/shard_map/ppermute | solution.py:321
  45.1 0.7 %collective-permute-start.2 = (f32[32,512]{1,0:T(8,128)S(1)}, f32[32,512]{1,0:T(8,128)S(1)}, u32[]{:S(2)}, u32[]{:S(2)}) collective-permute-start(f32[32,512]{1,0:T(8,128)S(1)} %get-tuple-element.11), channel_id=1, source_target_pairs={{0,128},{64,192},{128,0},{192,64},{1,129},{65,193},{129,1},{193,65... | collective-permute-start | bytes 196616 | tf_op jit(solution)/shard_map/ppermute | solution.py:321
  45.8 0.0 collective-permute-start.3
  45.8 0.6 %collective-permute-done.1.p1 = f32[32,512]{1,0:T(8,128)S(1)} collective-permute-done((f32[32,512]{1,0:T(8,128)S(1)}, f32[32,512]{1,0:T(8,128)S(1)}, u32[]{:S(2)}, u32[]{:S(2)}) %collective-permute-start.1) | collective-permute-done | bytes 65568 | tf_op jit(solution)/shard_map/ppermute | solution.py:321
  46.4 2.7 %collective-permute-done.2.p2 = f32[32,512]{1,0:T(8,128)S(1)} collective-permute-done((f32[32,512]{1,0:T(8,128)S(1)}, f32[32,512]{1,0:T(8,128)S(1)}, u32[]{:S(2)}, u32[]{:S(2)}) %collective-permute-start.2) | collective-permute-done | bytes 65568 | tf_op jit(solution)/shard_map/ppermute | solution.py:321
  49.1 0.5 collective-permute-done.3.p3
  49.5 0.0 copy-done.6
  49.5 1.2 %blend.1 = f32[3,1,4096]{2,1,0:T(1,128)} custom-call(s32[3]{0:T(128)S(1)} %pad_add_fusion.place_ref, f32[32,512]{1,0:T(8,128)S(1)} %get-tuple-element.9.p0, f32[32,512]{1,0:T(8,128)S(1)} %collective-permute-done.1.p1, f32[32,512]{1,0:T(8,128)S(1)} %collective-permute-done.2.p2, f32[32,512]{1,0:T(8,128)S(1)} %collective-permute-done.3.p3, ...), custom_call_target="tpu_custom_call" | custom-call | tf_op jit(solution)/shard_map/blend/pallas_call | solution.py:322
  (7 shorter events, 0.0 us)
Async XLA Ops:
  0.0 31.2 %copy-start = (bf16[512,1024]{1,0:T(8,128)(2,1)S(1)}, bf16[512,1024]{1,0:T(8,128)(2,1)}, u32[]{:S(2)}) copy-start(bf16[512,1024]{1,0:T(8,128)(2,1)} %constant.31.clone.first_ref) | copy-start | bytes 3145732
  0.0 0.8 %copy-start.3 = (s32[2,32,64]{2,1,0:T(8,128)S(1)}, s32[2,32,64]{2,1,0:T(8,128)}, u32[]{:S(2)}) copy-start(s32[2,32,64]{2,1,0:T(8,128)} %cells_ref.1) | copy-start | bytes 49156
  0.8 0.7 %copy-start.4 = (bf16[32,128]{1,0:T(8,128)(2,1)S(1)}, bf16[32,128]{1,0:T(8,128)(2,1)}, u32[]{:S(2)}) copy-start(bf16[32,128]{1,0:T(8,128)(2,1)} %vis_ref.1) | copy-start | bytes 24580
  1.5 0.7 %copy-start.5 = (f32[32,2]{0,1:T(2,128)S(1)}, f32[32,2]{0,1:T(2,128)}, u32[]{:S(2)}) copy-start(f32[32,2]{0,1:T(2,128)} %param.9) | copy-start | bytes 772
  2.2 0.7 %copy-start.7 = (f32[1,2]{1,0:T(1,128)S(1)}, f32[1,2]{1,0:T(1,128)}, u32[]{:S(2)}) copy-start(f32[1,2]{1,0:T(1,128)} %centre_ref.1) | copy-start | bytes 28
  3.1 7.8 %collective-permute-start = (bf16[112,128]{1,0:T(8,128)(2,1)S(1)}, bf16[112,128]{1,0:T(8,128)(2,1)S(1)}, u32[]{:S(2)}, u32[]{:S(2)}) collective-permute-start(bf16[112,128]{1,0:T(8,128)(2,1)S(1)} %pack.1), channel_id=1, source_target_pairs={{0,0},{1,1},{2,2},{3,3},{4,52},{5,53},{6,54},{7,55},{8,40},{9,41},... | collective-permute-start | bytes 86024 | tf_op jit(solution)/shard_map/ppermute | solution.py:288
  11.8 19.4 %copy-start.1 = (f32[96,192]{1,0:T(8,128)S(1)}, f32[96,192]{1,0:T(8,128)}, u32[]{:S(2)}) copy-start(f32[96,192]{1,0:T(8,128)} %constant.33.clone.second_ref) | copy-start | bytes 221188
  11.8 19.4 %all-to-all-start = ((bf16[16,112,128]{2,1,0:T(8,128)(2,1)}), bf16[16,112,128]{2,1,0:T(8,128)(2,1)S(1)}, u32[]{:S(2)}, u32[]{:S(2)}) async-start(bf16[16,112,128]{2,1,0:T(8,128)(2,1)} %broadcast_in_dim.2), calls=%async_computation | async-start | bytes 917504 | tf_op jit(solution)/shard_map/all_to_all | solution.py:290
  21.9 9.4 %copy-start.2 = (f32[16,512]{1,0:T(8,128)S(1)}, f32[16,512]{1,0:T(8,128)}, u32[]{:S(2)}) copy-start(f32[16,512]{1,0:T(8,128)} %constant.32.clone.twiddle_ref) | copy-start | bytes 98308
  42.0 4.4 %collective-permute-start.1 = (f32[32,512]{1,0:T(8,128)S(1)}, f32[32,512]{1,0:T(8,128)S(1)}, u32[]{:S(2)}, u32[]{:S(2)}) collective-permute-start(f32[32,512]{1,0:T(8,128)S(1)} %get-tuple-element.10), channel_id=1, source_target_pairs={{0,64},{64,128},{128,192},{192,0},{1,65},{65,129},{129,193},{193,1... | collective-permute-start | bytes 196616 | tf_op jit(solution)/shard_map/ppermute | solution.py:321
  45.1 4.0 %collective-permute-start.2 = (f32[32,512]{1,0:T(8,128)S(1)}, f32[32,512]{1,0:T(8,128)S(1)}, u32[]{:S(2)}, u32[]{:S(2)}) collective-permute-start(f32[32,512]{1,0:T(8,128)S(1)} %get-tuple-element.11), channel_id=1, source_target_pairs={{0,128},{64,192},{128,0},{192,64},{1,129},{65,193},{129,1},{193,65... | collective-permute-start | bytes 196616 | tf_op jit(solution)/shard_map/ppermute | solution.py:321
  45.8 3.8 %copy-start.6 = (s32[1,1,256]{2,1,0:T(1,128)S(1)}, s32[1,1,256]{2,1,0:T(1,128)}, u32[]{:S(2)}) copy-start(s32[1,1,256]{2,1,0:T(1,128)} %mask_ref.1) | copy-start | bytes 3076
  45.8 3.8 %collective-permute-start.3 = (f32[32,512]{1,0:T(8,128)S(1)}, f32[32,512]{1,0:T(8,128)S(1)}, u32[]{:S(2)}, u32[]{:S(2)}) collective-permute-start(f32[32,512]{1,0:T(8,128)S(1)} %get-tuple-element.12), channel_id=1, source_target_pairs={{0,192},{64,0},{128,64},{192,128},{1,193},{65,1},{129,65},{193,129... | collective-permute-start | bytes 196616 | tf_op jit(solution)/shard_map/ppermute | solution.py:321

commit v3 on v2

--- a/solution.py
+++ b/solution.py
@@ -20,7 +20,8 @@
 BLOCKS = SIDE * SIDE
 ROWS = VIS_ROWS // IMG_ROWS
 HALF = ROWS // 2
-SECT = 7
+PACKED = 4 * HALF + 8
+BEHIND = (0, -1, 1, 2)
 FINE = 8
 COARSE = GRID // 2 // FINE
 XB = GRID // FINE
@@ -69,7 +70,31 @@
     return cosine, sine * frac
 
 
-def pack_kernel(vis_ref, uv_ref, cells_ref, centre_ref, out_ref):
+def coded(cell):
+    size = ((cell & 127) + 128) << ((cell >> 7) & 15)
+    value = size.astype(jnp.float32)
+    return jnp.where(cell >= GRID // 2, -value, value).astype(jnp.bfloat16)
+
+
+def decoded(value):
+    size = jnp.abs(value)
+    high = jnp.where(value < 0.0, float(GRID // 2) - 128.0, -128.0)
+    for step in (8, 4, 2, 1):
+        over = size >= 128.0 * 2**step
+        size = jnp.where(over, size * 2.0**-step, size)
+        high = jnp.where(over, high + 128.0 * step, high)
+    return size + high
+
+
+def pack_kernel(
+    vis_hbm, uv_hbm, cells_hbm, centre_hbm, out_ref, vis_ref, uv_ref, cells_ref, centre_ref, sems
+):
+    pairs = ((vis_hbm, vis_ref), (uv_hbm, uv_ref), (cells_hbm, cells_ref), (centre_hbm, centre_ref))
+    copies = [pltpu.make_async_copy(a, b, sems.at[i]) for i, (a, b) in enumerate(pairs)]
+    for copy in copies:
+        copy.start()
+    for copy in copies:
+        copy.wait()
     lane = lax.broadcasted_iota(jnp.int32, (HALF, 2 * CH), 1)
     left = lane < CH
     vis = vis_ref[...].astype(jnp.float32)
@@ -79,9 +104,7 @@
     for which in range(2):
         cells = cells_ref[which]
         both = jnp.concatenate([cells[:HALF], cells[HALF:]], 1)
-        at = 32 + 32 * which
-        out_ref[at : at + 16] = (both >> 6).astype(jnp.float32).astype(jnp.bfloat16)
-        out_ref[at + 16 : at + 32] = (both & 63).astype(jnp.float32).astype(jnp.bfloat16)
+        out_ref[32 + 16 * which : 48 + 16 * which] = coded(both)
 
     def pieces(value):
         high = value.astype(jnp.bfloat16).astype(jnp.float32)
@@ -96,19 +119,22 @@
         split, spots.astype(jnp.float32).astype(jnp.bfloat16), (((0,), (0,)), ((), ())),
         preferred_element_type=jnp.float32,
     )
+    whole = columns[0:8]
+    for i in (1, 2, 3):
+        whole = whole + pltpu.roll(columns[8 * i : 8 * i + 8], 32 * i, 1)
+    lane = lane[0:8]
     cen = jnp.where(lane % 2 == 0, centre_ref[0:1, 0:1], centre_ref[0:1, 1:2])
-    whole = columns[:HALF] + pltpu.roll(columns[HALF:], CH, 1)
     for i, piece in enumerate(pieces(cen)):
         whole = jnp.where(lane // 2 == 3 + i, piece, whole)
-    out_ref[96:112] = whole.astype(jnp.bfloat16)
+    out_ref[64:72] = whole.astype(jnp.bfloat16)
 
 
 def grid_kernel(
-    place_ref, blocks_ref, first_ref, twiddle_ref, second_ref, o0, o1, o2, o3,
+    place_ref, blocks_ref, own_ref, pair_ref, first_ref, twiddle_ref, second_ref, o0, o1, o2, o3,
     terms0, terms1, cells0, cells1, left0, left1, right0, right1, total_ref, image_ref,
     iota_ref,
 ):
-    own, zpos, row = place_ref[0], place_ref[1], place_ref[2]
+    own, row = place_ref[0], place_ref[1]
     lane = lax.broadcasted_iota(jnp.int32, (HALF, 2 * CH), 1)
     chan = (lane % CH).astype(jnp.float32)
     nu = (2.0 * chan + 1.0 - CH) / CH
@@ -125,21 +151,29 @@
         return section + pltpu.roll(section, 2 * CH - 2, 1) + pltpu.roll(section, 2 * CH - 4, 1)
 
     cens = []
-    for q in range(SIDE):
-        sect = joined(blocks_ref[q * SIDE, 96:112].astype(jnp.float32))
+    for y in range(2):
+        sect = joined(blocks_ref[y * SIDE, 64:72].astype(jnp.float32))
         cens.append((sect[0:1, 6:7], sect[0:1, 7:8]))
+    for ref in (own_ref, pair_ref):
+        cens.append((ref[0:1, 0:1], ref[0:1, 1:2]))
 
     def elements(block, terms_ref, cell_ref):
         def section(at):
             return blocks_ref[block, 16 * at : 16 * at + 16].astype(jnp.float32)
 
         real, imag = section(0), section(1)
-        gr = section(2) * 64.0 + section(3)
-        gc = section(4) * 64.0 + section(5)
-        place = joined(section(6))
-        is_left = lane < CH
-        u = jnp.where(is_left, place[:, 0:1], place[:, CH : CH + 1])
-        v = jnp.where(is_left, place[:, 1:2], place[:, CH + 1 : CH + 2])
+        gr, gc = decoded(section(2)), decoded(section(3))
+        place = joined(blocks_ref[block, 64:72].astype(jnp.float32))
+        is_left = lane[0:8] < CH
+
+        def column(at):
+            both = [
+                jnp.where(is_left, place[:, i : i + 1], place[:, CH + i : CH + i + 1])
+                for i in (at, at + 32)
+            ]
+            return jnp.concatenate(both, 0)
+
+        u, v = column(0), column(1)
         mid = (gc == float(GRID // 2)).astype(jnp.float32)
         folded = jnp.where(gc > GRID // 2, GRID - gc, gc * (1.0 - mid))
         sign = jnp.where(gc > GRID // 2, -1.0, jnp.where(folded == 0.0, 0.0, 1.0))
@@ -229,10 +263,10 @@
     )
     size = TERMS * FINE
     for s, out in enumerate((o0, o1, o2, o3)):
-        facet = lax.rem(own + s, FACETS)
-        spot = lax.rem(facet - zpos + FACETS, FACETS)
-        before = lax.rem(facet - zpos + 2 * FACETS - 1, FACETS)
-        out[0:size] = image_ref[pl.ds(pl.multiple_of(spot * size, 8), size), :]
+        spot = (2, 3, 1, 0)[s]
+        before = ((own ^ s) + FACETS - 1) % FACETS ^ own
+        before = jnp.where(before < 2, before + 2, 3 - before)
+        out[0:size] = image_ref[spot * size : (spot + 1) * size]
         prior = image_ref[pl.ds(pl.multiple_of(before * size, 8), size), :]
         for term in range(TERMS):
             at = term * FINE + FINE - 1
@@ -266,26 +300,33 @@
         for z in range(SIDE):
             for y in range(SIDE):
                 for x in range(SIDE):
-                    source = facet * IMG_ROWS + z * BLOCKS + y * SIDE + x
-                    target = z * IMG_ROWS + ((facet - y) % FACETS) * BLOCKS + y * SIDE + x
-                    pairs.append((source, target))
+                    here = y * SIDE + x
+                    plane = (z + BEHIND[facet]) % SIDE
+                    source = ((3 - facet) ^ (y & 1)) * IMG_ROWS + plane * BLOCKS + here
+                    pairs.append((source, facet * IMG_ROWS + z * BLOCKS + here))
     return pairs
 
 
 def per_device(visibilities, uv_coords, cells, centres, intersection_mask):
     vmem = pl.BlockSpec(memory_space=pltpu.VMEM)
     smem = pl.BlockSpec(memory_space=pltpu.SMEM)
+    hbm = pl.BlockSpec(memory_space=pltpu.HBM)
     facet, spot = lax.axis_index("facet"), lax.axis_index("vis")
-    place = jnp.stack([facet, spot // BLOCKS, spot]).astype(jnp.int32)
+    place = jnp.stack([facet, spot]).astype(jnp.int32)
+    given = (visibilities, uv_coords.T, cells, centres)
     packed = pl.pallas_call(
         pack_kernel,
-        out_shape=jax.ShapeDtypeStruct((16 * SECT, 2 * CH), jnp.bfloat16),
-        in_specs=[vmem] * 4,
+        out_shape=jax.ShapeDtypeStruct((PACKED, 2 * CH), jnp.bfloat16),
+        in_specs=[hbm] * 4,
         out_specs=vmem,
-        compiler_params=pltpu.CompilerParams(vmem_limit_bytes=2 << 20),
+        scratch_shapes=[pltpu.VMEM(one.shape, one.dtype) for one in given]
+        + [pltpu.SemaphoreType.DMA((4,))],
+        compiler_params=pltpu.CompilerParams(vmem_limit_bytes=63 << 20),
         name="pack",
-    )(visibilities, uv_coords.T, cells, centres)
+    )(*given)
     packed = lax.ppermute(packed, ("facet", "vis"), swap_pairs())
+    packed, centre = lax.optimization_barrier((packed, centres))
+    pair = lax.ppermute(centre, "facet", [(i, i ^ 1) for i in range(FACETS)])
     planes = [[z * BLOCKS + i for i in range(BLOCKS)] for z in range(SIDE)]
     blocks = lax.all_to_all(
         jnp.broadcast_to(packed[None], (BLOCKS,) + packed.shape),
@@ -298,7 +339,7 @@
     parts = pl.pallas_call(
         grid_kernel,
         out_shape=[chunk] * FACETS,
-        in_specs=[smem] + [vmem] * 4,
+        in_specs=[smem] + [vmem] * 6,
         out_specs=[vmem] * FACETS,
         scratch_shapes=[
             pltpu.VMEM((2 * VALS, HALF, 2 * CH), jnp.float32),
@@ -315,10 +356,10 @@
         ],
         compiler_params=pltpu.CompilerParams(vmem_limit_bytes=40 << 20),
         name="grid",
-    )(place, blocks, first, twiddle, second)
+    )(place, blocks, centres, pair, first, twiddle, second)
     got = [parts[0]]
     for s in range(1, FACETS):
-        got.append(lax.ppermute(parts[s], "facet", [(i, (i + s) % FACETS) for i in range(FACETS)]))
+        got.append(lax.ppermute(parts[s], "facet", [(i, i ^ s) for i in range(FACETS)]))
     return pl.pallas_call(
         blend_kernel,
         out_shape=jax.ShapeDtypeStruct((TERMS, 1, GRID), jnp.float32),

time: 51 us -> 47 us (0.922)
  waiting for transfers between devices: 14.6 us -> 11.4 us
  Pallas kernels: 12.2 us -> 13.8 us
  starting transfers between devices: 20.1 us -> 18.9 us
  local copies, waits for them, and re-layouts: 3.72 us -> 2.57 us
    all_to_all x1, waiting for transfers between devices: 9.28 us -> 5.39 us  [per_device(): lax.all_to_all(jnp.broadcast_to(packed[None], (BLOCKS,) + packed.shape),...]
    all_to_all x1, starting transfers between devices: 10 us -> 6.89 us  [per_device(): lax.all_to_all(jnp.broadcast_to(packed[None], (BLOCKS,) + packed.shape),...]
    pallas_call x1, Pallas kernels: 0.24 us -> 1.69 us  [per_device(): pl.pallas_call(pack_kernel, out_shape=jax.ShapeDtypeStruct((PACKED, 2 * C...]
    ppermute x3 -> x4, starting transfers between devices: 3.79 us -> 4.93 us  [the longest x3 3.91 us: per_device(): lax.ppermute(parts[s], 'facet', [(i, i ^ s) for i in range(FACETS)])]
    unnamed x16 -> x10, local copies, waits for them, and re-layouts: 2.89 us -> 1.81 us
    ppermute x1, starting transfers between devices: 6.29 us -> 7.04 us  [per_device(): packed = lax.ppermute(packed, ('facet', 'vis'), swap_pairs())]
    ppermute x3 -> x4, waiting for transfers between devices: 3.75 us -> 4.33 us  [the longest x3 3.51 us: per_device(): lax.ppermute(parts[s], 'facet', [(i, i ^ s) for i in range(FACETS)])]
  transfers between devices with their start and end apart: 5 -> 6, of which waited for: 5 -> 5; matrix products, arithmetic and copies ran while one was open for 0% -> 0% of each run, Pallas kernels for 0% -> 0%
where the time goes in v3:
time: 47 us; the launch traced here: 46.7 us
  starting transfers between devices  18.9 us (40%)
  Pallas kernels  13.8 us (29%)
  waiting for transfers between devices  11.4 us (24%)
  local copies, waits for them, and re-layouts  2.57 us (5%)
    pallas_call x1, Pallas kernels, per_device(): pl.pallas_call(grid_kernel, out_shape=[chunk] * FACETS, in_specs=[smem] +...  10.9 us
    ppermute x1, starting transfers between devices, per_device(): packed = lax.ppermute(packed, ('facet', 'vis'), swap_pairs())  7.04 us
    all_to_all x1, starting transfers between devices, per_device(): lax.all_to_all(jnp.broadcast_to(packed[None], (BLOCKS,) + packed.shape),...  6.89 us
    all_to_all x1, waiting for transfers between devices, per_device(): lax.all_to_all(jnp.broadcast_to(packed[None], (BLOCKS,) + packed.shape),...  5.39 us
    ppermute x3, starting transfers between devices, per_device(): lax.ppermute(parts[s], 'facet', [(i, i ^ s) for i in range(FACETS)])  3.91 us
    ppermute x3, waiting for transfers between devices, per_device(): lax.ppermute(parts[s], 'facet', [(i, i ^ s) for i in range(FACETS)])  3.51 us
    unnamed x10, local copies, waits for them, and re-layouts  1.81 us
    pallas_call x1, Pallas kernels, per_device(): pl.pallas_call(pack_kernel, out_shape=jax.ShapeDtypeStruct((PACKED, 2 * C...  1.69 us
  transfers between devices with their start and end apart: 6, of which 5 were waited for; matrix products, arithmetic and copies ran while one was open for 0% of the time, Pallas kernels for 0%

profile of v3, /device:TPU:1, one launch (start us, length us, event | category | flops | bytes accessed | tf_op | source)
XLA Modules:
  0.0 46.7 jit_solution(7754307981508811814)
XLA Ops:
  0.0 1.7 %pack.1 = bf16[72,128]{1,0:T(8,128)(2,1)} custom-call(bf16[32,128]{1,0:T(8,128)(2,1)} %vis_hbm.1, f32[2,32]{1,0:T(2,128)} %bitcast.3, s32[2,32,64]{2,1,0:T(8,128)} %cells_hbm.1, f32[1,2]{1,0:T(1,128)} %own_ref.1), custom_call_target="tpu_custom_call" | custom-call | tf_op jit(solution)/shard_map/pack/pallas_call | solution.py:317
  1.7 7.0 %collective-permute-start = (bf16[72,128]{1,0:T(8,128)(2,1)}, bf16[72,128]{1,0:T(8,128)(2,1)S(1)}, u32[]{:S(2)}, u32[]{:S(2)}) collective-permute-start(bf16[72,128]{1,0:T(8,128)(2,1)} %pack.1), channel_id=1, source_target_pairs={{192,0},{193,1},{194,2},{195,3},{132,4},{133,5},{134,6},{135,7},{2... | collective-permute-start | bytes 55304 | tf_op jit(solution)/shard_map/ppermute | solution.py:327
  8.7 1.7 %collective-permute-done = bf16[72,128]{1,0:T(8,128)(2,1)S(1)} collective-permute-done((bf16[72,128]{1,0:T(8,128)(2,1)}, bf16[72,128]{1,0:T(8,128)(2,1)S(1)}, u32[]{:S(2)}, u32[]{:S(2)}) %collective-permute-start) | collective-permute-done | bytes 18464 | tf_op jit(solution)/shard_map/ppermute | solution.py:327
  10.4 0.8 %broadcast_in_dim.2 = bf16[16,72,128]{2,1,0:T(8,128)(2,1)} broadcast(bf16[72,128]{1,0:T(8,128)(2,1)S(1)} %collective-permute-done), dimensions={1,2} | broadcast | bytes 313344 | tf_op jit(solution)/shard_map/broadcast_in_dim | solution.py:332
  11.2 0.0 copy-start.1
  11.2 6.9 %all-to-all-start = ((bf16[16,72,128]{2,1,0:T(8,128)(2,1)}), bf16[16,72,128]{2,1,0:T(8,128)(2,1)S(1)}, u32[]{:S(2)}, u32[]{:S(2)}) async-start(bf16[16,72,128]{2,1,0:T(8,128)(2,1)} %broadcast_in_dim.2), calls=%async_computation | async-start | bytes 589824 | tf_op jit(solution)/shard_map/all_to_all | solution.py:331
  18.1 0.0 copy-start.3
  18.1 0.1 pad_add_fusion.place_ref
  18.1 0.6 %copy-done.3 = f32[1,2]{1,0:T(1,128)S(1)} copy-done((f32[1,2]{1,0:T(1,128)S(1)}, f32[1,2]{1,0:T(1,128)}, u32[]{:S(2)}) %copy-start.3) | copy-done | bytes 32
  18.7 1.0 %collective-permute-start.1 = (f32[1,2]{1,0:T(1,128)S(1)}, f32[1,2]{1,0:T(1,128)S(1)}, u32[]{:S(2)}, u32[]{:S(2)}) collective-permute-start(f32[1,2]{1,0:T(1,128)S(1)} %copy-done.3), channel_id=1, source_target_pairs={{0,64},{64,0},{128,192},{192,128},{1,65},{65,1},{129,193},{193,129... | collective-permute-start | bytes 32 | tf_op jit(solution)/shard_map/ppermute | solution.py:329
  19.7 0.8 %collective-permute-done.1.pair_ref = f32[1,2]{1,0:T(1,128)S(1)} collective-permute-done((f32[1,2]{1,0:T(1,128)S(1)}, f32[1,2]{1,0:T(1,128)S(1)}, u32[]{:S(2)}, u32[]{:S(2)}) %collective-permute-start.1) | collective-permute-done | bytes 40 | tf_op jit(solution)/shard_map/ppermute | solution.py:329
  20.6 5.4 %all-to-all-done.blocks_ref = bf16[16,72,128]{2,1,0:T(8,128)(2,1)S(1)} async-done(((bf16[16,72,128]{2,1,0:T(8,128)(2,1)}), bf16[16,72,128]{2,1,0:T(8,128)(2,1)S(1)}, u32[]{:S(2)}, u32[]{:S(2)}) %all-to-all-start) | async-done | bytes 294944 | tf_op jit(solution)/shard_map/all_to_all | solution.py:331
  25.9 0.0 copy-done.1
  25.9 0.0 copy-done.2
  26.0 1.2 %copy-done = bf16[512,1024]{1,0:T(8,128)(2,1)S(1)} copy-done((bf16[512,1024]{1,0:T(8,128)(2,1)S(1)}, bf16[512,1024]{1,0:T(8,128)(2,1)}, u32[]{:S(2)}) %copy-start) | copy-done | bytes 1048600
  27.2 10.9 %grid.1 = (f32[32,512]{1,0:T(8,128)S(1)}, f32[32,512]{1,0:T(8,128)S(1)}, f32[32,512]{1,0:T(8,128)S(1)}, f32[32,512]{1,0:T(8,128)S(1)}) custom-call(s32[2]{0:T(128)S(1)} %pad_add_fusion.place_ref, bf16[16,72,128]{2,1,0:T(8,128)(2,1)S(1)} %all-to-all-done.blocks_ref, f32[1,2]{1,0:T(1,128)S(1)} %copy-done.3, f32[1,2]{1,0:T(1,128)S(1)} %collective-permute-done.1.pair_ref, ...), custom_call_target="tpu_custom_call" | custom-call | tf_op jit(solution)/shard_map/grid/pallas_call | solution.py:339
  38.1 2.2 %collective-permute-start.2 = (f32[32,512]{1,0:T(8,128)S(1)}, f32[32,512]{1,0:T(8,128)S(1)}, u32[]{:S(2)}, u32[]{:S(2)}) collective-permute-start(f32[32,512]{1,0:T(8,128)S(1)} %get-tuple-element.14), channel_id=1, source_target_pairs={{0,64},{64,0},{128,192},{192,128},{1,65},{65,1},{129,193},{193,129... | collective-permute-start | bytes 196616 | tf_op jit(solution)/shard_map/ppermute | solution.py:362
  40.3 0.0 collective-permute-start.3
  40.3 1.7 %collective-permute-start.4 = (f32[32,512]{1,0:T(8,128)S(1)}, f32[32,512]{1,0:T(8,128)S(1)}, u32[]{:S(2)}, u32[]{:S(2)}) collective-permute-start(f32[32,512]{1,0:T(8,128)S(1)} %get-tuple-element.16), channel_id=1, source_target_pairs={{0,192},{64,128},{128,64},{192,0},{1,193},{65,129},{129,65},{193,1... | collective-permute-start | bytes 196616 | tf_op jit(solution)/shard_map/ppermute | solution.py:362
  42.0 0.0 collective-permute-done.2.p1
  42.0 1.9 %collective-permute-done.3.p2 = f32[32,512]{1,0:T(8,128)S(1)} collective-permute-done((f32[32,512]{1,0:T(8,128)S(1)}, f32[32,512]{1,0:T(8,128)S(1)}, u32[]{:S(2)}, u32[]{:S(2)}) %collective-permute-start.3) | collective-permute-done | bytes 65568 | tf_op jit(solution)/shard_map/ppermute | solution.py:362
  43.9 1.6 %collective-permute-done.4.p3 = f32[32,512]{1,0:T(8,128)S(1)} collective-permute-done((f32[32,512]{1,0:T(8,128)S(1)}, f32[32,512]{1,0:T(8,128)S(1)}, u32[]{:S(2)}, u32[]{:S(2)}) %collective-permute-start.4) | collective-permute-done | bytes 65568 | tf_op jit(solution)/shard_map/ppermute | solution.py:362
  45.5 0.0 copy-done.4
  45.5 1.2 %blend.1 = f32[3,1,4096]{2,1,0:T(1,128)} custom-call(s32[2]{0:T(128)S(1)} %pad_add_fusion.place_ref, f32[32,512]{1,0:T(8,128)S(1)} %get-tuple-element.13.p0, f32[32,512]{1,0:T(8,128)S(1)} %collective-permute-done.2.p1, f32[32,512]{1,0:T(8,128)S(1)} %collective-permute-done.3.p2, f32[32,512]{1,0:T(8,128)S(1)} %collective-permute-done.4.p3, ...), custom_call_target="tpu_custom_call" | custom-call | tf_op jit(solution)/shard_map/blend/pallas_call | solution.py:363
  (3 shorter events, 0.0 us)
Async XLA Ops:
  1.7 8.7 %collective-permute-start = (bf16[72,128]{1,0:T(8,128)(2,1)}, bf16[72,128]{1,0:T(8,128)(2,1)S(1)}, u32[]{:S(2)}, u32[]{:S(2)}) collective-permute-start(bf16[72,128]{1,0:T(8,128)(2,1)} %pack.1), channel_id=1, source_target_pairs={{192,0},{193,1},{194,2},{195,3},{132,4},{133,5},{134,6},{135,7},{2... | collective-permute-start | bytes 55304 | tf_op jit(solution)/shard_map/ppermute | solution.py:327
  11.2 14.8 %copy-start.1 = (f32[96,192]{1,0:T(8,128)S(1)}, f32[96,192]{1,0:T(8,128)}, u32[]{:S(2)}) copy-start(f32[96,192]{1,0:T(8,128)} %constant.17.clone.second_ref) | copy-start | bytes 221188
  11.2 14.8 %copy-start.2 = (f32[16,512]{1,0:T(8,128)S(1)}, f32[16,512]{1,0:T(8,128)}, u32[]{:S(2)}) copy-start(f32[16,512]{1,0:T(8,128)} %constant.16.clone.twiddle_ref) | copy-start | bytes 98308
  11.2 14.8 %all-to-all-start = ((bf16[16,72,128]{2,1,0:T(8,128)(2,1)}), bf16[16,72,128]{2,1,0:T(8,128)(2,1)S(1)}, u32[]{:S(2)}, u32[]{:S(2)}) async-start(bf16[16,72,128]{2,1,0:T(8,128)(2,1)} %broadcast_in_dim.2), calls=%async_computation | async-start | bytes 589824 | tf_op jit(solution)/shard_map/all_to_all | solution.py:331
  18.1 0.7 %copy-start.3 = (f32[1,2]{1,0:T(1,128)S(1)}, f32[1,2]{1,0:T(1,128)}, u32[]{:S(2)}) copy-start(f32[1,2]{1,0:T(1,128)} %own_ref.1) | copy-start | bytes 28
  18.7 1.8 %collective-permute-start.1 = (f32[1,2]{1,0:T(1,128)S(1)}, f32[1,2]{1,0:T(1,128)S(1)}, u32[]{:S(2)}, u32[]{:S(2)}) collective-permute-start(f32[1,2]{1,0:T(1,128)S(1)} %copy-done.3), channel_id=1, source_target_pairs={{0,64},{64,0},{128,192},{192,128},{1,65},{65,1},{129,193},{193,129... | collective-permute-start | bytes 32 | tf_op jit(solution)/shard_map/ppermute | solution.py:329
  26.0 1.2 %copy-start = (bf16[512,1024]{1,0:T(8,128)(2,1)S(1)}, bf16[512,1024]{1,0:T(8,128)(2,1)}, u32[]{:S(2)}) copy-start(bf16[512,1024]{1,0:T(8,128)(2,1)} %constant.15.clone.first_ref) | copy-start | bytes 3145732
  38.1 3.9 %collective-permute-start.2 = (f32[32,512]{1,0:T(8,128)S(1)}, f32[32,512]{1,0:T(8,128)S(1)}, u32[]{:S(2)}, u32[]{:S(2)}) collective-permute-start(f32[32,512]{1,0:T(8,128)S(1)} %get-tuple-element.14), channel_id=1, source_target_pairs={{0,64},{64,0},{128,192},{192,128},{1,65},{65,1},{129,193},{193,129... | collective-permute-start | bytes 196616 | tf_op jit(solution)/shard_map/ppermute | solution.py:362
  40.3 3.7 %collective-permute-start.3 = (f32[32,512]{1,0:T(8,128)S(1)}, f32[32,512]{1,0:T(8,128)S(1)}, u32[]{:S(2)}, u32[]{:S(2)}) collective-permute-start(f32[32,512]{1,0:T(8,128)S(1)} %get-tuple-element.15), channel_id=1, source_target_pairs={{0,128},{64,192},{128,0},{192,64},{1,129},{65,193},{129,1},{193,65... | collective-permute-start | bytes 196616 | tf_op jit(solution)/shard_map/ppermute | solution.py:362
  40.3 5.2 %copy-start.4 = (s32[1,1,256]{2,1,0:T(1,128)S(1)}, s32[1,1,256]{2,1,0:T(1,128)}, u32[]{:S(2)}) copy-start(s32[1,1,256]{2,1,0:T(1,128)} %mask_ref.1) | copy-start | bytes 3076
  40.3 5.2 %collective-permute-start.4 = (f32[32,512]{1,0:T(8,128)S(1)}, f32[32,512]{1,0:T(8,128)S(1)}, u32[]{:S(2)}, u32[]{:S(2)}) collective-permute-start(f32[32,512]{1,0:T(8,128)S(1)} %get-tuple-element.16), channel_id=1, source_target_pairs={{0,192},{64,128},{128,64},{192,0},{1,193},{65,129},{129,65},{193,1... | collective-permute-start | bytes 196616 | tf_op jit(solution)/shard_map/ppermute | solution.py:362

commit v4 on v3

--- a/solution.py
+++ b/solution.py
@@ -129,11 +129,18 @@
     out_ref[64:72] = whole.astype(jnp.bfloat16)
 
 
+def spread_kernel(block_ref, out_ref):
+    for i in range(BLOCKS):
+        out_ref[i] = block_ref[...]
+
+
 def grid_kernel(
-    place_ref, blocks_ref, own_ref, pair_ref, first_ref, twiddle_ref, second_ref, o0, o1, o2, o3,
+    place_ref, blocks_ref, own_ref, pair_ref, first_hbm, twiddle_ref, second_ref, o0, o1, o2, o3,
     terms0, terms1, cells0, cells1, left0, left1, right0, right1, total_ref, image_ref,
-    iota_ref,
+    iota_ref, first_ref, sem,
 ):
+    table = pltpu.make_async_copy(first_hbm, first_ref, sem)
+    table.start()
     own, row = place_ref[0], place_ref[1]
     lane = lax.broadcasted_iota(jnp.int32, (HALF, 2 * CH), 1)
     chan = (lane % CH).astype(jnp.float32)
@@ -246,6 +253,7 @@
     span = VALS * FINE
     flat = total_ref[...].T
     total = jnp.concatenate([flat[0:span], flat[span : 2 * span]], 1)
+    table.wait()
     mixed = jnp.dot(total.astype(jnp.bfloat16), first_ref[...], preferred_element_type=jnp.float32)
     ur = mixed[:, :XB].reshape(VALS, FINE, XB)
     ui = mixed[:, XB:].reshape(VALS, FINE, XB)
@@ -266,18 +274,19 @@
         spot = (2, 3, 1, 0)[s]
         before = ((own ^ s) + FACETS - 1) % FACETS ^ own
         before = jnp.where(before < 2, before + 2, 3 - before)
-        out[0:size] = image_ref[spot * size : (spot + 1) * size]
+        out[0:size] = image_ref[spot * size : (spot + 1) * size].astype(out.dtype)
         prior = image_ref[pl.ds(pl.multiple_of(before * size, 8), size), :]
-        for term in range(TERMS):
-            at = term * FINE + FINE - 1
-            out[size + term : size + term + 1, 0:OVER] = prior[at : at + 1, XB - OVER :]
+        strips = [prior[term * FINE + FINE - 1 : term * FINE + FINE] for term in range(TERMS)]
+        strips = jnp.concatenate(strips + [jnp.zeros((CHUNK - size - TERMS, XB), jnp.float32)], 0)
+        out[size:CHUNK] = strips.astype(out.dtype)
 
 
 def blend_kernel(place_ref, p0, p1, p2, p3, mask_ref, out_ref):
     size = TERMS * FINE
-    image = (p0[0:size] + p1[0:size]) + (p2[0:size] + p3[0:size])
-    tail = slice(size, size + TERMS)
-    strip = (p0[tail, 0:OVER] + p1[tail, 0:OVER]) + (p2[tail, 0:OVER] + p3[tail, 0:OVER])
+    image = p0[...]
+    for part in (p1, p2, p3):
+        image = image + part[...].astype(jnp.float32)
+    strip = image[size : size + TERMS, XB - OVER :]
     has_left = (place_ref[0] > 0).astype(jnp.float32)
     pixel = lax.broadcasted_iota(jnp.int32, (1, OVER), 1).astype(jnp.float32)
     ramp = 1.0 - (pixel + 0.5) / OVER
@@ -314,6 +323,7 @@
     facet, spot = lax.axis_index("facet"), lax.axis_index("vis")
     place = jnp.stack([facet, spot]).astype(jnp.int32)
     given = (visibilities, uv_coords.T, cells, centres)
+    given = [pltpu.with_memory_space_constraint(one, pltpu.HBM) for one in given]
     packed = pl.pallas_call(
         pack_kernel,
         out_shape=jax.ShapeDtypeStruct((PACKED, 2 * CH), jnp.bfloat16),
@@ -321,7 +331,7 @@
         out_specs=vmem,
         scratch_shapes=[pltpu.VMEM(one.shape, one.dtype) for one in given]
         + [pltpu.SemaphoreType.DMA((4,))],
-        compiler_params=pltpu.CompilerParams(vmem_limit_bytes=63 << 20),
+        compiler_params=pltpu.CompilerParams(vmem_limit_bytes=2 << 20),
         name="pack",
     )(*given)
     packed = lax.ppermute(packed, ("facet", "vis"), swap_pairs())
@@ -329,17 +339,28 @@
     pair = lax.ppermute(centre, "facet", [(i, i ^ 1) for i in range(FACETS)])
     planes = [[z * BLOCKS + i for i in range(BLOCKS)] for z in range(SIDE)]
     blocks = lax.all_to_all(
-        jnp.broadcast_to(packed[None], (BLOCKS,) + packed.shape),
+        pl.pallas_call(
+            spread_kernel,
+            out_shape=jax.ShapeDtypeStruct((BLOCKS,) + packed.shape, packed.dtype),
+            in_specs=[vmem],
+            out_specs=vmem,
+            compiler_params=pltpu.CompilerParams(vmem_limit_bytes=2 << 20),
+            name="spread",
+        )(packed),
         "vis", 0, 0, axis_index_groups=planes,
     )
     first, twiddle, second = tables()
-    chunk = jax.ShapeDtypeStruct((CHUNK, XB), jnp.float32)
+    first = pltpu.with_memory_space_constraint(first, pltpu.HBM)
+    chunk = [
+        jax.ShapeDtypeStruct((CHUNK, XB), jnp.bfloat16 if s else jnp.float32)
+        for s in range(FACETS)
+    ]
     span = 2 * VALS * FINE
     wide = ROWS * CH
     parts = pl.pallas_call(
         grid_kernel,
-        out_shape=[chunk] * FACETS,
-        in_specs=[smem] + [vmem] * 6,
+        out_shape=chunk,
+        in_specs=[smem] + [vmem] * 3 + [hbm] + [vmem] * 2,
         out_specs=[vmem] * FACETS,
         scratch_shapes=[
             pltpu.VMEM((2 * VALS, HALF, 2 * CH), jnp.float32),
@@ -353,6 +374,8 @@
             pltpu.VMEM((COARSE, span), jnp.float32),
             pltpu.VMEM((VALS * FINE, XB), jnp.float32),
             pltpu.VMEM((COARSE, 2 * CH), jnp.bfloat16),
+            pltpu.VMEM((2 * COARSE, 2 * XB), jnp.bfloat16),
+            pltpu.SemaphoreType.DMA,
         ],
         compiler_params=pltpu.CompilerParams(vmem_limit_bytes=40 << 20),
         name="grid",

time: 47 us -> 43.6 us (0.928)
  local copies, waits for them, and re-layouts: 2.57 us -> 0.59 us
  waiting for transfers between devices: 11.4 us -> 9.76 us
    ppermute x3, waiting for transfers between devices: 3.51 us -> 2.1 us  [per_device(): lax.ppermute(parts[s], 'facet', [(i, i ^ s) for i in range(FACETS)])]
    unnamed x10 -> x8, local copies, waits for them, and re-layouts: 1.81 us -> 0.59 us
    pallas_call x1 -> x2, Pallas kernels: 10.9 us -> 11.8 us  [the longest x1 11 us: per_device(): pl.pallas_call(grid_kernel, out_shape=chunk, in_specs=[smem] + [vmem] * 3...]
    broadcast_in_dim x1 -> x0, local copies, waits for them, and re-layouts: 0.76 us -> none  [per_device(): jnp.broadcast_to(packed[None], (BLOCKS,) + packed.shape)]
    pallas_call x1, Pallas kernels: 1.69 us -> 1.08 us  [per_device(): pl.pallas_call(pack_kernel, out_shape=jax.ShapeDtypeStruct((PACKED, 2 * C...]
where the time goes in v4:
time: 43.6 us; the launch traced here: 43.4 us
  starting transfers between devices  18.9 us (43%)
  Pallas kernels  14.1 us (32%)
  waiting for transfers between devices  9.76 us (22%)
  local copies, waits for them, and re-layouts  0.59 us (1%)
    pallas_call x1, Pallas kernels, per_device(): pl.pallas_call(grid_kernel, out_shape=chunk, in_specs=[smem] + [vmem] * 3...  11 us
    ppermute x1, starting transfers between devices, per_device(): packed = lax.ppermute(packed, ('facet', 'vis'), swap_pairs())  7.04 us
    all_to_all x1, starting transfers between devices, per_device(): lax.all_to_all(pl.pallas_call(spread_kernel, out_shape=jax.ShapeDtypeStru...  6.89 us
    all_to_all x1, waiting for transfers between devices, per_device(): lax.all_to_all(pl.pallas_call(spread_kernel, out_shape=jax.ShapeDtypeStru...  5.39 us
    ppermute x3, starting transfers between devices, per_device(): lax.ppermute(parts[s], 'facet', [(i, i ^ s) for i in range(FACETS)])  3.91 us
    ppermute x3, waiting for transfers between devices, per_device(): lax.ppermute(parts[s], 'facet', [(i, i ^ s) for i in range(FACETS)])  2.1 us
    ppermute x1, waiting for transfers between devices, per_device(): packed = lax.ppermute(packed, ('facet', 'vis'), swap_pairs())  1.45 us
    pallas_call x1, Pallas kernels, per_device(): pl.pallas_call(blend_kernel, out_shape=jax.ShapeDtypeStruct((TERMS, 1, GR...  1.2 us
  transfers between devices with their start and end apart: 6, of which 5 were waited for; matrix products, arithmetic and copies ran while one was open for 0% of the time, Pallas kernels for 0%

profile of v4, /device:TPU:1, one launch (start us, length us, event | category | flops | bytes accessed | tf_op | source)
XLA Modules:
  0.0 43.4 jit_solution(7003786456385325814)
XLA Ops:
  0.0 1.1 %pack.1 = bf16[72,128]{1,0:T(8,128)(2,1)S(1)} custom-call(bf16[32,128]{1,0:T(8,128)(2,1)} %vis_hbm.1, f32[2,32]{1,0:T(2,128)} %bitcast.3, s32[2,32,64]{2,1,0:T(8,128)} %cells_hbm.1, f32[1,2]{1,0:T(1,128)} %own_ref.1), custom_call_target="tpu_custom_call" | custom-call | tf_op jit(solution)/shard_map/pack/pallas_call | solution.py:327
  1.1 7.0 %collective-permute-start = (bf16[72,128]{1,0:T(8,128)(2,1)S(1)}, bf16[72,128]{1,0:T(8,128)(2,1)S(1)}, u32[]{:S(2)}, u32[]{:S(2)}) collective-permute-start(bf16[72,128]{1,0:T(8,128)(2,1)S(1)} %pack.1), channel_id=1, source_target_pairs={{192,0},{193,1},{194,2},{195,3},{132,4},{133,5},{134,6},{135,7},{2... | collective-permute-start | bytes 55304 | tf_op jit(solution)/shard_map/ppermute | solution.py:337
  8.1 1.4 %collective-permute-done.block_ref = bf16[72,128]{1,0:T(8,128)(2,1)S(1)} collective-permute-done((bf16[72,128]{1,0:T(8,128)(2,1)S(1)}, bf16[72,128]{1,0:T(8,128)(2,1)S(1)}, u32[]{:S(2)}, u32[]{:S(2)}) %collective-permute-start) | collective-permute-done | bytes 18464 | tf_op jit(solution)/shard_map/ppermute | solution.py:337
  9.6 0.7 %spread.1 = bf16[16,72,128]{2,1,0:T(8,128)(2,1)} custom-call(bf16[72,128]{1,0:T(8,128)(2,1)S(1)} %collective-permute-done.block_ref), custom_call_target="tpu_custom_call" | custom-call | tf_op jit(solution)/shard_map/spread/pallas_call | solution.py:342
  10.3 0.0 copy-start
  10.3 0.0 copy-start.1
  10.3 6.9 %all-to-all-start = ((bf16[16,72,128]{2,1,0:T(8,128)(2,1)}), bf16[16,72,128]{2,1,0:T(8,128)(2,1)S(1)}, u32[]{:S(2)}, u32[]{:S(2)}) async-start(bf16[16,72,128]{2,1,0:T(8,128)(2,1)} %spread.1), calls=%async_computation | async-start | bytes 589824 | tf_op jit(solution)/shard_map/all_to_all | solution.py:341
  17.2 0.0 copy-start.2
  17.2 0.1 pad_add_fusion.place_ref
  17.3 0.6 %copy-done.2 = f32[1,2]{1,0:T(1,128)S(1)} copy-done((f32[1,2]{1,0:T(1,128)S(1)}, f32[1,2]{1,0:T(1,128)}, u32[]{:S(2)}) %copy-start.2) | copy-done | bytes 32
  17.9 1.0 %collective-permute-start.1 = (f32[1,2]{1,0:T(1,128)S(1)}, f32[1,2]{1,0:T(1,128)S(1)}, u32[]{:S(2)}, u32[]{:S(2)}) collective-permute-start(f32[1,2]{1,0:T(1,128)S(1)} %copy-done.2), channel_id=1, source_target_pairs={{0,64},{64,0},{128,192},{192,128},{1,65},{65,1},{129,193},{193,129... | collective-permute-start | bytes 32 | tf_op jit(solution)/shard_map/ppermute | solution.py:339
  18.9 0.8 %collective-permute-done.1.pair_ref = f32[1,2]{1,0:T(1,128)S(1)} collective-permute-done((f32[1,2]{1,0:T(1,128)S(1)}, f32[1,2]{1,0:T(1,128)S(1)}, u32[]{:S(2)}, u32[]{:S(2)}) %collective-permute-start.1) | collective-permute-done | bytes 40 | tf_op jit(solution)/shard_map/ppermute | solution.py:339
  19.7 5.4 %all-to-all-done.blocks_ref = bf16[16,72,128]{2,1,0:T(8,128)(2,1)S(1)} async-done(((bf16[16,72,128]{2,1,0:T(8,128)(2,1)}), bf16[16,72,128]{2,1,0:T(8,128)(2,1)S(1)}, u32[]{:S(2)}, u32[]{:S(2)}) %all-to-all-start) | async-done | bytes 294944 | tf_op jit(solution)/shard_map/all_to_all | solution.py:341
  25.1 0.0 copy-done
  25.1 0.0 copy-done.1
  25.1 11.0 %grid.1 = (f32[32,512]{1,0:T(8,128)S(1)}, bf16[32,512]{1,0:T(8,128)(2,1)S(1)}, bf16[32,512]{1,0:T(8,128)(2,1)S(1)}, bf16[32,512]{1,0:T(8,128)(2,1)S(1)}) custom-call(s32[2]{0:T(128)S(1)} %pad_add_fusion.place_ref, bf16[16,72,128]{2,1,0:T(8,128)(2,1)S(1)} %all-to-all-done.blocks_ref, f32[1,2]{1,0:T(1,128)S(1)} %copy-done.2, ...), custom_call_target="tpu_custom_call" | custom-call | tf_op jit(solution)/shard_map/grid/pallas_call | solution.py:360
  36.2 2.2 %collective-permute-start.2 = (bf16[32,512]{1,0:T(8,128)(2,1)S(1)}, bf16[32,512]{1,0:T(8,128)(2,1)S(1)}, u32[]{:S(2)}, u32[]{:S(2)}) collective-permute-start(bf16[32,512]{1,0:T(8,128)(2,1)S(1)} %get-tuple-element.14), channel_id=1, source_target_pairs={{0,64},{64,0},{128,192},{192,128},{1,65},{65,1},{129,193},{193,129... | collective-permute-start | bytes 98312 | tf_op jit(solution)/shard_map/ppermute | solution.py:385
  38.3 0.0 collective-permute-start.3
  38.3 1.7 %collective-permute-start.4 = (bf16[32,512]{1,0:T(8,128)(2,1)S(1)}, bf16[32,512]{1,0:T(8,128)(2,1)S(1)}, u32[]{:S(2)}, u32[]{:S(2)}) collective-permute-start(bf16[32,512]{1,0:T(8,128)(2,1)S(1)} %get-tuple-element.16), channel_id=1, source_target_pairs={{0,192},{64,128},{128,64},{192,0},{1,193},{65,129},{129,65},{193,1... | collective-permute-start | bytes 98312 | tf_op jit(solution)/shard_map/ppermute | solution.py:385
  40.1 0.0 collective-permute-done.2.p1
  40.1 1.0 %collective-permute-done.3.p2 = bf16[32,512]{1,0:T(8,128)(2,1)S(1)} collective-permute-done((bf16[32,512]{1,0:T(8,128)(2,1)S(1)}, bf16[32,512]{1,0:T(8,128)(2,1)S(1)}, u32[]{:S(2)}, u32[]{:S(2)}) %collective-permute-start.3) | collective-permute-done | bytes 32800 | tf_op jit(solution)/shard_map/ppermute | solution.py:385
  41.1 1.1 %collective-permute-done.4.p3 = bf16[32,512]{1,0:T(8,128)(2,1)S(1)} collective-permute-done((bf16[32,512]{1,0:T(8,128)(2,1)S(1)}, bf16[32,512]{1,0:T(8,128)(2,1)S(1)}, u32[]{:S(2)}, u32[]{:S(2)}) %collective-permute-start.4) | collective-permute-done | bytes 32800 | tf_op jit(solution)/shard_map/ppermute | solution.py:385
  42.2 0.0 copy-done.3
  42.2 1.2 %blend.1 = f32[3,1,4096]{2,1,0:T(1,128)} custom-call(s32[2]{0:T(128)S(1)} %pad_add_fusion.place_ref, f32[32,512]{1,0:T(8,128)S(1)} %get-tuple-element.13.p0, bf16[32,512]{1,0:T(8,128)(2,1)S(1)} %collective-permute-done.2.p1, bf16[32,512]{1,0:T(8,128)(2,1)S(1)} %collective-permute-done.3.p2, bf16[32,512]{1,0:T(8,128)(2,1)S(1)} %collective-permute-done.4.p3, ...), custom_call_target="tpu_custom_call" | custom-call | tf_op jit(solution)/shard_map/blend/pallas_call | solution.py:386
  (1 shorter events, 0.0 us)
Async XLA Ops:
  1.1 8.5 %collective-permute-start = (bf16[72,128]{1,0:T(8,128)(2,1)S(1)}, bf16[72,128]{1,0:T(8,128)(2,1)S(1)}, u32[]{:S(2)}, u32[]{:S(2)}) collective-permute-start(bf16[72,128]{1,0:T(8,128)(2,1)S(1)} %pack.1), channel_id=1, source_target_pairs={{192,0},{193,1},{194,2},{195,3},{132,4},{133,5},{134,6},{135,7},{2... | collective-permute-start | bytes 55304 | tf_op jit(solution)/shard_map/ppermute | solution.py:337
  10.3 14.8 %copy-start = (f32[96,192]{1,0:T(8,128)S(1)}, f32[96,192]{1,0:T(8,128)}, u32[]{:S(2)}) copy-start(f32[96,192]{1,0:T(8,128)} %constant.17.clone.second_ref) | copy-start | bytes 221188
  10.3 14.8 %copy-start.1 = (f32[16,512]{1,0:T(8,128)S(1)}, f32[16,512]{1,0:T(8,128)}, u32[]{:S(2)}) copy-start(f32[16,512]{1,0:T(8,128)} %constant.16.clone.twiddle_ref) | copy-start | bytes 98308
  10.3 14.8 %all-to-all-start = ((bf16[16,72,128]{2,1,0:T(8,128)(2,1)}), bf16[16,72,128]{2,1,0:T(8,128)(2,1)S(1)}, u32[]{:S(2)}, u32[]{:S(2)}) async-start(bf16[16,72,128]{2,1,0:T(8,128)(2,1)} %spread.1), calls=%async_computation | async-start | bytes 589824 | tf_op jit(solution)/shard_map/all_to_all | solution.py:341
  17.2 0.7 %copy-start.2 = (f32[1,2]{1,0:T(1,128)S(1)}, f32[1,2]{1,0:T(1,128)}, u32[]{:S(2)}) copy-start(f32[1,2]{1,0:T(1,128)} %own_ref.1) | copy-start | bytes 28
  17.9 1.8 %collective-permute-start.1 = (f32[1,2]{1,0:T(1,128)S(1)}, f32[1,2]{1,0:T(1,128)S(1)}, u32[]{:S(2)}, u32[]{:S(2)}) collective-permute-start(f32[1,2]{1,0:T(1,128)S(1)} %copy-done.2), channel_id=1, source_target_pairs={{0,64},{64,0},{128,192},{192,128},{1,65},{65,1},{129,193},{193,129... | collective-permute-start | bytes 32 | tf_op jit(solution)/shard_map/ppermute | solution.py:339
  36.2 3.9 %collective-permute-start.2 = (bf16[32,512]{1,0:T(8,128)(2,1)S(1)}, bf16[32,512]{1,0:T(8,128)(2,1)S(1)}, u32[]{:S(2)}, u32[]{:S(2)}) collective-permute-start(bf16[32,512]{1,0:T(8,128)(2,1)S(1)} %get-tuple-element.14), channel_id=1, source_target_pairs={{0,64},{64,0},{128,192},{192,128},{1,65},{65,1},{129,193},{193,129... | collective-permute-start | bytes 98312 | tf_op jit(solution)/shard_map/ppermute | solution.py:385
  38.3 2.8 %collective-permute-start.3 = (bf16[32,512]{1,0:T(8,128)(2,1)S(1)}, bf16[32,512]{1,0:T(8,128)(2,1)S(1)}, u32[]{:S(2)}, u32[]{:S(2)}) collective-permute-start(bf16[32,512]{1,0:T(8,128)(2,1)S(1)} %get-tuple-element.15), channel_id=1, source_target_pairs={{0,128},{64,192},{128,0},{192,64},{1,129},{65,193},{129,1},{193,65... | collective-permute-start | bytes 98312 | tf_op jit(solution)/shard_map/ppermute | solution.py:385
  38.3 3.8 %copy-start.3 = (s32[1,1,256]{2,1,0:T(1,128)S(1)}, s32[1,1,256]{2,1,0:T(1,128)}, u32[]{:S(2)}) copy-start(s32[1,1,256]{2,1,0:T(1,128)} %mask_ref.1) | copy-start | bytes 3076
  38.3 3.8 %collective-permute-start.4 = (bf16[32,512]{1,0:T(8,128)(2,1)S(1)}, bf16[32,512]{1,0:T(8,128)(2,1)S(1)}, u32[]{:S(2)}, u32[]{:S(2)}) collective-permute-start(bf16[32,512]{1,0:T(8,128)(2,1)S(1)} %get-tuple-element.16), channel_id=1, source_target_pairs={{0,192},{64,128},{128,64},{192,0},{1,193},{65,129},{129,65},{193,1... | collective-permute-start | bytes 98312 | tf_op jit(solution)/shard_map/ppermute | solution.py:385

commit v5 on v4

--- a/solution.py
+++ b/solution.py
@@ -26,7 +26,7 @@
 COARSE = GRID // 2 // FINE
 XB = GRID // FINE
 VALS = FACETS * TERMS
-STEP = 256
+STEP = 2
 CHUNK = 32
 
 COS = (0.99999999, -19.73920447, 64.93911593, -85.45011343, 60.16742979, -25.96688461, 6.52770596)
@@ -136,8 +136,7 @@
 
 def grid_kernel(
     place_ref, blocks_ref, own_ref, pair_ref, first_hbm, twiddle_ref, second_ref, o0, o1, o2, o3,
-    terms0, terms1, cells0, cells1, left0, left1, right0, right1, total_ref, image_ref,
-    iota_ref, first_ref, sem,
+    terms0, terms1, cells0, cells1, total_ref, image_ref, iota_ref, first_ref, sem,
 ):
     table = pltpu.make_async_copy(first_hbm, first_ref, sem)
     table.start()
@@ -150,7 +149,7 @@
     step = (row - IMG_ROWS // 2).astype(jnp.float32) * (1.0 / GRID)
     count = lax.broadcasted_iota(jnp.int32, (COARSE, 2 * CH), 0)
     iota_ref[...] = count.astype(jnp.float32).astype(jnp.bfloat16)
-    fine_iota = (count[: 2 * FINE] & (FINE - 1)).astype(jnp.float32).astype(jnp.bfloat16)
+    fine_iota = count[:FINE].astype(jnp.float32)
     one = jnp.ones((2 * FINE, 2 * CH), jnp.bfloat16)
     zero = jnp.zeros((2 * FINE, 2 * CH), jnp.bfloat16)
 
@@ -198,57 +197,49 @@
             bi = ca * ri + sa * rr
             bi = bi * sign + br * mid
             br = br * keep
-            for part, base in ((0, br), (1, bi)):
-                at = part * VALS + q * TERMS
-                terms_ref[at] = base
-                terms_ref[at + 1] = base * nu
-                terms_ref[at + 2] = base * nu2
-
-    def expand(i, terms_ref, cell_ref, left_ref, right_ref):
-        cols = slice(i * 2 * CH, (i + 1) * 2 * CH)
-        fine = jnp.broadcast_to(cell_ref[0, i : i + 1, :], (2 * FINE, 2 * CH)).astype(jnp.bfloat16)
-        here = fine == fine_iota
-        vals = jnp.broadcast_to(terms_ref[:, i : i + 1, :], (2 * VALS, FINE, 2 * CH))
-        vals = vals.reshape(2 * VALS * FINE, 2 * CH).astype(jnp.bfloat16)
+            terms_ref[q] = br
+            terms_ref[SIDE + q] = bi
+
+    def expand(i, terms_ref, cell_ref):
+        fine = jnp.broadcast_to(cell_ref[0, i : i + 1, :], (FINE, 2 * CH)) == fine_iota
+        left = []
+        for k in range(FACETS):
+            terms = []
+            for base in (2 * k, 2 * k + 1):
+                base = jnp.broadcast_to(terms_ref[base, i : i + 1, :], (FINE, 2 * CH))
+                base = jnp.where(fine, base, 0.0)
+                terms += [base, base * nu[:FINE], base * nu2[:FINE]]
+            left.append(jnp.concatenate(terms, 0).astype(jnp.bfloat16))
         coarse = jnp.broadcast_to(cell_ref[1, i : i + 1, :], (2 * FINE, 2 * CH))
         coarse = coarse.astype(jnp.bfloat16)
-        for m in range(VALS):
-            rows = slice(m * 2 * FINE, (m + 1) * 2 * FINE)
-            left_ref[rows, cols] = jnp.where(here, vals[rows], zero)
-        for m in range(COARSE // (2 * FINE)):
-            rows = slice(m * 2 * FINE, (m + 1) * 2 * FINE)
-            right_ref[rows, cols] = jnp.where(coarse == iota_ref[rows], one, zero)
-
-    def product(i, left_ref, right_ref):
-        cols = slice(i * STEP, (i + 1) * STEP)
-        return lax.dot_general(
-            right_ref[:, cols], left_ref[:, cols], (((1,), (1,)), ((), ())),
-            preferred_element_type=jnp.float32,
-        )
+        right = [
+            jnp.where(coarse == iota_ref[m * 2 * FINE : (m + 1) * 2 * FINE], one, zero)
+            for m in range(COARSE // (2 * FINE))
+        ]
+        return jnp.concatenate(left, 0), jnp.concatenate(right, 0)
 
     def turn(block, here, ahead):
         part = total_ref[...]
-        per = STEP // (2 * CH)
-        elements(block, here[0], here[1])
-        for i in range(ROWS * CH // STEP):
-            part = part + product(i, here[2], here[3])
-            for j in range(per):
-                expand(i * per + j, *ahead)
+        elements(block, ahead[0], ahead[1])
+        for i in range(0, HALF, STEP):
+            both = [expand(i + j, here[0], here[1]) for j in range(STEP)]
+            left = jnp.concatenate([sides[0] for sides in both], 1)
+            right = jnp.concatenate([sides[1] for sides in both], 1)
+            part = part + lax.dot_general(
+                right, left, (((1,), (1,)), ((), ())), preferred_element_type=jnp.float32
+            )
         total_ref[...] = part
 
-    even, odd = (terms0, cells0, left0, right0), (terms1, cells1, left1, right1)
+    even, odd = (terms0, cells0), (terms1, cells1)
     total_ref[...] = jnp.zeros_like(total_ref)
     elements(0, terms0, cells0)
-    for i in range(HALF):
-        expand(i, *even)
-    elements(1, terms1, cells1)
 
     def two(i, carry):
-        turn(jnp.minimum(2 * i + 2, BLOCKS - 1), even, odd)
-        turn(jnp.minimum(2 * i + 3, BLOCKS - 1), odd, even)
+        turn(2 * i + 1, even, odd)
+        turn(jnp.minimum(2 * i + 2, BLOCKS - 1), odd, even)
         return carry
 
-    lax.fori_loop(0, BLOCKS // 2, two, 0)
+    lax.fori_loop(0, BLOCKS // 2, two, 0, unroll=4)
 
     span = VALS * FINE
     flat = total_ref[...].T
@@ -314,6 +305,38 @@
                     source = ((3 - facet) ^ (y & 1)) * IMG_ROWS + plane * BLOCKS + here
                     pairs.append((source, facet * IMG_ROWS + z * BLOCKS + here))
     return pairs
+
+
+def partial_images(place, blocks, centres, pair):
+    vmem = pl.BlockSpec(memory_space=pltpu.VMEM)
+    smem = pl.BlockSpec(memory_space=pltpu.SMEM)
+    hbm = pl.BlockSpec(memory_space=pltpu.HBM)
+    first, twiddle, second = tables()
+    first = pltpu.with_memory_space_constraint(first, pltpu.HBM)
+    chunk = [
+        jax.ShapeDtypeStruct((CHUNK, XB), jnp.bfloat16 if s else jnp.float32)
+        for s in range(FACETS)
+    ]
+    span = 2 * VALS * FINE
+    return pl.pallas_call(
+        grid_kernel,
+        out_shape=chunk,
+        in_specs=[smem] + [vmem] * 3 + [hbm] + [vmem] * 2,
+        out_specs=[vmem] * FACETS,
+        scratch_shapes=[
+            pltpu.VMEM((2 * FACETS, HALF, 2 * CH), jnp.float32),
+            pltpu.VMEM((2 * FACETS, HALF, 2 * CH), jnp.float32),
+            pltpu.VMEM((2, HALF, 2 * CH), jnp.float32),
+            pltpu.VMEM((2, HALF, 2 * CH), jnp.float32),
+            pltpu.VMEM((COARSE, span), jnp.float32),
+            pltpu.VMEM((VALS * FINE, XB), jnp.float32),
+            pltpu.VMEM((COARSE, 2 * CH), jnp.bfloat16),
+            pltpu.VMEM((2 * COARSE, 2 * XB), jnp.bfloat16),
+            pltpu.SemaphoreType.DMA,
+        ],
+        compiler_params=pltpu.CompilerParams(vmem_limit_bytes=16 << 20),
+        name="grid",
+    )(place, blocks, centres, pair, first, twiddle, second)
 
 
 def per_device(visibilities, uv_coords, cells, centres, intersection_mask):
@@ -349,37 +372,7 @@
         )(packed),
         "vis", 0, 0, axis_index_groups=planes,
     )
-    first, twiddle, second = tables()
-    first = pltpu.with_memory_space_constraint(first, pltpu.HBM)
-    chunk = [
-        jax.ShapeDtypeStruct((CHUNK, XB), jnp.bfloat16 if s else jnp.float32)
-        for s in range(FACETS)
-    ]
-    span = 2 * VALS * FINE
-    wide = ROWS * CH
-    parts = pl.pallas_call(
-        grid_kernel,
-        out_shape=chunk,
-        in_specs=[smem] + [vmem] * 3 + [hbm] + [vmem] * 2,
-        out_specs=[vmem] * FACETS,
-        scratch_shapes=[
-            pltpu.VMEM((2 * VALS, HALF, 2 * CH), jnp.float32),
-            pltpu.VMEM((2 * VALS, HALF, 2 * CH), jnp.float32),
-            pltpu.VMEM((2, HALF, 2 * CH), jnp.float32),
-            pltpu.VMEM((2, HALF, 2 * CH), jnp.float32),
-            pltpu.VMEM((span, wide), jnp.bfloat16),
-            pltpu.VMEM((span, wide), jnp.bfloat16),
-            pltpu.VMEM((COARSE, wide), jnp.bfloat16),
-            pltpu.VMEM((COARSE, wide), jnp.bfloat16),
-            pltpu.VMEM((COARSE, span), jnp.float32),
-            pltpu.VMEM((VALS * FINE, XB), jnp.float32),
-            pltpu.VMEM((COARSE, 2 * CH), jnp.bfloat16),
-            pltpu.VMEM((2 * COARSE, 2 * XB), jnp.bfloat16),
-            pltpu.SemaphoreType.DMA,
-        ],
-        compiler_params=pltpu.CompilerParams(vmem_limit_bytes=40 << 20),
-        name="grid",
-    )(place, blocks, centres, pair, first, twiddle, second)
+    parts = partial_images(place, blocks, centres, pair)
     got = [parts[0]]
     for s in range(1, FACETS):
         got.append(lax.ppermute(parts[s], "facet", [(i, i ^ s) for i in range(FACETS)]))

time: 43.6 us -> 39.5 us (0.906)
  Pallas kernels: 14.1 us -> 9.93 us
    pallas_call x1, Pallas kernels: 11 us -> 6.91 us  [partial_images(): pl.pallas_call(grid_kernel, out_shape=chunk, in_specs=[smem] + [vmem] * 3...]
where the time goes in v5:
time: 39.5 us; the launch traced here: 39.3 us
  starting transfers between devices  18.9 us (48%)
  Pallas kernels  9.93 us (25%)
  waiting for transfers between devices  9.76 us (25%)
  local copies, waits for them, and re-layouts  0.59 us (1%)
    ppermute x1, starting transfers between devices, per_device(): packed = lax.ppermute(packed, ('facet', 'vis'), swap_pairs())  7.04 us
    pallas_call x1, Pallas kernels, partial_images(): pl.pallas_call(grid_kernel, out_shape=chunk, in_specs=[smem] + [vmem] * 3...  6.91 us
    all_to_all x1, starting transfers between devices, per_device(): lax.all_to_all(pl.pallas_call(spread_kernel, out_shape=jax.ShapeDtypeStru...  6.89 us
    all_to_all x1, waiting for transfers between devices, per_device(): lax.all_to_all(pl.pallas_call(spread_kernel, out_shape=jax.ShapeDtypeStru...  5.39 us
    ppermute x3, starting transfers between devices, per_device(): lax.ppermute(parts[s], 'facet', [(i, i ^ s) for i in range(FACETS)])  3.91 us
    ppermute x3, waiting for transfers between devices, per_device(): lax.ppermute(parts[s], 'facet', [(i, i ^ s) for i in range(FACETS)])  2.1 us
    ppermute x1, waiting for transfers between devices, per_device(): packed = lax.ppermute(packed, ('facet', 'vis'), swap_pairs())  1.45 us
    pallas_call x1, Pallas kernels, per_device(): pl.pallas_call(blend_kernel, out_shape=jax.ShapeDtypeStruct((TERMS, 1, GR...  1.2 us
  transfers between devices with their start and end apart: 6, of which 5 were waited for; matrix products, arithmetic and copies ran while one was open for 0% of the time, Pallas kernels for 0%

profile of v5, /device:TPU:1, one launch (start us, length us, event | category | flops | bytes accessed | tf_op | source)
XLA Modules:
  0.0 39.3 jit_solution(4289446635438553524)
XLA Ops:
  0.0 1.1 %pack.1 = bf16[72,128]{1,0:T(8,128)(2,1)S(1)} custom-call(bf16[32,128]{1,0:T(8,128)(2,1)} %vis_hbm.1, f32[2,32]{1,0:T(2,128)} %bitcast.3, s32[2,32,64]{2,1,0:T(8,128)} %cells_hbm.1, f32[1,2]{1,0:T(1,128)} %own_ref.1), custom_call_target="tpu_custom_call" | custom-call | tf_op jit(solution)/shard_map/pack/pallas_call | solution.py:350
  1.1 7.0 %collective-permute-start = (bf16[72,128]{1,0:T(8,128)(2,1)S(1)}, bf16[72,128]{1,0:T(8,128)(2,1)S(1)}, u32[]{:S(2)}, u32[]{:S(2)}) collective-permute-start(bf16[72,128]{1,0:T(8,128)(2,1)S(1)} %pack.1), channel_id=1, source_target_pairs={{192,0},{193,1},{194,2},{195,3},{132,4},{133,5},{134,6},{135,7},{2... | collective-permute-start | bytes 55304 | tf_op jit(solution)/shard_map/ppermute | solution.py:360
  8.1 1.4 %collective-permute-done.block_ref = bf16[72,128]{1,0:T(8,128)(2,1)S(1)} collective-permute-done((bf16[72,128]{1,0:T(8,128)(2,1)S(1)}, bf16[72,128]{1,0:T(8,128)(2,1)S(1)}, u32[]{:S(2)}, u32[]{:S(2)}) %collective-permute-start) | collective-permute-done | bytes 18464 | tf_op jit(solution)/shard_map/ppermute | solution.py:360
  9.6 0.7 %spread.1 = bf16[16,72,128]{2,1,0:T(8,128)(2,1)} custom-call(bf16[72,128]{1,0:T(8,128)(2,1)S(1)} %collective-permute-done.block_ref), custom_call_target="tpu_custom_call" | custom-call | tf_op jit(solution)/shard_map/spread/pallas_call | solution.py:365
  10.3 0.0 copy-start
  10.3 0.0 copy-start.1
  10.3 6.9 %all-to-all-start = ((bf16[16,72,128]{2,1,0:T(8,128)(2,1)}), bf16[16,72,128]{2,1,0:T(8,128)(2,1)S(1)}, u32[]{:S(2)}, u32[]{:S(2)}) async-start(bf16[16,72,128]{2,1,0:T(8,128)(2,1)} %spread.1), calls=%async_computation | async-start | bytes 589824 | tf_op jit(solution)/shard_map/all_to_all | solution.py:364
  17.2 0.0 copy-start.2
  17.2 0.1 pad_add_fusion.place_ref
  17.3 0.6 %copy-done.2 = f32[1,2]{1,0:T(1,128)S(1)} copy-done((f32[1,2]{1,0:T(1,128)S(1)}, f32[1,2]{1,0:T(1,128)}, u32[]{:S(2)}) %copy-start.2) | copy-done | bytes 32
  17.9 1.0 %collective-permute-start.1 = (f32[1,2]{1,0:T(1,128)S(1)}, f32[1,2]{1,0:T(1,128)S(1)}, u32[]{:S(2)}, u32[]{:S(2)}) collective-permute-start(f32[1,2]{1,0:T(1,128)S(1)} %copy-done.2), channel_id=1, source_target_pairs={{0,64},{64,0},{128,192},{192,128},{1,65},{65,1},{129,193},{193,129... | collective-permute-start | bytes 32 | tf_op jit(solution)/shard_map/ppermute | solution.py:362
  18.9 0.8 %collective-permute-done.1.pair_ref = f32[1,2]{1,0:T(1,128)S(1)} collective-permute-done((f32[1,2]{1,0:T(1,128)S(1)}, f32[1,2]{1,0:T(1,128)S(1)}, u32[]{:S(2)}, u32[]{:S(2)}) %collective-permute-start.1) | collective-permute-done | bytes 40 | tf_op jit(solution)/shard_map/ppermute | solution.py:362
  19.7 5.4 %all-to-all-done.blocks_ref = bf16[16,72,128]{2,1,0:T(8,128)(2,1)S(1)} async-done(((bf16[16,72,128]{2,1,0:T(8,128)(2,1)}), bf16[16,72,128]{2,1,0:T(8,128)(2,1)S(1)}, u32[]{:S(2)}, u32[]{:S(2)}) %all-to-all-start) | async-done | bytes 294944 | tf_op jit(solution)/shard_map/all_to_all | solution.py:364
  25.1 0.0 copy-done
  25.1 0.0 copy-done.1
  25.1 6.9 %grid.1 = (f32[32,512]{1,0:T(8,128)S(1)}, bf16[32,512]{1,0:T(8,128)(2,1)S(1)}, bf16[32,512]{1,0:T(8,128)(2,1)S(1)}, bf16[32,512]{1,0:T(8,128)(2,1)S(1)}) custom-call(s32[2]{0:T(128)S(1)} %pad_add_fusion.place_ref, bf16[16,72,128]{2,1,0:T(8,128)(2,1)S(1)} %all-to-all-done.blocks_ref, f32[1,2]{1,0:T(1,128)S(1)} %copy-done.2, ...), custom_call_target="tpu_custom_call" | custom-call | tf_op jit(solution)/shard_map/grid/pallas_call | solution.py:321
  32.0 2.2 %collective-permute-start.2 = (bf16[32,512]{1,0:T(8,128)(2,1)S(1)}, bf16[32,512]{1,0:T(8,128)(2,1)S(1)}, u32[]{:S(2)}, u32[]{:S(2)}) collective-permute-start(bf16[32,512]{1,0:T(8,128)(2,1)S(1)} %get-tuple-element.14), channel_id=1, source_target_pairs={{0,64},{64,0},{128,192},{192,128},{1,65},{65,1},{129,193},{193,129... | collective-permute-start | bytes 98312 | tf_op jit(solution)/shard_map/ppermute | solution.py:378
  34.2 0.0 collective-permute-start.3
  34.2 1.7 %collective-permute-start.4 = (bf16[32,512]{1,0:T(8,128)(2,1)S(1)}, bf16[32,512]{1,0:T(8,128)(2,1)S(1)}, u32[]{:S(2)}, u32[]{:S(2)}) collective-permute-start(bf16[32,512]{1,0:T(8,128)(2,1)S(1)} %get-tuple-element.16), channel_id=1, source_target_pairs={{0,192},{64,128},{128,64},{192,0},{1,193},{65,129},{129,65},{193,1... | collective-permute-start | bytes 98312 | tf_op jit(solution)/shard_map/ppermute | solution.py:378
  36.0 0.0 collective-permute-done.2.p1
  36.0 1.0 %collective-permute-done.3.p2 = bf16[32,512]{1,0:T(8,128)(2,1)S(1)} collective-permute-done((bf16[32,512]{1,0:T(8,128)(2,1)S(1)}, bf16[32,512]{1,0:T(8,128)(2,1)S(1)}, u32[]{:S(2)}, u32[]{:S(2)}) %collective-permute-start.3) | collective-permute-done | bytes 32800 | tf_op jit(solution)/shard_map/ppermute | solution.py:378
  37.0 1.1 %collective-permute-done.4.p3 = bf16[32,512]{1,0:T(8,128)(2,1)S(1)} collective-permute-done((bf16[32,512]{1,0:T(8,128)(2,1)S(1)}, bf16[32,512]{1,0:T(8,128)(2,1)S(1)}, u32[]{:S(2)}, u32[]{:S(2)}) %collective-permute-start.4) | collective-permute-done | bytes 32800 | tf_op jit(solution)/shard_map/ppermute | solution.py:378
  38.1 0.0 copy-done.3
  38.1 1.2 %blend.1 = f32[3,1,4096]{2,1,0:T(1,128)} custom-call(s32[2]{0:T(128)S(1)} %pad_add_fusion.place_ref, f32[32,512]{1,0:T(8,128)S(1)} %get-tuple-element.13.p0, bf16[32,512]{1,0:T(8,128)(2,1)S(1)} %collective-permute-done.2.p1, bf16[32,512]{1,0:T(8,128)(2,1)S(1)} %collective-permute-done.3.p2, bf16[32,512]{1,0:T(8,128)(2,1)S(1)} %collective-permute-done.4.p3, ...), custom_call_target="tpu_custom_call" | custom-call | tf_op jit(solution)/shard_map/blend/pallas_call | solution.py:379
  (1 shorter events, 0.0 us)
Async XLA Ops:
  1.1 8.5 %collective-permute-start = (bf16[72,128]{1,0:T(8,128)(2,1)S(1)}, bf16[72,128]{1,0:T(8,128)(2,1)S(1)}, u32[]{:S(2)}, u32[]{:S(2)}) collective-permute-start(bf16[72,128]{1,0:T(8,128)(2,1)S(1)} %pack.1), channel_id=1, source_target_pairs={{192,0},{193,1},{194,2},{195,3},{132,4},{133,5},{134,6},{135,7},{2... | collective-permute-start | bytes 55304 | tf_op jit(solution)/shard_map/ppermute | solution.py:360
  10.3 14.8 %copy-start = (f32[96,192]{1,0:T(8,128)S(1)}, f32[96,192]{1,0:T(8,128)}, u32[]{:S(2)}) copy-start(f32[96,192]{1,0:T(8,128)} %constant.17.clone.second_ref) | copy-start | bytes 221188
  10.3 14.8 %copy-start.1 = (f32[16,512]{1,0:T(8,128)S(1)}, f32[16,512]{1,0:T(8,128)}, u32[]{:S(2)}) copy-start(f32[16,512]{1,0:T(8,128)} %constant.16.clone.twiddle_ref) | copy-start | bytes 98308
  10.3 14.8 %all-to-all-start = ((bf16[16,72,128]{2,1,0:T(8,128)(2,1)}), bf16[16,72,128]{2,1,0:T(8,128)(2,1)S(1)}, u32[]{:S(2)}, u32[]{:S(2)}) async-start(bf16[16,72,128]{2,1,0:T(8,128)(2,1)} %spread.1), calls=%async_computation | async-start | bytes 589824 | tf_op jit(solution)/shard_map/all_to_all | solution.py:364
  17.2 0.7 %copy-start.2 = (f32[1,2]{1,0:T(1,128)S(1)}, f32[1,2]{1,0:T(1,128)}, u32[]{:S(2)}) copy-start(f32[1,2]{1,0:T(1,128)} %own_ref.1) | copy-start | bytes 28
  17.9 1.8 %collective-permute-start.1 = (f32[1,2]{1,0:T(1,128)S(1)}, f32[1,2]{1,0:T(1,128)S(1)}, u32[]{:S(2)}, u32[]{:S(2)}) collective-permute-start(f32[1,2]{1,0:T(1,128)S(1)} %copy-done.2), channel_id=1, source_target_pairs={{0,64},{64,0},{128,192},{192,128},{1,65},{65,1},{129,193},{193,129... | collective-permute-start | bytes 32 | tf_op jit(solution)/shard_map/ppermute | solution.py:362
  32.0 3.9 %collective-permute-start.2 = (bf16[32,512]{1,0:T(8,128)(2,1)S(1)}, bf16[32,512]{1,0:T(8,128)(2,1)S(1)}, u32[]{:S(2)}, u32[]{:S(2)}) collective-permute-start(bf16[32,512]{1,0:T(8,128)(2,1)S(1)} %get-tuple-element.14), channel_id=1, source_target_pairs={{0,64},{64,0},{128,192},{192,128},{1,65},{65,1},{129,193},{193,129... | collective-permute-start | bytes 98312 | tf_op jit(solution)/shard_map/ppermute | solution.py:378
  34.2 2.8 %collective-permute-start.3 = (bf16[32,512]{1,0:T(8,128)(2,1)S(1)}, bf16[32,512]{1,0:T(8,128)(2,1)S(1)}, u32[]{:S(2)}, u32[]{:S(2)}) collective-permute-start(bf16[32,512]{1,0:T(8,128)(2,1)S(1)} %get-tuple-element.15), channel_id=1, source_target_pairs={{0,128},{64,192},{128,0},{192,64},{1,129},{65,193},{129,1},{193,65... | collective-permute-start | bytes 98312 | tf_op jit(solution)/shard_map/ppermute | solution.py:378
  34.2 3.8 %copy-start.3 = (s32[1,1,256]{2,1,0:T(1,128)S(1)}, s32[1,1,256]{2,1,0:T(1,128)}, u32[]{:S(2)}) copy-start(s32[1,1,256]{2,1,0:T(1,128)} %mask_ref.1) | copy-start | bytes 3076
  34.2 3.8 %collective-permute-start.4 = (bf16[32,512]{1,0:T(8,128)(2,1)S(1)}, bf16[32,512]{1,0:T(8,128)(2,1)S(1)}, u32[]{:S(2)}, u32[]{:S(2)}) collective-permute-start(bf16[32,512]{1,0:T(8,128)(2,1)S(1)} %get-tuple-element.16), channel_id=1, source_target_pairs={{0,192},{64,128},{128,64},{192,0},{1,193},{65,129},{129,65},{193,1... | collective-permute-start | bytes 98312 | tf_op jit(solution)/shard_map/ppermute | solution.py:378

commit v6 on v5

--- a/solution.py
+++ b/solution.py
@@ -2,6 +2,7 @@
 
 import jax
 import jax.numpy as jnp
+import ml_dtypes
 import numpy as np
 from jax import lax
 from jax.experimental import pallas as pl
@@ -50,11 +51,13 @@
     real, imag = np.cos(turn), -np.sin(turn)
     imag[:, 0] = 1.0
     eye = np.eye(VALS)
-    second = np.concatenate([np.kron(eye, real), np.kron(eye, imag)], 1)
+    second = np.concatenate([np.kron(eye, real), np.kron(eye, imag)], 1).astype(np.float32)
+    second_high = second.astype(ml_dtypes.bfloat16)
+    second_low = (second - second_high.astype(np.float32)).astype(ml_dtypes.bfloat16)
     return (
         jnp.asarray(first, jnp.bfloat16),
         jnp.asarray(twiddle, jnp.float32),
-        jnp.asarray(second, jnp.float32),
+        (jnp.asarray(second_high), jnp.asarray(second_low)),
     )
 
 
@@ -135,12 +138,12 @@
 
 
 def grid_kernel(
-    place_ref, blocks_ref, own_ref, pair_ref, first_hbm, twiddle_ref, second_ref, o0, o1, o2, o3,
+    blocks_ref, own_ref, pair_ref, first_hbm, twiddle_ref, high_ref, low_ref, o0, o1, o2, o3,
     terms0, terms1, cells0, cells1, total_ref, image_ref, iota_ref, first_ref, sem,
 ):
     table = pltpu.make_async_copy(first_hbm, first_ref, sem)
     table.start()
-    own, row = place_ref[0], place_ref[1]
+    own, row = lax.axis_index("facet"), lax.axis_index("vis")
     lane = lax.broadcasted_iota(jnp.int32, (HALF, 2 * CH), 1)
     chan = (lane % CH).astype(jnp.float32)
     nu = (2.0 * chan + 1.0 - CH) / CH
@@ -257,9 +260,12 @@
     at_zero = lax.broadcasted_iota(jnp.int32, (1, FINE, XB), 1) == 0
     vi = jnp.where(at_zero, middle * flip, vi)
     both = jnp.concatenate([vr.reshape(span, XB), vi.reshape(span, XB)], 0)
-    image_ref[...] = jnp.dot(
-        second_ref[...], both, preferred_element_type=jnp.float32, precision=lax.Precision.HIGHEST
-    )
+    high = both.astype(jnp.bfloat16)
+    low = (both - high.astype(jnp.float32)).astype(jnp.bfloat16)
+    image = jnp.dot(high_ref[...], high, preferred_element_type=jnp.float32)
+    image = image + jnp.dot(high_ref[...], low, preferred_element_type=jnp.float32)
+    image = image + jnp.dot(low_ref[...], high, preferred_element_type=jnp.float32)
+    image_ref[...] = image
     size = TERMS * FINE
     for s, out in enumerate((o0, o1, o2, o3)):
         spot = (2, 3, 1, 0)[s]
@@ -272,13 +278,13 @@
         out[size:CHUNK] = strips.astype(out.dtype)
 
 
-def blend_kernel(place_ref, p0, p1, p2, p3, mask_ref, out_ref):
+def blend_kernel(p0, p1, p2, p3, mask_ref, out_ref):
     size = TERMS * FINE
     image = p0[...]
     for part in (p1, p2, p3):
         image = image + part[...].astype(jnp.float32)
     strip = image[size : size + TERMS, XB - OVER :]
-    has_left = (place_ref[0] > 0).astype(jnp.float32)
+    has_left = (lax.axis_index("facet") > 0).astype(jnp.float32)
     pixel = lax.broadcasted_iota(jnp.int32, (1, OVER), 1).astype(jnp.float32)
     ramp = 1.0 - (pixel + 0.5) / OVER
     weight = mask_ref[0].astype(jnp.float32) * ramp * has_left
@@ -307,9 +313,8 @@
     return pairs
 
 
-def partial_images(place, blocks, centres, pair):
+def partial_images(blocks, centres, pair):
     vmem = pl.BlockSpec(memory_space=pltpu.VMEM)
-    smem = pl.BlockSpec(memory_space=pltpu.SMEM)
     hbm = pl.BlockSpec(memory_space=pltpu.HBM)
     first, twiddle, second = tables()
     first = pltpu.with_memory_space_constraint(first, pltpu.HBM)
@@ -321,7 +326,7 @@
     return pl.pallas_call(
         grid_kernel,
         out_shape=chunk,
-        in_specs=[smem] + [vmem] * 3 + [hbm] + [vmem] * 2,
+        in_specs=[vmem] * 3 + [hbm] + [vmem] * 3,
         out_specs=[vmem] * FACETS,
         scratch_shapes=[
             pltpu.VMEM((2 * FACETS, HALF, 2 * CH), jnp.float32),
@@ -336,15 +341,12 @@
         ],
         compiler_params=pltpu.CompilerParams(vmem_limit_bytes=16 << 20),
         name="grid",
-    )(place, blocks, centres, pair, first, twiddle, second)
+    )(blocks, centres, pair, first, twiddle, *second)
 
 
 def per_device(visibilities, uv_coords, cells, centres, intersection_mask):
     vmem = pl.BlockSpec(memory_space=pltpu.VMEM)
-    smem = pl.BlockSpec(memory_space=pltpu.SMEM)
     hbm = pl.BlockSpec(memory_space=pltpu.HBM)
-    facet, spot = lax.axis_index("facet"), lax.axis_index("vis")
-    place = jnp.stack([facet, spot]).astype(jnp.int32)
     given = (visibilities, uv_coords.T, cells, centres)
     given = [pltpu.with_memory_space_constraint(one, pltpu.HBM) for one in given]
     packed = pl.pallas_call(
@@ -372,18 +374,18 @@
         )(packed),
         "vis", 0, 0, axis_index_groups=planes,
     )
-    parts = partial_images(place, blocks, centres, pair)
+    parts = partial_images(blocks, centres, pair)
     got = [parts[0]]
-    for s in range(1, FACETS):
+    for s in (2, 3, 1):
         got.append(lax.ppermute(parts[s], "facet", [(i, i ^ s) for i in range(FACETS)]))
     return pl.pallas_call(
         blend_kernel,
         out_shape=jax.ShapeDtypeStruct((TERMS, 1, GRID), jnp.float32),
-        in_specs=[smem] + [vmem] * 5,
+        in_specs=[vmem] * 5,
         out_specs=vmem,
         compiler_params=pltpu.CompilerParams(vmem_limit_bytes=2 << 20),
         name="blend",
-    )(place, *got, intersection_mask)
+    )(*got, intersection_mask)
 
 
 def solution(mesh):

time: 39.5 us -> 38.1 us (0.965)
  Pallas kernels: 9.93 us -> 8.77 us
  local copies, waits for them, and re-layouts: 0.59 us -> 0.02 us
  waiting for transfers between devices: 9.76 us -> 10.2 us
    pallas_call x1, Pallas kernels: 6.91 us -> 6.26 us  [partial_images(): pl.pallas_call(grid_kernel, out_shape=chunk, in_specs=[vmem] * 3 + [hbm]...]
    unnamed x8 -> x10, local copies, waits for them, and re-layouts: 0.59 us -> 0.02 us
    all_to_all x1, waiting for transfers between devices: 5.39 us -> 5.96 us  [per_device(): lax.all_to_all(pl.pallas_call(spread_kernel, out_shape=jax.ShapeDtypeStru...]
    pallas_call x1, Pallas kernels: 1.2 us -> 0.66 us  [per_device(): pl.pallas_call(blend_kernel, out_shape=jax.ShapeDtypeStruct((TERMS, 1, GR...]
  transfers between devices with their start and end apart: 6 -> 6, of which waited for: 5 -> 4; matrix products, arithmetic and copies ran while one was open for 0% -> 0% of each run, Pallas kernels for 0% -> 0%
where the time goes in v6:
time: 38.1 us; the launch traced here: 37.9 us
  starting transfers between devices  18.9 us (50%)
  waiting for transfers between devices  10.2 us (27%)
  Pallas kernels  8.77 us (23%)
    ppermute x1, starting transfers between devices, per_device(): packed = lax.ppermute(packed, ('facet', 'vis'), swap_pairs())  7.04 us
    all_to_all x1, starting transfers between devices, per_device(): lax.all_to_all(pl.pallas_call(spread_kernel, out_shape=jax.ShapeDtypeStru...  6.9 us
    pallas_call x1, Pallas kernels, partial_images(): pl.pallas_call(grid_kernel, out_shape=chunk, in_specs=[vmem] * 3 + [hbm]...  6.26 us
    all_to_all x1, waiting for transfers between devices, per_device(): lax.all_to_all(pl.pallas_call(spread_kernel, out_shape=jax.ShapeDtypeStru...  5.96 us
    ppermute x3, starting transfers between devices, per_device(): lax.ppermute(parts[s], 'facet', [(i, i ^ s) for i in range(FACETS)])  3.81 us
    ppermute x3, waiting for transfers between devices, per_device(): lax.ppermute(parts[s], 'facet', [(i, i ^ s) for i in range(FACETS)])  1.94 us
    ppermute x1, waiting for transfers between devices, per_device(): packed = lax.ppermute(packed, ('facet', 'vis'), swap_pairs())  1.45 us
    ppermute x1, starting transfers between devices, per_device(): pair = lax.ppermute(centre, 'facet', [(i, i ^ 1) for i in range(FACETS)])  1.11 us
  transfers between devices with their start and end apart: 6, of which 4 were waited for; matrix products, arithmetic and copies ran while one was open for 0% of the time, Pallas kernels for 0%

profile of v6, /device:TPU:1, one launch (start us, length us, event | category | flops | bytes accessed | tf_op | source)
XLA Modules:
  0.0 37.9 jit_solution(17158404468809937994)
XLA Ops:
  0.0 1.1 %pack.1 = bf16[72,128]{1,0:T(8,128)(2,1)S(1)} custom-call(bf16[32,128]{1,0:T(8,128)(2,1)} %vis_hbm.1, f32[2,32]{1,0:T(2,128)} %bitcast.1, s32[2,32,64]{2,1,0:T(8,128)} %cells_hbm.1, f32[1,2]{1,0:T(1,128)} %own_ref.1), custom_call_target="tpu_custom_call" | custom-call | tf_op jit(solution)/shard_map/pack/pallas_call | solution.py:352
  1.1 7.0 %collective-permute-start = (bf16[72,128]{1,0:T(8,128)(2,1)S(1)}, bf16[72,128]{1,0:T(8,128)(2,1)S(1)}, u32[]{:S(2)}, u32[]{:S(2)}) collective-permute-start(bf16[72,128]{1,0:T(8,128)(2,1)S(1)} %pack.1), channel_id=1, source_target_pairs={{192,0},{193,1},{194,2},{195,3},{132,4},{133,5},{134,6},{135,7},{2... | collective-permute-start | bytes 55304 | tf_op jit(solution)/shard_map/ppermute | solution.py:362
  8.1 1.4 %collective-permute-done.block_ref = bf16[72,128]{1,0:T(8,128)(2,1)S(1)} collective-permute-done((bf16[72,128]{1,0:T(8,128)(2,1)S(1)}, bf16[72,128]{1,0:T(8,128)(2,1)S(1)}, u32[]{:S(2)}, u32[]{:S(2)}) %collective-permute-start) | collective-permute-done | bytes 18464 | tf_op jit(solution)/shard_map/ppermute | solution.py:362
  9.6 0.8 %spread.1 = bf16[16,72,128]{2,1,0:T(8,128)(2,1)} custom-call(bf16[72,128]{1,0:T(8,128)(2,1)S(1)} %collective-permute-done.block_ref), custom_call_target="tpu_custom_call" | custom-call | tf_op jit(solution)/shard_map/spread/pallas_call | solution.py:367
  10.3 0.0 copy-start.3
  10.3 0.0 copy-start
  10.3 0.0 copy-start.1
  10.4 6.9 %all-to-all-start = ((bf16[16,72,128]{2,1,0:T(8,128)(2,1)}), bf16[16,72,128]{2,1,0:T(8,128)(2,1)S(1)}, u32[]{:S(2)}, u32[]{:S(2)}) async-start(bf16[16,72,128]{2,1,0:T(8,128)(2,1)} %spread.1), calls=%async_computation | async-start | bytes 589824 | tf_op jit(solution)/shard_map/all_to_all | solution.py:366
  17.3 0.0 copy-done.3
  17.3 1.1 %collective-permute-start.1 = (f32[1,2]{1,0:T(1,128)S(1)}, f32[1,2]{1,0:T(1,128)S(1)}, u32[]{:S(2)}, u32[]{:S(2)}) collective-permute-start(f32[1,2]{1,0:T(1,128)S(1)} %copy-done.3), channel_id=1, source_target_pairs={{0,64},{64,0},{128,192},{192,128},{1,65},{65,1},{129,193},{193,129... | collective-permute-start | bytes 32 | tf_op jit(solution)/shard_map/ppermute | solution.py:364
  18.4 0.8 %collective-permute-done.1.pair_ref = f32[1,2]{1,0:T(1,128)S(1)} collective-permute-done((f32[1,2]{1,0:T(1,128)S(1)}, f32[1,2]{1,0:T(1,128)S(1)}, u32[]{:S(2)}, u32[]{:S(2)}) %collective-permute-start.1) | collective-permute-done | bytes 40 | tf_op jit(solution)/shard_map/ppermute | solution.py:364
  19.2 6.0 %all-to-all-done.blocks_ref = bf16[16,72,128]{2,1,0:T(8,128)(2,1)S(1)} async-done(((bf16[16,72,128]{2,1,0:T(8,128)(2,1)}), bf16[16,72,128]{2,1,0:T(8,128)(2,1)S(1)}, u32[]{:S(2)}, u32[]{:S(2)}) %all-to-all-start) | async-done | bytes 294944 | tf_op jit(solution)/shard_map/all_to_all | solution.py:366
  25.1 0.0 copy-done
  25.2 0.0 copy-done.1
  25.2 0.0 copy-done.2
  25.2 6.3 %grid.1 = (f32[32,512]{1,0:T(8,128)S(1)}, bf16[32,512]{1,0:T(8,128)(2,1)S(1)}, bf16[32,512]{1,0:T(8,128)(2,1)S(1)}, bf16[32,512]{1,0:T(8,128)(2,1)S(1)}) custom-call(bf16[16,72,128]{2,1,0:T(8,128)(2,1)S(1)} %all-to-all-done.blocks_ref, f32[1,2]{1,0:T(1,128)S(1)} %copy-done.3, f32[1,2]{1,0:T(1,128)S(1)} %collective-permute-done.1.pair_ref, ...), custom_call_target="tpu_custom_call" | custom-call | tf_op jit(solution)/shard_map/grid/pallas_call | solution.py:326
  31.4 1.5 %collective-permute-start.2 = (bf16[32,512]{1,0:T(8,128)(2,1)S(1)}, bf16[32,512]{1,0:T(8,128)(2,1)S(1)}, u32[]{:S(2)}, u32[]{:S(2)}) collective-permute-start(bf16[32,512]{1,0:T(8,128)(2,1)S(1)} %get-tuple-element.14), channel_id=1, source_target_pairs={{0,128},{64,192},{128,0},{192,64},{1,129},{65,193},{129,1},{193,65... | collective-permute-start | bytes 98312 | tf_op jit(solution)/shard_map/ppermute | solution.py:380
  33.0 2.3 %collective-permute-start.3 = (bf16[32,512]{1,0:T(8,128)(2,1)S(1)}, bf16[32,512]{1,0:T(8,128)(2,1)S(1)}, u32[]{:S(2)}, u32[]{:S(2)}) collective-permute-start(bf16[32,512]{1,0:T(8,128)(2,1)S(1)} %get-tuple-element.15), channel_id=1, source_target_pairs={{0,192},{64,128},{128,64},{192,0},{1,193},{65,129},{129,65},{193,1... | collective-permute-start | bytes 98312 | tf_op jit(solution)/shard_map/ppermute | solution.py:380
  35.2 0.0 collective-permute-start.4
  35.2 0.0 collective-permute-done.2.p1
  35.3 1.9 %collective-permute-done.3.p2 = bf16[32,512]{1,0:T(8,128)(2,1)S(1)} collective-permute-done((bf16[32,512]{1,0:T(8,128)(2,1)S(1)}, bf16[32,512]{1,0:T(8,128)(2,1)S(1)}, u32[]{:S(2)}, u32[]{:S(2)}) %collective-permute-start.3) | collective-permute-done | bytes 32800 | tf_op jit(solution)/shard_map/ppermute | solution.py:380
  37.2 0.0 collective-permute-done.4.p3
  37.2 0.0 copy-done.4
  37.2 0.7 %blend.1 = f32[3,1,4096]{2,1,0:T(1,128)} custom-call(f32[32,512]{1,0:T(8,128)S(1)} %get-tuple-element.13.p0, bf16[32,512]{1,0:T(8,128)(2,1)S(1)} %collective-permute-done.2.p1, bf16[32,512]{1,0:T(8,128)(2,1)S(1)} %collective-permute-done.3.p2, bf16[32,512]{1,0:T(8,128)(2,1)S(1)} %collective-permute-done.4.p3, s32[1,1,256]{2,1,0:T(1,128)S(1)} %copy-done.4), custom_call_target="tpu_custom_call" | custom-call | tf_op jit(solution)/shard_map/blend/pallas_call | solution.py:381
  (2 shorter events, 0.0 us)
Async XLA Ops:
  1.1 8.5 %collective-permute-start = (bf16[72,128]{1,0:T(8,128)(2,1)S(1)}, bf16[72,128]{1,0:T(8,128)(2,1)S(1)}, u32[]{:S(2)}, u32[]{:S(2)}) collective-permute-start(bf16[72,128]{1,0:T(8,128)(2,1)S(1)} %pack.1), channel_id=1, source_target_pairs={{192,0},{193,1},{194,2},{195,3},{132,4},{133,5},{134,6},{135,7},{2... | collective-permute-start | bytes 55304 | tf_op jit(solution)/shard_map/ppermute | solution.py:362
  10.3 6.9 %copy-start.3 = (f32[1,2]{1,0:T(1,128)S(1)}, f32[1,2]{1,0:T(1,128)}, u32[]{:S(2)}) copy-start(f32[1,2]{1,0:T(1,128)} %own_ref.1) | copy-start | bytes 28
  10.3 14.8 %copy-start = (bf16[96,192]{1,0:T(8,128)(2,1)S(1)}, bf16[96,192]{1,0:T(8,128)(2,1)}, u32[]{:S(2)}) copy-start(bf16[96,192]{1,0:T(8,128)(2,1)} %constant.10.clone.high_ref) | copy-start | bytes 110596
  10.3 14.8 %copy-start.1 = (bf16[96,192]{1,0:T(8,128)(2,1)S(1)}, bf16[96,192]{1,0:T(8,128)(2,1)}, u32[]{:S(2)}) copy-start(bf16[96,192]{1,0:T(8,128)(2,1)} %constant.11.clone.low_ref) | copy-start | bytes 110596
  10.3 14.8 %copy-start.2 = (f32[16,512]{1,0:T(8,128)S(1)}, f32[16,512]{1,0:T(8,128)}, u32[]{:S(2)}) copy-start(f32[16,512]{1,0:T(8,128)} %constant.9.clone.twiddle_ref) | copy-start | bytes 98308
  10.4 14.8 %all-to-all-start = ((bf16[16,72,128]{2,1,0:T(8,128)(2,1)}), bf16[16,72,128]{2,1,0:T(8,128)(2,1)S(1)}, u32[]{:S(2)}, u32[]{:S(2)}) async-start(bf16[16,72,128]{2,1,0:T(8,128)(2,1)} %spread.1), calls=%async_computation | async-start | bytes 589824 | tf_op jit(solution)/shard_map/all_to_all | solution.py:366
  17.3 1.9 %collective-permute-start.1 = (f32[1,2]{1,0:T(1,128)S(1)}, f32[1,2]{1,0:T(1,128)S(1)}, u32[]{:S(2)}, u32[]{:S(2)}) collective-permute-start(f32[1,2]{1,0:T(1,128)S(1)} %copy-done.3), channel_id=1, source_target_pairs={{0,64},{64,0},{128,192},{192,128},{1,65},{65,1},{129,193},{193,129... | collective-permute-start | bytes 32 | tf_op jit(solution)/shard_map/ppermute | solution.py:364
  31.4 3.8 %collective-permute-start.2 = (bf16[32,512]{1,0:T(8,128)(2,1)S(1)}, bf16[32,512]{1,0:T(8,128)(2,1)S(1)}, u32[]{:S(2)}, u32[]{:S(2)}) collective-permute-start(bf16[32,512]{1,0:T(8,128)(2,1)S(1)} %get-tuple-element.14), channel_id=1, source_target_pairs={{0,128},{64,192},{128,0},{192,64},{1,129},{65,193},{129,1},{193,65... | collective-permute-start | bytes 98312 | tf_op jit(solution)/shard_map/ppermute | solution.py:380
  33.0 4.2 %collective-permute-start.3 = (bf16[32,512]{1,0:T(8,128)(2,1)S(1)}, bf16[32,512]{1,0:T(8,128)(2,1)S(1)}, u32[]{:S(2)}, u32[]{:S(2)}) collective-permute-start(bf16[32,512]{1,0:T(8,128)(2,1)S(1)} %get-tuple-element.15), channel_id=1, source_target_pairs={{0,192},{64,128},{128,64},{192,0},{1,193},{65,129},{129,65},{193,1... | collective-permute-start | bytes 98312 | tf_op jit(solution)/shard_map/ppermute | solution.py:380
  35.2 1.9 %copy-start.4 = (s32[1,1,256]{2,1,0:T(1,128)S(1)}, s32[1,1,256]{2,1,0:T(1,128)}, u32[]{:S(2)}) copy-start(s32[1,1,256]{2,1,0:T(1,128)} %mask_ref.1) | copy-start | bytes 3076
  35.2 1.9 %collective-permute-start.4 = (bf16[32,512]{1,0:T(8,128)(2,1)S(1)}, bf16[32,512]{1,0:T(8,128)(2,1)S(1)}, u32[]{:S(2)}, u32[]{:S(2)}) collective-permute-start(bf16[32,512]{1,0:T(8,128)(2,1)S(1)} %get-tuple-element.16), channel_id=1, source_target_pairs={{0,64},{64,0},{128,192},{192,128},{1,65},{65,1},{129,193},{193,129... | collective-permute-start | bytes 98312 | tf_op jit(solution)/shard_map/ppermute | solution.py:380

commit v7 on v6

--- a/solution.py
+++ b/solution.py
@@ -28,7 +28,8 @@
 XB = GRID // FINE
 VALS = FACETS * TERMS
 STEP = 2
-CHUNK = 32
+LANES = 128
+CHUNK = 104
 
 COS = (0.99999999, -19.73920447, 64.93911593, -85.45011343, 60.16742979, -25.96688461, 6.52770596)
 SIN = (6.28318491, -41.3415883, 81.59991362, -76.6141403, 41.34136538, -12.46881862)
@@ -90,7 +91,7 @@
 
 
 def pack_kernel(
-    vis_hbm, uv_hbm, cells_hbm, centre_hbm, out_ref, vis_ref, uv_ref, cells_ref, centre_ref, sems
+    vis_hbm, uv_hbm, cells_hbm, centre_hbm, out_ref, copy_ref, vis_ref, uv_ref, cells_ref, centre_ref, sems
 ):
     pairs = ((vis_hbm, vis_ref), (uv_hbm, uv_ref), (cells_hbm, cells_ref), (centre_hbm, centre_ref))
     copies = [pltpu.make_async_copy(a, b, sems.at[i]) for i, (a, b) in enumerate(pairs)]
@@ -130,11 +131,7 @@
     for i, piece in enumerate(pieces(cen)):
         whole = jnp.where(lane // 2 == 3 + i, piece, whole)
     out_ref[64:72] = whole.astype(jnp.bfloat16)
-
-
-def spread_kernel(block_ref, out_ref):
-    for i in range(BLOCKS):
-        out_ref[i] = block_ref[...]
+    copy_ref[...] = centre_ref[...]
 
 
 def grid_kernel(
@@ -271,11 +268,17 @@
         spot = (2, 3, 1, 0)[s]
         before = ((own ^ s) + FACETS - 1) % FACETS ^ own
         before = jnp.where(before < 2, before + 2, 3 - before)
-        out[0:size] = image_ref[spot * size : (spot + 1) * size].astype(out.dtype)
+        mine = image_ref[spot * size : (spot + 1) * size]
         prior = image_ref[pl.ds(pl.multiple_of(before * size, 8), size), :]
-        strips = [prior[term * FINE + FINE - 1 : term * FINE + FINE] for term in range(TERMS)]
-        strips = jnp.concatenate(strips + [jnp.zeros((CHUNK - size - TERMS, XB), jnp.float32)], 0)
-        out[size:CHUNK] = strips.astype(out.dtype)
+        for c in range(XB // LANES):
+            out[c * size : (c + 1) * size] = mine[:, c * LANES : (c + 1) * LANES].astype(out.dtype)
+        strips = [
+            prior[term * FINE + FINE - 1 : term * FINE + FINE, at : at + LANES]
+            for at in range(XB - OVER, XB, LANES)
+            for term in range(TERMS)
+        ]
+        strips = jnp.concatenate(strips + [jnp.zeros((2, LANES), jnp.float32)], 0)
+        out[CHUNK - 8 : CHUNK] = strips.astype(out.dtype)
 
 
 def blend_kernel(p0, p1, p2, p3, mask_ref, out_ref):
@@ -283,21 +286,21 @@
     image = p0[...]
     for part in (p1, p2, p3):
         image = image + part[...].astype(jnp.float32)
-    strip = image[size : size + TERMS, XB - OVER :]
     has_left = (lax.axis_index("facet") > 0).astype(jnp.float32)
     pixel = lax.broadcasted_iota(jnp.int32, (1, OVER), 1).astype(jnp.float32)
     ramp = 1.0 - (pixel + 0.5) / OVER
     weight = mask_ref[0].astype(jnp.float32) * ramp * has_left
     for term in range(TERMS):
         for xa in range(FINE):
-            line = image[term * FINE + xa : term * FINE + xa + 1]
-            if xa == 0:
-                head = line[:, :OVER]
-                head = head + weight * (strip[term : term + 1] - head)
-                out_ref[term, :, 0:OVER] = head
-                out_ref[term, :, OVER:XB] = line[:, OVER:]
-            else:
-                out_ref[term, :, xa * XB : (xa + 1) * XB] = line
+            for c in range(XB // LANES):
+                row = c * size + term * FINE + xa
+                line = image[row : row + 1]
+                if xa == 0 and c < OVER // LANES:
+                    at = CHUNK - 8 + c * TERMS + term
+                    strip = image[at : at + 1]
+                    line = line + weight[:, c * LANES : (c + 1) * LANES] * (strip - line)
+                at = xa * XB + c * LANES
+                out_ref[term, :, at : at + LANES] = line
 
 
 def swap_pairs():
@@ -319,7 +322,7 @@
     first, twiddle, second = tables()
     first = pltpu.with_memory_space_constraint(first, pltpu.HBM)
     chunk = [
-        jax.ShapeDtypeStruct((CHUNK, XB), jnp.bfloat16 if s else jnp.float32)
+        jax.ShapeDtypeStruct((CHUNK, LANES), jnp.bfloat16 if s else jnp.float32)
         for s in range(FACETS)
     ]
     span = 2 * VALS * FINE
@@ -349,32 +352,28 @@
     hbm = pl.BlockSpec(memory_space=pltpu.HBM)
     given = (visibilities, uv_coords.T, cells, centres)
     given = [pltpu.with_memory_space_constraint(one, pltpu.HBM) for one in given]
-    packed = pl.pallas_call(
+    packed, centre = pl.pallas_call(
         pack_kernel,
-        out_shape=jax.ShapeDtypeStruct((PACKED, 2 * CH), jnp.bfloat16),
+        out_shape=[
+            jax.ShapeDtypeStruct((PACKED, 2 * CH), jnp.bfloat16),
+            jax.ShapeDtypeStruct((1, 2), jnp.float32),
+        ],
         in_specs=[hbm] * 4,
-        out_specs=vmem,
+        out_specs=[vmem] * 2,
         scratch_shapes=[pltpu.VMEM(one.shape, one.dtype) for one in given]
         + [pltpu.SemaphoreType.DMA((4,))],
         compiler_params=pltpu.CompilerParams(vmem_limit_bytes=2 << 20),
         name="pack",
     )(*given)
+    pair = lax.ppermute(centre, "facet", [(i, i ^ 1) for i in range(FACETS)])
     packed = lax.ppermute(packed, ("facet", "vis"), swap_pairs())
-    packed, centre = lax.optimization_barrier((packed, centres))
-    pair = lax.ppermute(centre, "facet", [(i, i ^ 1) for i in range(FACETS)])
+    packed, pair = lax.optimization_barrier((packed, pair))
     planes = [[z * BLOCKS + i for i in range(BLOCKS)] for z in range(SIDE)]
     blocks = lax.all_to_all(
-        pl.pallas_call(
-            spread_kernel,
-            out_shape=jax.ShapeDtypeStruct((BLOCKS,) + packed.shape, packed.dtype),
-            in_specs=[vmem],
-            out_specs=vmem,
-            compiler_params=pltpu.CompilerParams(vmem_limit_bytes=2 << 20),
-            name="spread",
-        )(packed),
+        jnp.broadcast_to(packed[None], (BLOCKS,) + packed.shape),
         "vis", 0, 0, axis_index_groups=planes,
     )
-    parts = partial_images(blocks, centres, pair)
+    parts = partial_images(blocks, centre, pair)
     got = [parts[0]]
     for s in (2, 3, 1):
         got.append(lax.ppermute(parts[s], "facet", [(i, i ^ s) for i in range(FACETS)]))

time: 38.1 us -> 37.2 us (0.976)
  blocking collectives: 0 us -> 14.8 us
  starting transfers between devices: 18.9 us -> 11.3 us
  waiting for transfers between devices: 10.2 us -> 2.64 us
  Pallas kernels: 8.77 us -> 8.01 us
    all_to_all x0 -> x1, blocking collectives: none -> 14.8 us  [per_device(): lax.all_to_all(jnp.broadcast_to(packed[None], (BLOCKS,) + packed.shape),...]
    all_to_all x1 -> x0, starting transfers between devices: 6.9 us -> none  [per_device(): lax.all_to_all(pl.pallas_call(spread_kernel, out_shape=jax.ShapeDtypeStru...]
    all_to_all x1 -> x0, waiting for transfers between devices: 5.96 us -> none  [per_device(): lax.all_to_all(pl.pallas_call(spread_kernel, out_shape=jax.ShapeDtypeStru...]
    ppermute x1, waiting for transfers between devices: 1.45 us -> 0.01 us  [per_device(): packed = lax.ppermute(packed, ('facet', 'vis'), swap_pairs())]
    pallas_call x2 -> x1, Pallas kernels: 1.84 us -> 1.08 us  [per_device(): pl.pallas_call(pack_kernel, out_shape=[jax.ShapeDtypeStruct((PACKED, 2 *...]
    ppermute x1, starting transfers between devices: 1.11 us -> 0.72 us  [per_device(): pair = lax.ppermute(centre, 'facet', [(i, i ^ 1) for i in range(FACETS)])]
  transfers between devices with their start and end apart: 6 -> 5, of which waited for: 4 -> 2; matrix products, arithmetic and copies ran while one was open for 0% -> 0% of each run, Pallas kernels for 0% -> 0%
where the time goes in v7:
time: 37.2 us; the launch traced here: 36.9 us
  blocking collectives  14.8 us (40%)
  starting transfers between devices  11.3 us (30%)
  Pallas kernels  8.01 us (22%)
  waiting for transfers between devices  2.64 us (7%)
    all_to_all x1, blocking collectives, per_device(): lax.all_to_all(jnp.broadcast_to(packed[None], (BLOCKS,) + packed.shape),...  14.8 us
    ppermute x1, starting transfers between devices, per_device(): packed = lax.ppermute(packed, ('facet', 'vis'), swap_pairs())  7.04 us
    pallas_call x1, Pallas kernels, partial_images(): pl.pallas_call(grid_kernel, out_shape=chunk, in_specs=[vmem] * 3 + [hbm]...  6.27 us
    ppermute x3, starting transfers between devices, per_device(): lax.ppermute(parts[s], 'facet', [(i, i ^ s) for i in range(FACETS)])  3.55 us
    ppermute x3, waiting for transfers between devices, per_device(): lax.ppermute(parts[s], 'facet', [(i, i ^ s) for i in range(FACETS)])  1.82 us
    pallas_call x1, Pallas kernels, per_device(): pl.pallas_call(pack_kernel, out_shape=[jax.ShapeDtypeStruct((PACKED, 2 *...  1.08 us
    ppermute x1, waiting for transfers between devices, per_device(): pair = lax.ppermute(centre, 'facet', [(i, i ^ 1) for i in range(FACETS)])  0.82 us
  transfers between devices with their start and end apart: 5, of which 2 were waited for; matrix products, arithmetic and copies ran while one was open for 0% of the time, Pallas kernels for 0%

profile of v7, /device:TPU:1, one launch (start us, length us, event | category | flops | bytes accessed | tf_op | source)
XLA Modules:
  0.0 36.9 jit_solution(1975199747972485798)
XLA Ops:
  0.0 1.1 %pack.1 = (bf16[72,128]{1,0:T(8,128)(2,1)S(1)}, f32[1,2]{1,0:T(1,128)S(1)}) custom-call(bf16[32,128]{1,0:T(8,128)(2,1)} %vis_hbm.1, f32[2,32]{1,0:T(2,128)} %bitcast.1, s32[2,32,64]{2,1,0:T(8,128)} %cells_hbm.1, f32[1,2]{1,0:T(1,128)} %centre_hbm.1), custom_call_target="tpu_custom_call" | custom-call | tf_op jit(solution)/shard_map/pack/pallas_call | solution.py:355
  1.1 7.0 %collective-permute-start = (bf16[72,128]{1,0:T(8,128)(2,1)S(1)}, bf16[72,128]{1,0:T(8,128)(2,1)S(1)}, u32[]{:S(2)}, u32[]{:S(2)}) collective-permute-start(bf16[72,128]{1,0:T(8,128)(2,1)S(1)} %get-tuple-element.13), channel_id=1, source_target_pairs={{192,0},{193,1},{194,2},{195,3},{132,4},{133,5},{134,6},{135,7},{2... | collective-permute-start | bytes 55304 | tf_op jit(solution)/shard_map/ppermute | solution.py:369
  8.1 0.7 %collective-permute-start.1 = (f32[1,2]{1,0:T(1,128)S(1)}, f32[1,2]{1,0:T(1,128)S(1)}, u32[]{:S(2)}, u32[]{:S(2)}) collective-permute-start(f32[1,2]{1,0:T(1,128)S(1)} %get-tuple-element.14.own_ref), channel_id=1, source_target_pairs={{0,64},{64,0},{128,192},{192,128},{1,65},{65,1},{129,193},{193,129... | collective-permute-start | bytes 32 | tf_op jit(solution)/shard_map/ppermute | solution.py:368
  8.9 0.8 %collective-permute-done.1.pair_ref = f32[1,2]{1,0:T(1,128)S(1)} collective-permute-done((f32[1,2]{1,0:T(1,128)S(1)}, f32[1,2]{1,0:T(1,128)S(1)}, u32[]{:S(2)}, u32[]{:S(2)}) %collective-permute-start.1) | collective-permute-done | bytes 40 | tf_op jit(solution)/shard_map/ppermute | solution.py:368
  9.7 0.0 collective-permute-done
  9.7 0.0 copy-start
  9.7 0.0 copy-start.1
  9.7 0.0 copy-start.2
  9.8 14.8 %all_to_all.5.blocks_ref = bf16[16,72,128]{2,1,0:T(8,128)(2,1)S(1)} all-to-all(bf16[16,72,128]{2,1,0:T(8,128)(2,1)S(1)} %broadcast_in_dim.2), channel_id=1, replica_groups={{0,1,2,3,4,5,6,7,8,9,10,11,12,13,14,15},{16,17,18,19,20,21,22,23,24,25,..., dimensions={0} | all-to-all | bytes 589824 | tf_op jit(solution)/shard_map/all_to_all | solution.py:372
  24.6 0.0 copy-done
  24.6 0.0 copy-done.1
  24.6 0.0 copy-done.2
  24.6 6.3 %grid.1 = (f32[104,128]{1,0:T(8,128)S(1)}, bf16[104,128]{1,0:T(8,128)(2,1)S(1)}, bf16[104,128]{1,0:T(8,128)(2,1)S(1)}, bf16[104,128]{1,0:T(8,128)(2,1)S(1)}) custom-call(bf16[16,72,128]{2,1,0:T(8,128)(2,1)S(1)} %all_to_all.5.blocks_ref, f32[1,2]{1,0:T(1,128)S(1)} %get-tuple-element.14.own_ref, f32[1,2]{1,0:T(1,128)S(1)} %collective-permute-done.1.pair_ref, ...), custom_call_target="tpu_custom_call" | custom-call | tf_op jit(solution)/shard_map/grid/pallas_call | solution.py:329
  30.9 1.2 %collective-permute-start.2 = (bf16[104,128]{1,0:T(8,128)(2,1)S(1)}, bf16[104,128]{1,0:T(8,128)(2,1)S(1)}, u32[]{:S(2)}, u32[]{:S(2)}) collective-permute-start(bf16[104,128]{1,0:T(8,128)(2,1)S(1)} %get-tuple-element.18), channel_id=1, source_target_pairs={{0,128},{64,192},{128,0},{192,64},{1,129},{65,193},{129,1},{193,65... | collective-permute-start | bytes 79880 | tf_op jit(solution)/shard_map/ppermute | solution.py:379
  32.1 2.4 %collective-permute-start.3 = (bf16[104,128]{1,0:T(8,128)(2,1)S(1)}, bf16[104,128]{1,0:T(8,128)(2,1)S(1)}, u32[]{:S(2)}, u32[]{:S(2)}) collective-permute-start(bf16[104,128]{1,0:T(8,128)(2,1)S(1)} %get-tuple-element.19), channel_id=1, source_target_pairs={{0,192},{64,128},{128,64},{192,0},{1,193},{65,129},{129,65},{193,1... | collective-permute-start | bytes 79880 | tf_op jit(solution)/shard_map/ppermute | solution.py:379
  34.4 0.0 copy-start.3
  34.4 0.0 collective-permute-start.4
  34.4 0.0 collective-permute-done.2.p1
  34.4 1.8 %collective-permute-done.3.p2 = bf16[104,128]{1,0:T(8,128)(2,1)S(1)} collective-permute-done((bf16[104,128]{1,0:T(8,128)(2,1)S(1)}, bf16[104,128]{1,0:T(8,128)(2,1)S(1)}, u32[]{:S(2)}, u32[]{:S(2)}) %collective-permute-start.3) | collective-permute-done | bytes 26656 | tf_op jit(solution)/shard_map/ppermute | solution.py:379
  36.3 0.0 collective-permute-done.4.p3
  36.3 0.0 copy-done.3
  36.3 0.7 %blend.1 = f32[3,1,4096]{2,1,0:T(1,128)} custom-call(f32[104,128]{1,0:T(8,128)S(1)} %get-tuple-element.17.p0, bf16[104,128]{1,0:T(8,128)(2,1)S(1)} %collective-permute-done.2.p1, bf16[104,128]{1,0:T(8,128)(2,1)S(1)} %collective-permute-done.3.p2, bf16[104,128]{1,0:T(8,128)(2,1)S(1)} %collective-permute-done.4.p3, s32[1,1,256]{2,1,0:T(1,128)S(1)} %copy-done.3), custom_call_target="tpu_custom_call" | custom-call | tf_op jit(solution)/shard_map/blend/pallas_call | solution.py:380
  (1 shorter events, 0.0 us)
Async XLA Ops:
  1.1 8.6 %collective-permute-start = (bf16[72,128]{1,0:T(8,128)(2,1)S(1)}, bf16[72,128]{1,0:T(8,128)(2,1)S(1)}, u32[]{:S(2)}, u32[]{:S(2)}) collective-permute-start(bf16[72,128]{1,0:T(8,128)(2,1)S(1)} %get-tuple-element.13), channel_id=1, source_target_pairs={{192,0},{193,1},{194,2},{195,3},{132,4},{133,5},{134,6},{135,7},{2... | collective-permute-start | bytes 55304 | tf_op jit(solution)/shard_map/ppermute | solution.py:369
  8.1 1.5 %collective-permute-start.1 = (f32[1,2]{1,0:T(1,128)S(1)}, f32[1,2]{1,0:T(1,128)S(1)}, u32[]{:S(2)}, u32[]{:S(2)}) collective-permute-start(f32[1,2]{1,0:T(1,128)S(1)} %get-tuple-element.14.own_ref), channel_id=1, source_target_pairs={{0,64},{64,0},{128,192},{192,128},{1,65},{65,1},{129,193},{193,129... | collective-permute-start | bytes 32 | tf_op jit(solution)/shard_map/ppermute | solution.py:368
  9.7 14.9 %copy-start = (bf16[96,192]{1,0:T(8,128)(2,1)S(1)}, bf16[96,192]{1,0:T(8,128)(2,1)}, u32[]{:S(2)}) copy-start(bf16[96,192]{1,0:T(8,128)(2,1)} %constant.11.clone.low_ref) | copy-start | bytes 110596
  9.7 14.9 %copy-start.1 = (bf16[96,192]{1,0:T(8,128)(2,1)S(1)}, bf16[96,192]{1,0:T(8,128)(2,1)}, u32[]{:S(2)}) copy-start(bf16[96,192]{1,0:T(8,128)(2,1)} %constant.10.clone.high_ref) | copy-start | bytes 110596
  9.7 14.9 %copy-start.2 = (f32[16,512]{1,0:T(8,128)S(1)}, f32[16,512]{1,0:T(8,128)}, u32[]{:S(2)}) copy-start(f32[16,512]{1,0:T(8,128)} %constant.9.clone.twiddle_ref) | copy-start | bytes 98308
  30.9 3.6 %collective-permute-start.2 = (bf16[104,128]{1,0:T(8,128)(2,1)S(1)}, bf16[104,128]{1,0:T(8,128)(2,1)S(1)}, u32[]{:S(2)}, u32[]{:S(2)}) collective-permute-start(bf16[104,128]{1,0:T(8,128)(2,1)S(1)} %get-tuple-element.18), channel_id=1, source_target_pairs={{0,128},{64,192},{128,0},{192,64},{1,129},{65,193},{129,1},{193,65... | collective-permute-start | bytes 79880 | tf_op jit(solution)/shard_map/ppermute | solution.py:379
  32.1 4.2 %collective-permute-start.3 = (bf16[104,128]{1,0:T(8,128)(2,1)S(1)}, bf16[104,128]{1,0:T(8,128)(2,1)S(1)}, u32[]{:S(2)}, u32[]{:S(2)}) collective-permute-start(bf16[104,128]{1,0:T(8,128)(2,1)S(1)} %get-tuple-element.19), channel_id=1, source_target_pairs={{0,192},{64,128},{128,64},{192,0},{1,193},{65,129},{129,65},{193,1... | collective-permute-start | bytes 79880 | tf_op jit(solution)/shard_map/ppermute | solution.py:379
  34.4 1.8 %copy-start.3 = (s32[1,1,256]{2,1,0:T(1,128)S(1)}, s32[1,1,256]{2,1,0:T(1,128)}, u32[]{:S(2)}) copy-start(s32[1,1,256]{2,1,0:T(1,128)} %mask_ref.1) | copy-start | bytes 3076
  34.4 1.8 %collective-permute-start.4 = (bf16[104,128]{1,0:T(8,128)(2,1)S(1)}, bf16[104,128]{1,0:T(8,128)(2,1)S(1)}, u32[]{:S(2)}, u32[]{:S(2)}) collective-permute-start(bf16[104,128]{1,0:T(8,128)(2,1)S(1)} %get-tuple-element.20), channel_id=1, source_target_pairs={{0,64},{64,0},{128,192},{192,128},{1,65},{65,1},{129,193},{193,129... | collective-permute-start | bytes 79880 | tf_op jit(solution)/shard_map/ppermute | solution.py:379

commit v8 on v7

--- a/solution.py
+++ b/solution.py
@@ -95,11 +95,36 @@
 ):
     pairs = ((vis_hbm, vis_ref), (uv_hbm, uv_ref), (cells_hbm, cells_ref), (centre_hbm, centre_ref))
     copies = [pltpu.make_async_copy(a, b, sems.at[i]) for i, (a, b) in enumerate(pairs)]
-    for copy in copies:
-        copy.start()
-    for copy in copies:
-        copy.wait()
+    for i in (1, 3, 0, 2):
+        copies[i].start()
+    copies[1].wait()
+    copies[3].wait()
     lane = lax.broadcasted_iota(jnp.int32, (HALF, 2 * CH), 1)
+
+    def pieces(value):
+        high = value.astype(jnp.bfloat16).astype(jnp.float32)
+        rest = value - high
+        mid = rest.astype(jnp.bfloat16).astype(jnp.float32)
+        return high, mid, rest - mid
+
+    split = jnp.concatenate(pieces(uv_ref[...]), 0).astype(jnp.bfloat16)
+    spots = lax.broadcasted_iota(jnp.int32, (6, 2 * CH), 0)
+    spots = spots == lax.broadcasted_iota(jnp.int32, (6, 2 * CH), 1)
+    columns = lax.dot_general(
+        split, spots.astype(jnp.float32).astype(jnp.bfloat16), (((0,), (0,)), ((), ())),
+        preferred_element_type=jnp.float32,
+    )
+    whole = columns[0:8]
+    for i in (1, 2, 3):
+        whole = whole + pltpu.roll(columns[8 * i : 8 * i + 8], 32 * i, 1)
+    cen = jnp.where(lane[0:8] % 2 == 0, centre_ref[0:1, 0:1], centre_ref[0:1, 1:2])
+    for i, piece in enumerate(pieces(cen)):
+        whole = jnp.where(lane[0:8] // 2 == 3 + i, piece, whole)
+    out_ref[64:72] = whole.astype(jnp.bfloat16)
+    copy_ref[...] = centre_ref[...]
+
+    copies[0].wait()
+    copies[2].wait()
     left = lane < CH
     vis = vis_ref[...].astype(jnp.float32)
     top, low = vis[:HALF], vis[HALF:]
@@ -109,29 +134,6 @@
         cells = cells_ref[which]
         both = jnp.concatenate([cells[:HALF], cells[HALF:]], 1)
         out_ref[32 + 16 * which : 48 + 16 * which] = coded(both)
-
-    def pieces(value):
-        high = value.astype(jnp.bfloat16).astype(jnp.float32)
-        rest = value - high
-        mid = rest.astype(jnp.bfloat16).astype(jnp.float32)
-        return high, mid, rest - mid
-
-    split = jnp.concatenate(pieces(uv_ref[...]), 0).astype(jnp.bfloat16)
-    spots = lax.broadcasted_iota(jnp.int32, (6, 2 * CH), 0)
-    spots = spots == lax.broadcasted_iota(jnp.int32, (6, 2 * CH), 1)
-    columns = lax.dot_general(
-        split, spots.astype(jnp.float32).astype(jnp.bfloat16), (((0,), (0,)), ((), ())),
-        preferred_element_type=jnp.float32,
-    )
-    whole = columns[0:8]
-    for i in (1, 2, 3):
-        whole = whole + pltpu.roll(columns[8 * i : 8 * i + 8], 32 * i, 1)
-    lane = lane[0:8]
-    cen = jnp.where(lane % 2 == 0, centre_ref[0:1, 0:1], centre_ref[0:1, 1:2])
-    for i, piece in enumerate(pieces(cen)):
-        whole = jnp.where(lane // 2 == 3 + i, piece, whole)
-    out_ref[64:72] = whole.astype(jnp.bfloat16)
-    copy_ref[...] = centre_ref[...]
 
 
 def grid_kernel(
@@ -375,7 +377,7 @@
     )
     parts = partial_images(blocks, centre, pair)
     got = [parts[0]]
-    for s in (2, 3, 1):
+    for s in (3, 2, 1):
         got.append(lax.ppermute(parts[s], "facet", [(i, i ^ s) for i in range(FACETS)]))
     return pl.pallas_call(
         blend_kernel,

time: 37.2 us -> 36.5 us (0.981)
  transfers between devices with their start and end apart: 5 -> 5, of which waited for: 2 -> 3; matrix products, arithmetic and copies ran while one was open for 0% -> 0% of each run, Pallas kernels for 0% -> 0%
where the time goes in v8:
time: 36.5 us; the launch traced here: 36.3 us
  blocking collectives  14.8 us (41%)
  starting transfers between devices  11 us (30%)
  Pallas kernels  7.99 us (22%)
  waiting for transfers between devices  2.35 us (6%)
    all_to_all x1, blocking collectives, per_device(): lax.all_to_all(jnp.broadcast_to(packed[None], (BLOCKS,) + packed.shape),...  14.8 us
    ppermute x1, starting transfers between devices, per_device(): packed = lax.ppermute(packed, ('facet', 'vis'), swap_pairs())  7.04 us
    pallas_call x1, Pallas kernels, partial_images(): pl.pallas_call(grid_kernel, out_shape=chunk, in_specs=[vmem] * 3 + [hbm]...  6.28 us
    ppermute x3, starting transfers between devices, per_device(): lax.ppermute(parts[s], 'facet', [(i, i ^ s) for i in range(FACETS)])  3.25 us
    ppermute x3, waiting for transfers between devices, per_device(): lax.ppermute(parts[s], 'facet', [(i, i ^ s) for i in range(FACETS)])  1.52 us
    pallas_call x1, Pallas kernels, per_device(): pl.pallas_call(pack_kernel, out_shape=[jax.ShapeDtypeStruct((PACKED, 2 *...  1.05 us
    ppermute x1, waiting for transfers between devices, per_device(): pair = lax.ppermute(centre, 'facet', [(i, i ^ 1) for i in range(FACETS)])  0.82 us
  transfers between devices with their start and end apart: 5, of which 3 were waited for; matrix products, arithmetic and copies ran while one was open for 0% of the time, Pallas kernels for 0%

profile of v8, /device:TPU:1, one launch (start us, length us, event | category | flops | bytes accessed | tf_op | source)
XLA Modules:
  0.0 36.3 jit_solution(507568744856872553)
XLA Ops:
  0.0 1.0 %pack.1 = (bf16[72,128]{1,0:T(8,128)(2,1)S(1)}, f32[1,2]{1,0:T(1,128)S(1)}) custom-call(bf16[32,128]{1,0:T(8,128)(2,1)} %vis_hbm.1, f32[2,32]{1,0:T(2,128)} %bitcast.1, s32[2,32,64]{2,1,0:T(8,128)} %cells_hbm.1, f32[1,2]{1,0:T(1,128)} %centre_hbm.1), custom_call_target="tpu_custom_call" | custom-call | tf_op jit(solution)/shard_map/pack/pallas_call | solution.py:357
  1.1 7.0 %collective-permute-start = (bf16[72,128]{1,0:T(8,128)(2,1)S(1)}, bf16[72,128]{1,0:T(8,128)(2,1)S(1)}, u32[]{:S(2)}, u32[]{:S(2)}) collective-permute-start(bf16[72,128]{1,0:T(8,128)(2,1)S(1)} %get-tuple-element.13), channel_id=1, source_target_pairs={{192,0},{193,1},{194,2},{195,3},{132,4},{133,5},{134,6},{135,7},{2... | collective-permute-start | bytes 55304 | tf_op jit(solution)/shard_map/ppermute | solution.py:371
  8.1 0.7 %collective-permute-start.1 = (f32[1,2]{1,0:T(1,128)S(1)}, f32[1,2]{1,0:T(1,128)S(1)}, u32[]{:S(2)}, u32[]{:S(2)}) collective-permute-start(f32[1,2]{1,0:T(1,128)S(1)} %get-tuple-element.14.own_ref), channel_id=1, source_target_pairs={{0,64},{64,0},{128,192},{192,128},{1,65},{65,1},{129,193},{193,129... | collective-permute-start | bytes 32 | tf_op jit(solution)/shard_map/ppermute | solution.py:370
  8.8 0.8 %collective-permute-done.1.pair_ref = f32[1,2]{1,0:T(1,128)S(1)} collective-permute-done((f32[1,2]{1,0:T(1,128)S(1)}, f32[1,2]{1,0:T(1,128)S(1)}, u32[]{:S(2)}, u32[]{:S(2)}) %collective-permute-start.1) | collective-permute-done | bytes 40 | tf_op jit(solution)/shard_map/ppermute | solution.py:370
  9.6 0.0 collective-permute-done
  9.7 0.0 copy-start
  9.7 0.0 copy-start.1
  9.7 0.0 copy-start.2
  9.7 14.8 %all_to_all.5.blocks_ref = bf16[16,72,128]{2,1,0:T(8,128)(2,1)S(1)} all-to-all(bf16[16,72,128]{2,1,0:T(8,128)(2,1)S(1)} %broadcast_in_dim.2), channel_id=1, replica_groups={{0,1,2,3,4,5,6,7,8,9,10,11,12,13,14,15},{16,17,18,19,20,21,22,23,24,25,..., dimensions={0} | all-to-all | bytes 589824 | tf_op jit(solution)/shard_map/all_to_all | solution.py:374
  24.6 0.0 copy-done
  24.6 0.0 copy-done.1
  24.6 0.0 copy-done.2
  24.6 6.3 %grid.1 = (f32[104,128]{1,0:T(8,128)S(1)}, bf16[104,128]{1,0:T(8,128)(2,1)S(1)}, bf16[104,128]{1,0:T(8,128)(2,1)S(1)}, bf16[104,128]{1,0:T(8,128)(2,1)S(1)}) custom-call(bf16[16,72,128]{2,1,0:T(8,128)(2,1)S(1)} %all_to_all.5.blocks_ref, f32[1,2]{1,0:T(1,128)S(1)} %get-tuple-element.14.own_ref, f32[1,2]{1,0:T(1,128)S(1)} %collective-permute-done.1.pair_ref, ...), custom_call_target="tpu_custom_call" | custom-call | tf_op jit(solution)/shard_map/grid/pallas_call | solution.py:331
  30.9 0.1 collective-permute-start.2
  31.0 3.2 %collective-permute-start.3 = (bf16[104,128]{1,0:T(8,128)(2,1)S(1)}, bf16[104,128]{1,0:T(8,128)(2,1)S(1)}, u32[]{:S(2)}, u32[]{:S(2)}) collective-permute-start(bf16[104,128]{1,0:T(8,128)(2,1)S(1)} %get-tuple-element.19), channel_id=1, source_target_pairs={{0,128},{64,192},{128,0},{192,64},{1,129},{65,193},{129,1},{193,65... | collective-permute-start | bytes 79880 | tf_op jit(solution)/shard_map/ppermute | solution.py:381
  34.1 0.0 copy-start.3
  34.1 0.0 collective-permute-start.4
  34.1 0.1 collective-permute-done.2.p1
  34.2 1.4 %collective-permute-done.3.p2 = bf16[104,128]{1,0:T(8,128)(2,1)S(1)} collective-permute-done((bf16[104,128]{1,0:T(8,128)(2,1)S(1)}, bf16[104,128]{1,0:T(8,128)(2,1)S(1)}, u32[]{:S(2)}, u32[]{:S(2)}) %collective-permute-start.3) | collective-permute-done | bytes 26656 | tf_op jit(solution)/shard_map/ppermute | solution.py:381
  35.7 0.0 collective-permute-done.4.p3
  35.7 0.0 copy-done.3
  35.7 0.7 %blend.1 = f32[3,1,4096]{2,1,0:T(1,128)} custom-call(f32[104,128]{1,0:T(8,128)S(1)} %get-tuple-element.17.p0, bf16[104,128]{1,0:T(8,128)(2,1)S(1)} %collective-permute-done.2.p1, bf16[104,128]{1,0:T(8,128)(2,1)S(1)} %collective-permute-done.3.p2, bf16[104,128]{1,0:T(8,128)(2,1)S(1)} %collective-permute-done.4.p3, s32[1,1,256]{2,1,0:T(1,128)S(1)} %copy-done.3), custom_call_target="tpu_custom_call" | custom-call | tf_op jit(solution)/shard_map/blend/pallas_call | solution.py:382
  (1 shorter events, 0.0 us)
Async XLA Ops:
  1.1 8.6 %collective-permute-start = (bf16[72,128]{1,0:T(8,128)(2,1)S(1)}, bf16[72,128]{1,0:T(8,128)(2,1)S(1)}, u32[]{:S(2)}, u32[]{:S(2)}) collective-permute-start(bf16[72,128]{1,0:T(8,128)(2,1)S(1)} %get-tuple-element.13), channel_id=1, source_target_pairs={{192,0},{193,1},{194,2},{195,3},{132,4},{133,5},{134,6},{135,7},{2... | collective-permute-start | bytes 55304 | tf_op jit(solution)/shard_map/ppermute | solution.py:371
  8.1 1.5 %collective-permute-start.1 = (f32[1,2]{1,0:T(1,128)S(1)}, f32[1,2]{1,0:T(1,128)S(1)}, u32[]{:S(2)}, u32[]{:S(2)}) collective-permute-start(f32[1,2]{1,0:T(1,128)S(1)} %get-tuple-element.14.own_ref), channel_id=1, source_target_pairs={{0,64},{64,0},{128,192},{192,128},{1,65},{65,1},{129,193},{193,129... | collective-permute-start | bytes 32 | tf_op jit(solution)/shard_map/ppermute | solution.py:370
  9.7 14.9 %copy-start = (bf16[96,192]{1,0:T(8,128)(2,1)S(1)}, bf16[96,192]{1,0:T(8,128)(2,1)}, u32[]{:S(2)}) copy-start(bf16[96,192]{1,0:T(8,128)(2,1)} %constant.11.clone.low_ref) | copy-start | bytes 110596
  9.7 14.9 %copy-start.1 = (bf16[96,192]{1,0:T(8,128)(2,1)S(1)}, bf16[96,192]{1,0:T(8,128)(2,1)}, u32[]{:S(2)}) copy-start(bf16[96,192]{1,0:T(8,128)(2,1)} %constant.10.clone.high_ref) | copy-start | bytes 110596
  9.7 14.9 %copy-start.2 = (f32[16,512]{1,0:T(8,128)S(1)}, f32[16,512]{1,0:T(8,128)}, u32[]{:S(2)}) copy-start(f32[16,512]{1,0:T(8,128)} %constant.9.clone.twiddle_ref) | copy-start | bytes 98308
  30.9 3.4 %collective-permute-start.2 = (bf16[104,128]{1,0:T(8,128)(2,1)S(1)}, bf16[104,128]{1,0:T(8,128)(2,1)S(1)}, u32[]{:S(2)}, u32[]{:S(2)}) collective-permute-start(bf16[104,128]{1,0:T(8,128)(2,1)S(1)} %get-tuple-element.18), channel_id=1, source_target_pairs={{0,192},{64,128},{128,64},{192,0},{1,193},{65,129},{129,65},{193,1... | collective-permute-start | bytes 79880 | tf_op jit(solution)/shard_map/ppermute | solution.py:381
  31.0 4.7 %collective-permute-start.3 = (bf16[104,128]{1,0:T(8,128)(2,1)S(1)}, bf16[104,128]{1,0:T(8,128)(2,1)S(1)}, u32[]{:S(2)}, u32[]{:S(2)}) collective-permute-start(bf16[104,128]{1,0:T(8,128)(2,1)S(1)} %get-tuple-element.19), channel_id=1, source_target_pairs={{0,128},{64,192},{128,0},{192,64},{1,129},{65,193},{129,1},{193,65... | collective-permute-start | bytes 79880 | tf_op jit(solution)/shard_map/ppermute | solution.py:381
  34.1 1.5 %copy-start.3 = (s32[1,1,256]{2,1,0:T(1,128)S(1)}, s32[1,1,256]{2,1,0:T(1,128)}, u32[]{:S(2)}) copy-start(s32[1,1,256]{2,1,0:T(1,128)} %mask_ref.1) | copy-start | bytes 3076
  34.1 1.5 %collective-permute-start.4 = (bf16[104,128]{1,0:T(8,128)(2,1)S(1)}, bf16[104,128]{1,0:T(8,128)(2,1)S(1)}, u32[]{:S(2)}, u32[]{:S(2)}) collective-permute-start(bf16[104,128]{1,0:T(8,128)(2,1)S(1)} %get-tuple-element.20), channel_id=1, source_target_pairs={{0,64},{64,0},{128,192},{192,128},{1,65},{65,1},{129,193},{193,129... | collective-permute-start | bytes 79880 | tf_op jit(solution)/shard_map/ppermute | solution.py:381

commit v9 on v8

--- a/solution.py
+++ b/solution.py
@@ -283,7 +283,7 @@
         out[CHUNK - 8 : CHUNK] = strips.astype(out.dtype)
 
 
-def blend_kernel(p0, p1, p2, p3, mask_ref, out_ref):
+def blend_kernel(p0, p1, p2, p3, mask_ref, out_hbm, out_ref, sems):
     size = TERMS * FINE
     image = p0[...]
     for part in (p1, p2, p3):
@@ -292,6 +292,7 @@
     pixel = lax.broadcasted_iota(jnp.int32, (1, OVER), 1).astype(jnp.float32)
     ramp = 1.0 - (pixel + 0.5) / OVER
     weight = mask_ref[0].astype(jnp.float32) * ramp * has_left
+    copies = []
     for term in range(TERMS):
         for xa in range(FINE):
             for c in range(XB // LANES):
@@ -303,6 +304,10 @@
                     line = line + weight[:, c * LANES : (c + 1) * LANES] * (strip - line)
                 at = xa * XB + c * LANES
                 out_ref[term, :, at : at + LANES] = line
+        copies.append(pltpu.make_async_copy(out_ref.at[term], out_hbm.at[term], sems.at[term]))
+        copies[-1].start()
+    for copy in copies:
+        copy.wait()
 
 
 def swap_pairs():
@@ -383,7 +388,11 @@
         blend_kernel,
         out_shape=jax.ShapeDtypeStruct((TERMS, 1, GRID), jnp.float32),
         in_specs=[vmem] * 5,
-        out_specs=vmem,
+        out_specs=hbm,
+        scratch_shapes=[
+            pltpu.VMEM((TERMS, 1, GRID), jnp.float32),
+            pltpu.SemaphoreType.DMA((TERMS,)),
+        ],
         compiler_params=pltpu.CompilerParams(vmem_limit_bytes=2 << 20),
         name="blend",
     )(*got, intersection_mask)

time: 36.5 us -> 36.6 us (level)
  no operation moved by 1% of the time
where the time goes in v9:
time: 36.6 us; the launch traced here: 36.3 us
  blocking collectives  14.8 us (40%)
  starting transfers between devices  11 us (30%)
  Pallas kernels  8.01 us (22%)
  waiting for transfers between devices  2.35 us (6%)
    all_to_all x1, blocking collectives, per_device(): lax.all_to_all(jnp.broadcast_to(packed[None], (BLOCKS,) + packed.shape),...  14.8 us
    ppermute x1, starting transfers between devices, per_device(): packed = lax.ppermute(packed, ('facet', 'vis'), swap_pairs())  7.04 us
    pallas_call x1, Pallas kernels, partial_images(): pl.pallas_call(grid_kernel, out_shape=chunk, in_specs=[vmem] * 3 + [hbm]...  6.28 us
    ppermute x3, starting transfers between devices, per_device(): lax.ppermute(parts[s], 'facet', [(i, i ^ s) for i in range(FACETS)])  3.25 us
    ppermute x3, waiting for transfers between devices, per_device(): lax.ppermute(parts[s], 'facet', [(i, i ^ s) for i in range(FACETS)])  1.52 us
    pallas_call x1, Pallas kernels, per_device(): pl.pallas_call(pack_kernel, out_shape=[jax.ShapeDtypeStruct((PACKED, 2 *...  1.05 us
    ppermute x1, waiting for transfers between devices, per_device(): pair = lax.ppermute(centre, 'facet', [(i, i ^ 1) for i in range(FACETS)])  0.82 us
  transfers between devices with their start and end apart: 5, of which 3 were waited for; matrix products, arithmetic and copies ran while one was open for 0% of the time, Pallas kernels for 0%

profile of v9, /device:TPU:1, one launch (start us, length us, event | category | flops | bytes accessed | tf_op | source)
XLA Modules:
  0.0 36.3 jit_solution(8753886304095429380)
XLA Ops:
  0.0 1.0 %pack.1 = (bf16[72,128]{1,0:T(8,128)(2,1)S(1)}, f32[1,2]{1,0:T(1,128)S(1)}) custom-call(bf16[32,128]{1,0:T(8,128)(2,1)} %vis_hbm.1, f32[2,32]{1,0:T(2,128)} %bitcast.1, s32[2,32,64]{2,1,0:T(8,128)} %cells_hbm.1, f32[1,2]{1,0:T(1,128)} %centre_hbm.1), custom_call_target="tpu_custom_call" | custom-call | tf_op jit(solution)/shard_map/pack/pallas_call | solution.py:362
  1.1 7.0 %collective-permute-start = (bf16[72,128]{1,0:T(8,128)(2,1)S(1)}, bf16[72,128]{1,0:T(8,128)(2,1)S(1)}, u32[]{:S(2)}, u32[]{:S(2)}) collective-permute-start(bf16[72,128]{1,0:T(8,128)(2,1)S(1)} %get-tuple-element.13), channel_id=1, source_target_pairs={{192,0},{193,1},{194,2},{195,3},{132,4},{133,5},{134,6},{135,7},{2... | collective-permute-start | bytes 55304 | tf_op jit(solution)/shard_map/ppermute | solution.py:376
  8.1 0.7 %collective-permute-start.1 = (f32[1,2]{1,0:T(1,128)S(1)}, f32[1,2]{1,0:T(1,128)S(1)}, u32[]{:S(2)}, u32[]{:S(2)}) collective-permute-start(f32[1,2]{1,0:T(1,128)S(1)} %get-tuple-element.14.own_ref), channel_id=1, source_target_pairs={{0,64},{64,0},{128,192},{192,128},{1,65},{65,1},{129,193},{193,129... | collective-permute-start | bytes 32 | tf_op jit(solution)/shard_map/ppermute | solution.py:375
  8.8 0.8 %collective-permute-done.1.pair_ref = f32[1,2]{1,0:T(1,128)S(1)} collective-permute-done((f32[1,2]{1,0:T(1,128)S(1)}, f32[1,2]{1,0:T(1,128)S(1)}, u32[]{:S(2)}, u32[]{:S(2)}) %collective-permute-start.1) | collective-permute-done | bytes 40 | tf_op jit(solution)/shard_map/ppermute | solution.py:375
  9.6 0.0 collective-permute-done
  9.7 0.0 copy-start
  9.7 0.0 copy-start.1
  9.7 0.0 copy-start.2
  9.7 14.8 %all_to_all.5.blocks_ref = bf16[16,72,128]{2,1,0:T(8,128)(2,1)S(1)} all-to-all(bf16[16,72,128]{2,1,0:T(8,128)(2,1)S(1)} %broadcast_in_dim.2), channel_id=1, replica_groups={{0,1,2,3,4,5,6,7,8,9,10,11,12,13,14,15},{16,17,18,19,20,21,22,23,24,25,..., dimensions={0} | all-to-all | bytes 589824 | tf_op jit(solution)/shard_map/all_to_all | solution.py:379
  24.6 0.0 copy-done
  24.6 0.0 copy-done.1
  24.6 0.0 copy-done.2
  24.6 6.3 %grid.1 = (f32[104,128]{1,0:T(8,128)S(1)}, bf16[104,128]{1,0:T(8,128)(2,1)S(1)}, bf16[104,128]{1,0:T(8,128)(2,1)S(1)}, bf16[104,128]{1,0:T(8,128)(2,1)S(1)}) custom-call(bf16[16,72,128]{2,1,0:T(8,128)(2,1)S(1)} %all_to_all.5.blocks_ref, f32[1,2]{1,0:T(1,128)S(1)} %get-tuple-element.14.own_ref, f32[1,2]{1,0:T(1,128)S(1)} %collective-permute-done.1.pair_ref, ...), custom_call_target="tpu_custom_call" | custom-call | tf_op jit(solution)/shard_map/grid/pallas_call | solution.py:336
  30.9 0.1 collective-permute-start.2
  31.0 3.2 %collective-permute-start.3 = (bf16[104,128]{1,0:T(8,128)(2,1)S(1)}, bf16[104,128]{1,0:T(8,128)(2,1)S(1)}, u32[]{:S(2)}, u32[]{:S(2)}) collective-permute-start(bf16[104,128]{1,0:T(8,128)(2,1)S(1)} %get-tuple-element.19), channel_id=1, source_target_pairs={{0,128},{64,192},{128,0},{192,64},{1,129},{65,193},{129,1},{193,65... | collective-permute-start | bytes 79880 | tf_op jit(solution)/shard_map/ppermute | solution.py:386
  34.1 0.0 copy-start.3
  34.1 0.0 collective-permute-start.4
  34.1 0.1 collective-permute-done.2.p1
  34.2 1.4 %collective-permute-done.3.p2 = bf16[104,128]{1,0:T(8,128)(2,1)S(1)} collective-permute-done((bf16[104,128]{1,0:T(8,128)(2,1)S(1)}, bf16[104,128]{1,0:T(8,128)(2,1)S(1)}, u32[]{:S(2)}, u32[]{:S(2)}) %collective-permute-start.3) | collective-permute-done | bytes 26656 | tf_op jit(solution)/shard_map/ppermute | solution.py:386
  35.7 0.0 collective-permute-done.4.p3
  35.7 0.0 copy-done.3
  35.7 0.7 %blend.1 = f32[3,1,4096]{2,1,0:T(1,128)} custom-call(f32[104,128]{1,0:T(8,128)S(1)} %get-tuple-element.17.p0, bf16[104,128]{1,0:T(8,128)(2,1)S(1)} %collective-permute-done.2.p1, bf16[104,128]{1,0:T(8,128)(2,1)S(1)} %collective-permute-done.3.p2, bf16[104,128]{1,0:T(8,128)(2,1)S(1)} %collective-permute-done.4.p3, s32[1,1,256]{2,1,0:T(1,128)S(1)} %copy-done.3), custom_call_target="tpu_custom_call" | custom-call | tf_op jit(solution)/shard_map/blend/pallas_call | solution.py:387
  (1 shorter events, 0.0 us)
Async XLA Ops:
  1.1 8.6 %collective-permute-start = (bf16[72,128]{1,0:T(8,128)(2,1)S(1)}, bf16[72,128]{1,0:T(8,128)(2,1)S(1)}, u32[]{:S(2)}, u32[]{:S(2)}) collective-permute-start(bf16[72,128]{1,0:T(8,128)(2,1)S(1)} %get-tuple-element.13), channel_id=1, source_target_pairs={{192,0},{193,1},{194,2},{195,3},{132,4},{133,5},{134,6},{135,7},{2... | collective-permute-start | bytes 55304 | tf_op jit(solution)/shard_map/ppermute | solution.py:376
  8.1 1.5 %collective-permute-start.1 = (f32[1,2]{1,0:T(1,128)S(1)}, f32[1,2]{1,0:T(1,128)S(1)}, u32[]{:S(2)}, u32[]{:S(2)}) collective-permute-start(f32[1,2]{1,0:T(1,128)S(1)} %get-tuple-element.14.own_ref), channel_id=1, source_target_pairs={{0,64},{64,0},{128,192},{192,128},{1,65},{65,1},{129,193},{193,129... | collective-permute-start | bytes 32 | tf_op jit(solution)/shard_map/ppermute | solution.py:375
  9.7 14.9 %copy-start = (bf16[96,192]{1,0:T(8,128)(2,1)S(1)}, bf16[96,192]{1,0:T(8,128)(2,1)}, u32[]{:S(2)}) copy-start(bf16[96,192]{1,0:T(8,128)(2,1)} %constant.11.clone.low_ref) | copy-start | bytes 110596
  9.7 14.9 %copy-start.1 = (bf16[96,192]{1,0:T(8,128)(2,1)S(1)}, bf16[96,192]{1,0:T(8,128)(2,1)}, u32[]{:S(2)}) copy-start(bf16[96,192]{1,0:T(8,128)(2,1)} %constant.10.clone.high_ref) | copy-start | bytes 110596
  9.7 14.9 %copy-start.2 = (f32[16,512]{1,0:T(8,128)S(1)}, f32[16,512]{1,0:T(8,128)}, u32[]{:S(2)}) copy-start(f32[16,512]{1,0:T(8,128)} %constant.9.clone.twiddle_ref) | copy-start | bytes 98308
  30.9 3.4 %collective-permute-start.2 = (bf16[104,128]{1,0:T(8,128)(2,1)S(1)}, bf16[104,128]{1,0:T(8,128)(2,1)S(1)}, u32[]{:S(2)}, u32[]{:S(2)}) collective-permute-start(bf16[104,128]{1,0:T(8,128)(2,1)S(1)} %get-tuple-element.18), channel_id=1, source_target_pairs={{0,192},{64,128},{128,64},{192,0},{1,193},{65,129},{129,65},{193,1... | collective-permute-start | bytes 79880 | tf_op jit(solution)/shard_map/ppermute | solution.py:386
  31.0 4.7 %collective-permute-start.3 = (bf16[104,128]{1,0:T(8,128)(2,1)S(1)}, bf16[104,128]{1,0:T(8,128)(2,1)S(1)}, u32[]{:S(2)}, u32[]{:S(2)}) collective-permute-start(bf16[104,128]{1,0:T(8,128)(2,1)S(1)} %get-tuple-element.19), channel_id=1, source_target_pairs={{0,128},{64,192},{128,0},{192,64},{1,129},{65,193},{129,1},{193,65... | collective-permute-start | bytes 79880 | tf_op jit(solution)/shard_map/ppermute | solution.py:386
  34.1 1.5 %copy-start.3 = (s32[1,1,256]{2,1,0:T(1,128)S(1)}, s32[1,1,256]{2,1,0:T(1,128)}, u32[]{:S(2)}) copy-start(s32[1,1,256]{2,1,0:T(1,128)} %mask_ref.1) | copy-start | bytes 3076
  34.1 1.5 %collective-permute-start.4 = (bf16[104,128]{1,0:T(8,128)(2,1)S(1)}, bf16[104,128]{1,0:T(8,128)(2,1)S(1)}, u32[]{:S(2)}, u32[]{:S(2)}) collective-permute-start(bf16[104,128]{1,0:T(8,128)(2,1)S(1)} %get-tuple-element.20), channel_id=1, source_target_pairs={{0,64},{64,0},{128,192},{192,128},{1,65},{65,1},{129,193},{193,129... | collective-permute-start | bytes 79880 | tf_op jit(solution)/shard_map/ppermute | solution.py:386

commit v10 on v8

--- a/solution.py
+++ b/solution.py
@@ -261,9 +261,10 @@
     both = jnp.concatenate([vr.reshape(span, XB), vi.reshape(span, XB)], 0)
     high = both.astype(jnp.bfloat16)
     low = (both - high.astype(jnp.float32)).astype(jnp.bfloat16)
-    image = jnp.dot(high_ref[...], high, preferred_element_type=jnp.float32)
+    stages = jnp.concatenate([high_ref[...], low_ref[...]], 0)
+    image = jnp.dot(stages, high, preferred_element_type=jnp.float32)
+    image = image[:span] + image[span:]
     image = image + jnp.dot(high_ref[...], low, preferred_element_type=jnp.float32)
-    image = image + jnp.dot(low_ref[...], high, preferred_element_type=jnp.float32)
     image_ref[...] = image
     size = TERMS * FINE
     for s, out in enumerate((o0, o1, o2, o3)):

time: 36.5 us -> 36.5 us (level)
  no operation moved by 1% of the time
where the time goes in v10:
time: 36.5 us; the launch traced here: 36.3 us
  blocking collectives  14.8 us (41%)
  starting transfers between devices  11 us (30%)
  Pallas kernels  7.97 us (22%)
  waiting for transfers between devices  2.35 us (6%)
    all_to_all x1, blocking collectives, per_device(): lax.all_to_all(jnp.broadcast_to(packed[None], (BLOCKS,) + packed.shape),...  14.8 us
    ppermute x1, starting transfers between devices, per_device(): packed = lax.ppermute(packed, ('facet', 'vis'), swap_pairs())  7.04 us
    pallas_call x1, Pallas kernels, partial_images(): pl.pallas_call(grid_kernel, out_shape=chunk, in_specs=[vmem] * 3 + [hbm]...  6.26 us
    ppermute x3, starting transfers between devices, per_device(): lax.ppermute(parts[s], 'facet', [(i, i ^ s) for i in range(FACETS)])  3.25 us
    ppermute x3, waiting for transfers between devices, per_device(): lax.ppermute(parts[s], 'facet', [(i, i ^ s) for i in range(FACETS)])  1.52 us
    pallas_call x1, Pallas kernels, per_device(): pl.pallas_call(pack_kernel, out_shape=[jax.ShapeDtypeStruct((PACKED, 2 *...  1.05 us
    ppermute x1, waiting for transfers between devices, per_device(): pair = lax.ppermute(centre, 'facet', [(i, i ^ 1) for i in range(FACETS)])  0.82 us
  transfers between devices with their start and end apart: 5, of which 3 were waited for; matrix products, arithmetic and copies ran while one was open for 0% of the time, Pallas kernels for 0%

profile of v10, /device:TPU:1, one launch (start us, length us, event | category | flops | bytes accessed | tf_op | source)
XLA Modules:
  0.0 36.3 jit_solution(15443628107263415911)
XLA Ops:
  0.0 1.0 %pack.1 = (bf16[72,128]{1,0:T(8,128)(2,1)S(1)}, f32[1,2]{1,0:T(1,128)S(1)}) custom-call(bf16[32,128]{1,0:T(8,128)(2,1)} %vis_hbm.1, f32[2,32]{1,0:T(2,128)} %bitcast.1, s32[2,32,64]{2,1,0:T(8,128)} %cells_hbm.1, f32[1,2]{1,0:T(1,128)} %centre_hbm.1), custom_call_target="tpu_custom_call" | custom-call | tf_op jit(solution)/shard_map/pack/pallas_call | solution.py:358
  1.1 7.0 %collective-permute-start = (bf16[72,128]{1,0:T(8,128)(2,1)S(1)}, bf16[72,128]{1,0:T(8,128)(2,1)S(1)}, u32[]{:S(2)}, u32[]{:S(2)}) collective-permute-start(bf16[72,128]{1,0:T(8,128)(2,1)S(1)} %get-tuple-element.13), channel_id=1, source_target_pairs={{192,0},{193,1},{194,2},{195,3},{132,4},{133,5},{134,6},{135,7},{2... | collective-permute-start | bytes 55304 | tf_op jit(solution)/shard_map/ppermute | solution.py:372
  8.1 0.7 %collective-permute-start.1 = (f32[1,2]{1,0:T(1,128)S(1)}, f32[1,2]{1,0:T(1,128)S(1)}, u32[]{:S(2)}, u32[]{:S(2)}) collective-permute-start(f32[1,2]{1,0:T(1,128)S(1)} %get-tuple-element.14.own_ref), channel_id=1, source_target_pairs={{0,64},{64,0},{128,192},{192,128},{1,65},{65,1},{129,193},{193,129... | collective-permute-start | bytes 32 | tf_op jit(solution)/shard_map/ppermute | solution.py:371
  8.8 0.8 %collective-permute-done.1.pair_ref = f32[1,2]{1,0:T(1,128)S(1)} collective-permute-done((f32[1,2]{1,0:T(1,128)S(1)}, f32[1,2]{1,0:T(1,128)S(1)}, u32[]{:S(2)}, u32[]{:S(2)}) %collective-permute-start.1) | collective-permute-done | bytes 40 | tf_op jit(solution)/shard_map/ppermute | solution.py:371
  9.6 0.0 collective-permute-done
  9.7 0.0 copy-start
  9.7 0.0 copy-start.1
  9.7 0.0 copy-start.2
  9.7 14.8 %all_to_all.5.blocks_ref = bf16[16,72,128]{2,1,0:T(8,128)(2,1)S(1)} all-to-all(bf16[16,72,128]{2,1,0:T(8,128)(2,1)S(1)} %broadcast_in_dim.2), channel_id=1, replica_groups={{0,1,2,3,4,5,6,7,8,9,10,11,12,13,14,15},{16,17,18,19,20,21,22,23,24,25,..., dimensions={0} | all-to-all | bytes 589824 | tf_op jit(solution)/shard_map/all_to_all | solution.py:375
  24.6 0.0 copy-done
  24.6 0.0 copy-done.1
  24.6 0.0 copy-done.2
  24.6 6.3 %grid.1 = (f32[104,128]{1,0:T(8,128)S(1)}, bf16[104,128]{1,0:T(8,128)(2,1)S(1)}, bf16[104,128]{1,0:T(8,128)(2,1)S(1)}, bf16[104,128]{1,0:T(8,128)(2,1)S(1)}) custom-call(bf16[16,72,128]{2,1,0:T(8,128)(2,1)S(1)} %all_to_all.5.blocks_ref, f32[1,2]{1,0:T(1,128)S(1)} %get-tuple-element.14.own_ref, f32[1,2]{1,0:T(1,128)S(1)} %collective-permute-done.1.pair_ref, ...), custom_call_target="tpu_custom_call" | custom-call | tf_op jit(solution)/shard_map/grid/pallas_call | solution.py:332
  30.9 0.1 collective-permute-start.2
  31.0 3.2 %collective-permute-start.3 = (bf16[104,128]{1,0:T(8,128)(2,1)S(1)}, bf16[104,128]{1,0:T(8,128)(2,1)S(1)}, u32[]{:S(2)}, u32[]{:S(2)}) collective-permute-start(bf16[104,128]{1,0:T(8,128)(2,1)S(1)} %get-tuple-element.19), channel_id=1, source_target_pairs={{0,128},{64,192},{128,0},{192,64},{1,129},{65,193},{129,1},{193,65... | collective-permute-start | bytes 79880 | tf_op jit(solution)/shard_map/ppermute | solution.py:382
  34.1 0.0 copy-start.3
  34.1 0.0 collective-permute-start.4
  34.1 0.1 collective-permute-done.2.p1
  34.2 1.4 %collective-permute-done.3.p2 = bf16[104,128]{1,0:T(8,128)(2,1)S(1)} collective-permute-done((bf16[104,128]{1,0:T(8,128)(2,1)S(1)}, bf16[104,128]{1,0:T(8,128)(2,1)S(1)}, u32[]{:S(2)}, u32[]{:S(2)}) %collective-permute-start.3) | collective-permute-done | bytes 26656 | tf_op jit(solution)/shard_map/ppermute | solution.py:382
  35.6 0.0 collective-permute-done.4.p3
  35.6 0.0 copy-done.3
  35.6 0.7 %blend.1 = f32[3,1,4096]{2,1,0:T(1,128)} custom-call(f32[104,128]{1,0:T(8,128)S(1)} %get-tuple-element.17.p0, bf16[104,128]{1,0:T(8,128)(2,1)S(1)} %collective-permute-done.2.p1, bf16[104,128]{1,0:T(8,128)(2,1)S(1)} %collective-permute-done.3.p2, bf16[104,128]{1,0:T(8,128)(2,1)S(1)} %collective-permute-done.4.p3, s32[1,1,256]{2,1,0:T(1,128)S(1)} %copy-done.3), custom_call_target="tpu_custom_call" | custom-call | tf_op jit(solution)/shard_map/blend/pallas_call | solution.py:383
  (1 shorter events, 0.0 us)
Async XLA Ops:
  1.1 8.6 %collective-permute-start = (bf16[72,128]{1,0:T(8,128)(2,1)S(1)}, bf16[72,128]{1,0:T(8,128)(2,1)S(1)}, u32[]{:S(2)}, u32[]{:S(2)}) collective-permute-start(bf16[72,128]{1,0:T(8,128)(2,1)S(1)} %get-tuple-element.13), channel_id=1, source_target_pairs={{192,0},{193,1},{194,2},{195,3},{132,4},{133,5},{134,6},{135,7},{2... | collective-permute-start | bytes 55304 | tf_op jit(solution)/shard_map/ppermute | solution.py:372
  8.1 1.5 %collective-permute-start.1 = (f32[1,2]{1,0:T(1,128)S(1)}, f32[1,2]{1,0:T(1,128)S(1)}, u32[]{:S(2)}, u32[]{:S(2)}) collective-permute-start(f32[1,2]{1,0:T(1,128)S(1)} %get-tuple-element.14.own_ref), channel_id=1, source_target_pairs={{0,64},{64,0},{128,192},{192,128},{1,65},{65,1},{129,193},{193,129... | collective-permute-start | bytes 32 | tf_op jit(solution)/shard_map/ppermute | solution.py:371
  9.7 14.9 %copy-start = (bf16[96,192]{1,0:T(8,128)(2,1)S(1)}, bf16[96,192]{1,0:T(8,128)(2,1)}, u32[]{:S(2)}) copy-start(bf16[96,192]{1,0:T(8,128)(2,1)} %constant.11.clone.low_ref) | copy-start | bytes 110596
  9.7 14.9 %copy-start.1 = (bf16[96,192]{1,0:T(8,128)(2,1)S(1)}, bf16[96,192]{1,0:T(8,128)(2,1)}, u32[]{:S(2)}) copy-start(bf16[96,192]{1,0:T(8,128)(2,1)} %constant.10.clone.high_ref) | copy-start | bytes 110596
  9.7 14.9 %copy-start.2 = (f32[16,512]{1,0:T(8,128)S(1)}, f32[16,512]{1,0:T(8,128)}, u32[]{:S(2)}) copy-start(f32[16,512]{1,0:T(8,128)} %constant.9.clone.twiddle_ref) | copy-start | bytes 98308
  30.9 3.4 %collective-permute-start.2 = (bf16[104,128]{1,0:T(8,128)(2,1)S(1)}, bf16[104,128]{1,0:T(8,128)(2,1)S(1)}, u32[]{:S(2)}, u32[]{:S(2)}) collective-permute-start(bf16[104,128]{1,0:T(8,128)(2,1)S(1)} %get-tuple-element.18), channel_id=1, source_target_pairs={{0,192},{64,128},{128,64},{192,0},{1,193},{65,129},{129,65},{193,1... | collective-permute-start | bytes 79880 | tf_op jit(solution)/shard_map/ppermute | solution.py:382
  31.0 4.7 %collective-permute-start.3 = (bf16[104,128]{1,0:T(8,128)(2,1)S(1)}, bf16[104,128]{1,0:T(8,128)(2,1)S(1)}, u32[]{:S(2)}, u32[]{:S(2)}) collective-permute-start(bf16[104,128]{1,0:T(8,128)(2,1)S(1)} %get-tuple-element.19), channel_id=1, source_target_pairs={{0,128},{64,192},{128,0},{192,64},{1,129},{65,193},{129,1},{193,65... | collective-permute-start | bytes 79880 | tf_op jit(solution)/shard_map/ppermute | solution.py:382
  34.1 1.5 %copy-start.3 = (s32[1,1,256]{2,1,0:T(1,128)S(1)}, s32[1,1,256]{2,1,0:T(1,128)}, u32[]{:S(2)}) copy-start(s32[1,1,256]{2,1,0:T(1,128)} %mask_ref.1) | copy-start | bytes 3076
  34.1 1.5 %collective-permute-start.4 = (bf16[104,128]{1,0:T(8,128)(2,1)S(1)}, bf16[104,128]{1,0:T(8,128)(2,1)S(1)}, u32[]{:S(2)}, u32[]{:S(2)}) collective-permute-start(bf16[104,128]{1,0:T(8,128)(2,1)S(1)} %get-tuple-element.20), channel_id=1, source_target_pairs={{0,64},{64,0},{128,192},{192,128},{1,65},{65,1},{129,193},{193,129... | collective-permute-start | bytes 79880 | tf_op jit(solution)/shard_map/ppermute | solution.py:382
